TPU v7x, 256 devices: a whole 4x4x8 slice. The times are simulated.
256 devices in a mesh: tile: 32 (over x, y, core), mode: 8 (over z).
Axes of the slice: x: 4, y: 4, z: 8, core: 2. Of those that a mesh axis runs over, the one named last changes fastest.
Arguments:
- mode_shapes: bfloat16 [64, 256, 2048], P('mode', 'tile'), may hold values from -6 to 6
- stiffness: float32 [256, 2048], P('tile'), may hold values from 0.5 to 4
- node_slot: int32 [256, 2048], P('tile'), may hold values from 0 to 255, as said below
- slot_zone: int32 [32, 32, 8], replicated, may hold values from 0 to 15, as said below
Outputs:
- energy: float32 [512, 64, 64], P('tile', 'mode')
Inputs may be any that keep to these rules, and one draw needn't show every extreme that they name: `slot_zone`: for each tile and owner, the 8 zone numbers are distinct. `node_slot`: slots that no node of a tile names carry no zone's nodes.
All inputs are finite; a program needn't handle non-finite values.
Results may differ from a plain program's by a relative error of at most 0.00099.
Values may be sent and summed in bfloat16 or wider, within the bound.
No kernel may reach another device: no remote copies, remote signals or barrier semaphores. Data moves between devices by JAX's collectives and lax.ppermute only.
A program may use at most 64 MiB of HBM per device.

v0:
```python
import math

import jax
import jax.numpy as jnp
from jax import lax
from jax.sharding import PartitionSpec as P

ZONES = 512


POISSON = 0.3
SHEAR = 2.0 * (1.0 - POISSON)


def with_halo(cells, sides, width):
    for axis, dim in sides:
        count = lax.axis_size(axis)
        ends = count - 1
        head = lax.slice_in_dim(cells, 0, width, axis=dim)
        tail = lax.slice_in_dim(cells, cells.shape[dim] - width, cells.shape[dim], axis=dim)
        cells = jnp.concatenate(
            [
                lax.ppermute(tail, axis, [(i, (i + 1) % count) for i in range(ends)]),
                cells,
                lax.ppermute(head, axis, [((i + 1) % count, i) for i in range(ends)]),
            ],
            axis=dim,
        )
    return cells


def curvatures(shapes_framed):
    framed = jnp.pad(shapes_framed, ((0, 0), (0, 0), (1, 1)))
    centre = framed[:, 1:-1, 1:-1]
    along_x = framed[:, 2:, 1:-1] - 2.0 * centre + framed[:, :-2, 1:-1]
    along_y = framed[:, 1:-1, 2:] - 2.0 * centre + framed[:, 1:-1, :-2]
    twist_xy = 0.25 * (
        framed[:, 2:, 2:] - framed[:, 2:, :-2] - framed[:, :-2, 2:] + framed[:, :-2, :-2]
    )
    return jnp.stack([along_x, along_y, twist_xy]).astype(jnp.bfloat16)


def left_factor(bending, stiffness):
    along_x, along_y, twist_xy = (bending[0], bending[1], bending[2])
    return jnp.stack(
        [
            stiffness * (along_x + POISSON * along_y),
            stiffness * (along_y + POISSON * along_x),
            stiffness * (SHEAR * twist_xy),
        ]
    )


def per_device(mode_shapes, stiffness, node_slot, slot_zone):
    panel_modes, tile_rows, row_cells = mode_shapes.shape
    node_count = tile_rows * row_cells
    tile_count = lax.axis_size("tile")
    mode_count = panel_modes * lax.axis_size("mode")
    owner_slots = slot_zone.shape[2]
    slot_count = tile_count * owner_slots
    owned_zones = ZONES // tile_count
    pair_count = panel_modes * mode_count
    padded = with_halo(mode_shapes, (("tile", 1),), 1)
    own_bending = curvatures(padded.astype(jnp.float32))
    own_float = own_bending.astype(jnp.float32)
    weighted = left_factor(own_float, stiffness)
    own_sums = jnp.sum(weighted * own_float, axis=(0, 2, 3))
    placed_sums = lax.dynamic_update_slice_in_dim(
        jnp.zeros((mode_count,), jnp.float32), own_sums, lax.axis_index("mode") * panel_modes, 0
    )
    totals = 0.5 * lax.psum(placed_sums, ("tile", "mode"))
    gathered_bend = lax.all_gather(own_bending, "mode", axis=1, tiled=True)
    right_flat = gathered_bend.reshape(3, mode_count, node_count)
    left_flat = weighted.astype(jnp.bfloat16).reshape(3, panel_modes, node_count)
    slot_flat = node_slot.reshape(node_count)
    slot_range = jnp.arange(slot_count, dtype=jnp.int32)
    block_nodes = math.gcd(node_count, max(128, (1 << 20) // pair_count))

    def one_block(number, running):
        first_node = number * block_nodes
        left_block = lax.dynamic_slice_in_dim(left_flat, first_node, block_nodes, 2).astype(
            jnp.float32
        )
        right_block = lax.dynamic_slice_in_dim(right_flat, first_node, block_nodes, 2).astype(
            jnp.float32
        )
        slot_block = lax.dynamic_slice_in_dim(slot_flat, first_node, block_nodes, 0)
        products = jnp.sum(left_block[:, :, None, :] * right_block[:, None, :, :], axis=0)
        products = products.reshape(pair_count, block_nodes)
        member_block = (slot_block[:, None] == slot_range[None, :]).astype(jnp.float32)
        return running + jnp.dot(products, member_block, precision=lax.Precision.HIGHEST)

    by_pair = lax.fori_loop(
        0, node_count // block_nodes, one_block, jnp.zeros((pair_count, slot_count), jnp.float32)
    )
    routed = by_pair.T.reshape(tile_count, owner_slots, pair_count)
    tile_index = lax.axis_index("tile")
    own_lists = lax.dynamic_index_in_dim(slot_zone, tile_index, 0, keepdims=False)
    selector = (
        own_lists[:, :, None] == jnp.arange(owned_zones, dtype=jnp.int32)[None, None, :]
    ).astype(jnp.float32)
    spread_zones = jnp.einsum("dcz,dcm->dzm", selector, routed, precision=lax.Precision.HIGHEST)
    spread_zones = spread_zones.reshape(tile_count * owned_zones, pair_count)
    summed = lax.psum_scatter(spread_zones, "tile", scatter_dimension=0, tiled=True)
    own_totals = lax.dynamic_slice_in_dim(
        totals, lax.axis_index("mode") * panel_modes, panel_modes, 0
    )
    denominator = jnp.sqrt(own_totals[:, None] * totals[None, :])
    return ZONES * (0.5 * summed.reshape(owned_zones, panel_modes, mode_count)) / denominator


def solution(mesh):
    placed = (P("mode", "tile", None), P("tile", None), P("tile", None), P())
    return jax.shard_map(
        per_device, mesh=mesh, in_specs=placed, out_specs=P("tile", "mode", None), check_vma=False
    )
```

profile of v0, /device:TPU:4, one launch (start us, length us, event | category | flops | bytes accessed | tf_op | source)
XLA Modules:
  0.0 281.9 jit_solution(18030605691731812583)
XLA Ops:
  7.7 1.9 collective-permute-start
  9.6 5.8 %collective-permute-start.1 = (bf16[8,1,2048]{2,1,0:T(2,128)(2,1)S(1)}, bf16[8,1,2048]{2,1,0:T(2,128)(2,1)S(1)}, u32[]{:S(2)}, u32[]{:S(2)}) collective-permute-start(bf16[8,1,2048]{2,1,0:T(2,128)(2,1)S(1)} %get-tuple-element.161), channel_id=1, source_target_pairs={{8,0},{16,8},{24,16},{32,24},{40,32},{48,40},{56,48},{64,56},{72,6... | collective-permute-start | bytes 98312 | tf_op jit(solution)/shard_map/ppermute | solution.py:25
  15.4 1.9 collective-permute-done.1
  21.3 2.2 fusion.22
  26.8 71.7 %all-gather.2.cloned.1.call-done = bf16[3,64,8,2048]{3,2,1,0:T(8,128)(2,1)} async-done(((bf16[3,8,8,2048]{3,2,1,0:T(8,128)(2,1)}), bf16[3,64,8,2048]{3,2,1,0:T(8,128)(2,1)}) %all-gather.2.cloned.1.call-update) | async-done | bytes 6291472 | tf_op jit(solution)/shard_map/all_gather | solution.py:72
  98.5 10.4 %reshape.64 = bf16[3,64,16384]{2,1,0:T(8,128)(2,1)} reshape(bf16[3,64,8,2048]{3,2,1,0:T(8,128)(2,1)} %all-gather.2.cloned.1.call-done) | data formatting | bytes 12582912 | tf_op jit(solution)/shard_map/reshape | solution.py:73
  108.9 78.5 %while.14 = (s32[]{:T(128)}, f32[512,256]{1,0:T(8,128)S(1)}, bf16[3,8,16384]{2,1,0:T(8,128)(2,1)S(1)}, bf16[3,64,16384]{2,1,0:T(8,128)(2,1)}, s32[16384]{0:T(102...) while((s32[]{:T(128)}, f32[512,256]{1,0:T(8,128)S(1)}, bf16[3,8,16384]{2,1,0:T(8,128)(2,1)S(1)}, ...), condition=%wide.region_2.3_spmd.clone, body=%wide.region_0.0_spmd.clone.sunk | while | flops 3227697152 | bytes 13885601 | solution.py:93
  110.2 3.1 %multiply_reduce_fusion.2 = f32[8,64,2048]{2,1,0:T(8,128)} fusion(f32[3,64,2048]{2,1,0:T(8,128)S(1)} %dynamic-slice_convert_fusion.4, f32[3,8,2048]{2,1,0:T(8,128)S(1)} %dynamic-slice_convert_fusion.5), kind=kLoop, calls=%fused_computation.1.clone.1 | loop fusion | flops 5242880 | bytes 5963776 | tf_op jit(solution)/shard_map/while/body/eval_jaxpr/reduce_sum | solution.py:88
  114.0 4.7 %fusion.30 = f32[512,256]{1,0:T(8,128)S(1)} fusion(f32[512,2048]{1,0:T(8,128)} %bitcast.30, s32[2048]{0:T(1024)S(1)} %dynamic_slice.41, f32[512,256]{1,0:T(8,128)S(1)} %get-tuple-element.203, pred[]{:T(512)S(6)} %compare.4), kind=kOutput, calls=%fused_computation.4.clone.1 | convolution fusion | flops 3222011904 | bytes 5251073 | tf_op jit(solution)/shard_map/while/body/eval_jaxpr/dot_general | solution.py:91
  118.7 1.3 dynamic-slice_convert_fusion.4
  120.0 3.1 %multiply_reduce_fusion.2 = f32[8,64,2048]{2,1,0:T(8,128)} fusion(f32[3,64,2048]{2,1,0:T(8,128)S(1)} %dynamic-slice_convert_fusion.4, f32[3,8,2048]{2,1,0:T(8,128)S(1)} %dynamic-slice_convert_fusion.5), kind=kLoop, calls=%fused_computation.1.clone.1 | loop fusion | flops 5242880 | bytes 5963776 | tf_op jit(solution)/shard_map/while/body/eval_jaxpr/reduce_sum | solution.py:88
  123.8 4.7 %fusion.30 = f32[512,256]{1,0:T(8,128)S(1)} fusion(f32[512,2048]{1,0:T(8,128)} %bitcast.30, s32[2048]{0:T(1024)S(1)} %dynamic_slice.41, f32[512,256]{1,0:T(8,128)S(1)} %get-tuple-element.203, pred[]{:T(512)S(6)} %compare.4), kind=kOutput, calls=%fused_computation.4.clone.1 | convolution fusion | flops 3222011904 | bytes 5251073 | tf_op jit(solution)/shard_map/while/body/eval_jaxpr/dot_general | solution.py:91
  128.5 1.3 dynamic-slice_convert_fusion.4
  129.9 3.1 %multiply_reduce_fusion.2 = f32[8,64,2048]{2,1,0:T(8,128)} fusion(f32[3,64,2048]{2,1,0:T(8,128)S(1)} %dynamic-slice_convert_fusion.4, f32[3,8,2048]{2,1,0:T(8,128)S(1)} %dynamic-slice_convert_fusion.5), kind=kLoop, calls=%fused_computation.1.clone.1 | loop fusion | flops 5242880 | bytes 5963776 | tf_op jit(solution)/shard_map/while/body/eval_jaxpr/reduce_sum | solution.py:88
  133.6 4.7 %fusion.30 = f32[512,256]{1,0:T(8,128)S(1)} fusion(f32[512,2048]{1,0:T(8,128)} %bitcast.30, s32[2048]{0:T(1024)S(1)} %dynamic_slice.41, f32[512,256]{1,0:T(8,128)S(1)} %get-tuple-element.203, pred[]{:T(512)S(6)} %compare.4), kind=kOutput, calls=%fused_computation.4.clone.1 | convolution fusion | flops 3222011904 | bytes 5251073 | tf_op jit(solution)/shard_map/while/body/eval_jaxpr/dot_general | solution.py:91
  138.3 1.3 dynamic-slice_convert_fusion.4
  139.7 3.1 %multiply_reduce_fusion.2 = f32[8,64,2048]{2,1,0:T(8,128)} fusion(f32[3,64,2048]{2,1,0:T(8,128)S(1)} %dynamic-slice_convert_fusion.4, f32[3,8,2048]{2,1,0:T(8,128)S(1)} %dynamic-slice_convert_fusion.5), kind=kLoop, calls=%fused_computation.1.clone.1 | loop fusion | flops 5242880 | bytes 5963776 | tf_op jit(solution)/shard_map/while/body/eval_jaxpr/reduce_sum | solution.py:88
  143.4 4.7 %fusion.30 = f32[512,256]{1,0:T(8,128)S(1)} fusion(f32[512,2048]{1,0:T(8,128)} %bitcast.30, s32[2048]{0:T(1024)S(1)} %dynamic_slice.41, f32[512,256]{1,0:T(8,128)S(1)} %get-tuple-element.203, pred[]{:T(512)S(6)} %compare.4), kind=kOutput, calls=%fused_computation.4.clone.1 | convolution fusion | flops 3222011904 | bytes 5251073 | tf_op jit(solution)/shard_map/while/body/eval_jaxpr/dot_general | solution.py:91
  148.1 1.3 dynamic-slice_convert_fusion.4
  149.5 3.1 %multiply_reduce_fusion.2 = f32[8,64,2048]{2,1,0:T(8,128)} fusion(f32[3,64,2048]{2,1,0:T(8,128)S(1)} %dynamic-slice_convert_fusion.4, f32[3,8,2048]{2,1,0:T(8,128)S(1)} %dynamic-slice_convert_fusion.5), kind=kLoop, calls=%fused_computation.1.clone.1 | loop fusion | flops 5242880 | bytes 5963776 | tf_op jit(solution)/shard_map/while/body/eval_jaxpr/reduce_sum | solution.py:88
  153.3 4.7 %fusion.30 = f32[512,256]{1,0:T(8,128)S(1)} fusion(f32[512,2048]{1,0:T(8,128)} %bitcast.30, s32[2048]{0:T(1024)S(1)} %dynamic_slice.41, f32[512,256]{1,0:T(8,128)S(1)} %get-tuple-element.203, pred[]{:T(512)S(6)} %compare.4), kind=kOutput, calls=%fused_computation.4.clone.1 | convolution fusion | flops 3222011904 | bytes 5251073 | tf_op jit(solution)/shard_map/while/body/eval_jaxpr/dot_general | solution.py:91
  158.0 1.3 dynamic-slice_convert_fusion.4
  159.3 3.1 %multiply_reduce_fusion.2 = f32[8,64,2048]{2,1,0:T(8,128)} fusion(f32[3,64,2048]{2,1,0:T(8,128)S(1)} %dynamic-slice_convert_fusion.4, f32[3,8,2048]{2,1,0:T(8,128)S(1)} %dynamic-slice_convert_fusion.5), kind=kLoop, calls=%fused_computation.1.clone.1 | loop fusion | flops 5242880 | bytes 5963776 | tf_op jit(solution)/shard_map/while/body/eval_jaxpr/reduce_sum | solution.py:88
  163.1 4.7 %fusion.30 = f32[512,256]{1,0:T(8,128)S(1)} fusion(f32[512,2048]{1,0:T(8,128)} %bitcast.30, s32[2048]{0:T(1024)S(1)} %dynamic_slice.41, f32[512,256]{1,0:T(8,128)S(1)} %get-tuple-element.203, pred[]{:T(512)S(6)} %compare.4), kind=kOutput, calls=%fused_computation.4.clone.1 | convolution fusion | flops 3222011904 | bytes 5251073 | tf_op jit(solution)/shard_map/while/body/eval_jaxpr/dot_general | solution.py:91
  167.8 1.3 dynamic-slice_convert_fusion.4
  169.1 3.1 %multiply_reduce_fusion.2 = f32[8,64,2048]{2,1,0:T(8,128)} fusion(f32[3,64,2048]{2,1,0:T(8,128)S(1)} %dynamic-slice_convert_fusion.4, f32[3,8,2048]{2,1,0:T(8,128)S(1)} %dynamic-slice_convert_fusion.5), kind=kLoop, calls=%fused_computation.1.clone.1 | loop fusion | flops 5242880 | bytes 5963776 | tf_op jit(solution)/shard_map/while/body/eval_jaxpr/reduce_sum | solution.py:88
  172.9 4.7 %fusion.30 = f32[512,256]{1,0:T(8,128)S(1)} fusion(f32[512,2048]{1,0:T(8,128)} %bitcast.30, s32[2048]{0:T(1024)S(1)} %dynamic_slice.41, f32[512,256]{1,0:T(8,128)S(1)} %get-tuple-element.203, pred[]{:T(512)S(6)} %compare.4), kind=kOutput, calls=%fused_computation.4.clone.1 | convolution fusion | flops 3222011904 | bytes 5251073 | tf_op jit(solution)/shard_map/while/body/eval_jaxpr/dot_general | solution.py:91
  178.9 3.1 %multiply_reduce_fusion.2 = f32[8,64,2048]{2,1,0:T(8,128)} fusion(f32[3,64,2048]{2,1,0:T(8,128)S(1)} %dynamic-slice_convert_fusion.4, f32[3,8,2048]{2,1,0:T(8,128)S(1)} %dynamic-slice_convert_fusion.5), kind=kLoop, calls=%fused_computation.1.clone.1 | loop fusion | flops 5242880 | bytes 5963776 | tf_op jit(solution)/shard_map/while/body/eval_jaxpr/reduce_sum | solution.py:88
  182.7 4.7 %fusion.30 = f32[512,256]{1,0:T(8,128)S(1)} fusion(f32[512,2048]{1,0:T(8,128)} %bitcast.30, s32[2048]{0:T(1024)S(1)} %dynamic_slice.41, f32[512,256]{1,0:T(8,128)S(1)} %get-tuple-element.203, pred[]{:T(512)S(6)} %compare.4), kind=kOutput, calls=%fused_computation.4.clone.1 | convolution fusion | flops 3222011904 | bytes 5251073 | tf_op jit(solution)/shard_map/while/body/eval_jaxpr/dot_general | solution.py:91
  187.6 1.9 fusion.15
  190.1 74.7 %psum.7 = f32[64]{0:T(128)S(1)} all-reduce(f32[64]{0:T(128)S(1)} %dynamic_update_slice.3), channel_id=1, replica_groups=mesh['tile'=32,'mode'=8] {'tile','mode'}, use_global_device_ids=true, to_apply=%region_5.6 | all-reduce | flops 64 | bytes 512 | tf_op jit(solution)/shard_map/psum | solution.py:71
  264.9 8.6 %reduce-scatter.2.cloned.1.call-done = f32[16,512]{1,0:T(8,128)} async-done(((f32[512,512]{1,0:T(8,128)}), f32[16,512]{1,0:T(8,128)}) %reduce-scatter.2.cloned.1.call-update) | async-done | bytes 32784 | tf_op jit(solution)/shard_map/reduce_scatter | solution.py:104
  (56 shorter events, 19.1 us)
Async XLA Ops:
  6.5 14.6 %copy-start = (s32[32,32,8]{1,2,0:T(8,128)S(1)}, s32[32,32,8]{1,2,0:T(8,128)}, u32[]{:S(2)}) copy-start(s32[32,32,8]{1,2,0:T(8,128)} %param.9) | copy-start | bytes 98308
  6.5 91.9 %all-gather.2.cloned.1.call-start = ((), (), s32[]{:S(2)}) async-start(), calls=%async_computation.1 | async-start | bytes 7077888 | tf_op jit(solution)/shard_map/all_gather | solution.py:72
  7.7 7.7 %collective-permute-start = (bf16[8,1,2048]{2,1,0:T(2,128)(2,1)S(1)}, bf16[8,1,2048]{2,1,0:T(2,128)(2,1)S(1)}, u32[]{:S(2)}, u32[]{:S(2)}) collective-permute-start(bf16[8,1,2048]{2,1,0:T(2,128)(2,1)S(1)} %get-tuple-element.160), channel_id=1, source_target_pairs={{0,8},{8,16},{16,24},{24,32},{32,40},{40,48},{48,56},{56,64},{64,7... | collective-permute-start | bytes 98312 | tf_op jit(solution)/shard_map/ppermute | solution.py:23
  9.6 7.6 %collective-permute-start.1 = (bf16[8,1,2048]{2,1,0:T(2,128)(2,1)S(1)}, bf16[8,1,2048]{2,1,0:T(2,128)(2,1)S(1)}, u32[]{:S(2)}, u32[]{:S(2)}) collective-permute-start(bf16[8,1,2048]{2,1,0:T(2,128)(2,1)S(1)} %get-tuple-element.161), channel_id=1, source_target_pairs={{8,0},{16,8},{24,16},{32,24},{40,32},{48,40},{56,48},{64,56},{72,6... | collective-permute-start | bytes 98312 | tf_op jit(solution)/shard_map/ppermute | solution.py:25
  19.4 1.2 copy-start.4
  19.4 1.9 copy-start.3
  20.5 253.1 %reduce-scatter.2.cloned.1.call-start = ((), (), s32[]{:S(2)}) async-start(), calls=%async_computation.2 | async-start | bytes 1081344 | tf_op jit(solution)/shard_map/reduce_scatter | solution.py:104
  187.6 2.0 copy-start.1
  187.6 2.0 copy-start.2
Sparse Core Ops, SparseCore 0:
  20.6 77.8 all-gather.1
  189.7 83.7 reduce-scatter.1
where the time goes:
time: 283 us; the launch traced here: 282 us
  waiting for transfers between devices  82.2 us (29%)
  blocking collectives  74.7 us (26%)
  other arithmetic  42.3 us (15%)
  matrix products  39.4 us (14%)
  local copies, waits for them, and re-layouts  21.7 us (8%)
  between operations  13.5 us (5%)
  starting transfers between devices  7.72 us (3%)
    psum x1, blocking collectives, per_device(): totals = 0.5 * lax.psum(placed_sums, ('tile', 'mode'))  74.7 us
    all_gather x1, waiting for transfers between devices, per_device(): gathered_bend = lax.all_gather(own_bending, 'mode', axis=1, tiled=True)  71.7 us
    dot_general x8, matrix products, one_block(): jnp.dot(products, member_block, precision=lax.Precision.HIGHEST)  37.5 us
    reduce_sum x8, other arithmetic, one_block(): jnp.sum(left_block[:, :, None, :] * right_block[:, None, :, :], axis=0)  24.5 us
    reshape x1, local copies, waits for them, and re-layouts, per_device(): right_flat = gathered_bend.reshape(3, mode_count, node_count)  10.4 us
    convert_element_type x8, other arithmetic, one_block(): lax.dynamic_slice_in_dim(right_flat, first_node, block_nodes, 2)  10.4 us
    reduce_scatter x1, waiting for transfers between devices, per_device(): lax.psum_scatter(spread_zones, 'tile', scatter_dimension=0, tiled=True)  8.6 us
    ppermute x1, starting transfers between devices, with_halo(): lax.ppermute(head, axis, [((i + 1) % count, i) for i in range(ends)])  5.75 us
  transfers between devices with their start and end apart: 4, of which 3 were waited for; matrix products, arithmetic and copies ran while one was open for 2% of the time, Pallas kernels for 0%

commit v1 on v0

v1 whole, which is shorter than its diff:
```python
import functools

import jax
import jax.numpy as jnp
from jax import lax
from jax.experimental import pallas as pl
from jax.experimental.pallas import tpu as pltpu
from jax.sharding import PartitionSpec as P

ZONES = 512
POISSON = 0.3
SHEAR = 2.0 * (1.0 - POISSON)
CHUNK = 512

f32 = jnp.float32
bf16 = jnp.bfloat16


def stencil(shapes, stiff, cross, second, bend_out, left_out, total_out):
    framed_rows, modes, cells = shapes.shape
    lane = lax.broadcasted_iota(jnp.int32, (modes, cells), 1)

    def across(r, carry):
        w = shapes[r].astype(f32)
        right = jnp.where(lane == cells - 1, 0.0, pltpu.roll(w, cells - 1, 1))
        left = jnp.where(lane == 0, 0.0, pltpu.roll(w, 1, 1))
        cross[r] = right - left
        second[r] = (right - 2.0 * w) + left
        return carry

    lax.fori_loop(0, framed_rows, across, 0)

    def along(r, total):
        w = shapes[r + 1].astype(f32)
        along_x = (shapes[r + 2].astype(f32) - 2.0 * w) + shapes[r].astype(f32)
        bent = [along_x, second[r + 1], 0.25 * (cross[r + 2] - cross[r])]
        rounded = [b.astype(bf16) for b in bent]
        bx, by, bt = [b.astype(f32) for b in rounded]
        s = jnp.broadcast_to(stiff[pl.ds(r, 1), :], (modes, cells))
        weighted = [s * (bx + POISSON * by), s * (by + POISSON * bx), s * (SHEAR * bt)]
        for c in range(3):
            bend_out[c, r] = rounded[c]
            if left_out is not None:
                left_out[c, r] = weighted[c].astype(bf16)
        if total_out is None:
            return total
        energy = weighted[0] * bx + weighted[1] * by + weighted[2] * bt
        for k in range(cells // 128):
            total = total + energy[:, k * 128 : (k + 1) * 128]
        return total

    total = lax.fori_loop(0, framed_rows - 2, along, jnp.zeros((modes, 128), f32))
    if total_out is not None:
        total_out[...] = jnp.broadcast_to(jnp.sum(total, axis=1, keepdims=True), (modes, 128))


def pair_sums(slot, blocks, rows_scratch, acc):
    rows, cells = slot.shape
    slots = acc.shape[0]
    per_row = cells // CHUNK
    acc[...] = jnp.zeros_like(acc)
    slot_id = lax.broadcasted_iota(jnp.int32, (slots, CHUNK), 0).astype(f32).astype(bf16)

    def step(n, carry):
        r = n // per_row
        first = pl.multiple_of((n % per_row) * CHUNK, CHUNK)
        here = slot[pl.ds(r, 1), pl.ds(first, CHUNK)].astype(f32).astype(bf16)
        member = jnp.where(
            jnp.broadcast_to(here, (slots, CHUNK)) == slot_id,
            jnp.ones((slots, CHUNK), bf16),
            jnp.zeros((slots, CHUNK), bf16),
        )
        high, low = [], []
        for index, (left, bend) in enumerate(blocks):
            modes = left.shape[2]
            for c in range(3):
                rows_scratch[index, c] = left[c, r, :, pl.ds(first, CHUNK)].astype(f32)
            right = [bend[c, r, :, pl.ds(first, CHUNK)].astype(f32) for c in range(3)]
            for i in range(0, modes, 2):
                pair = []
                for k in (i, i + 1):
                    spread = [
                        jnp.broadcast_to(rows_scratch[index, c, pl.ds(k, 1), :], (modes, CHUNK))
                        for c in range(3)
                    ]
                    pair.append(spread[0] * right[0] + spread[1] * right[1] + spread[2] * right[2])
                product = jnp.concatenate(pair, axis=0)
                top = product.astype(bf16)
                high.append(top)
                low.append((product - top.astype(f32)).astype(bf16))
        contract = (((1,), (1,)), ((), ()))
        acc[...] += lax.dot_general(
            member, jnp.concatenate(high, axis=0), contract, preferred_element_type=f32
        ) + lax.dot_general(
            member, jnp.concatenate(low, axis=0), contract, preferred_element_type=f32
        )
        return carry

    lax.fori_loop(0, rows * per_row, step, 0)


def stage_own(shapes, stiff, slot, bend, left, total, sums, cross, second, rows_scratch):
    stencil(shapes, stiff, cross, second, bend, left, total)
    pair_sums(slot, [(left, bend)], rows_scratch, sums)


def stage_near(
    below, above, stiff, slot, bend, left,
    bend_below, left_below, total_below, bend_above, left_above, total_above, sums,
    cross, second, rows_scratch,
):
    stencil(below, stiff, cross, second, bend_below, left_below, total_below)
    stencil(above, stiff, cross, second, bend_above, left_above, total_above)
    blocks = [(left_below, bend_above), (left_above, bend_below), (left, bend_above), (left, bend_below)]
    pair_sums(slot, blocks, rows_scratch, sums)


def stage_far(
    below, above, stiff, slot, left_below, left_above,
    total, total_below, total_above, own_sums, near_sums,
    message,
    bend_far_below, left_far_below, bend_far_above, total_far_below, total_far_above,
    cross, second, rows_scratch, sums,
):
    stencil(below, stiff, cross, second, bend_far_below, left_far_below, total_far_below)
    stencil(above, stiff, cross, second, bend_far_above, None, total_far_above)
    blocks = [(left_below, bend_far_above), (left_above, bend_far_below), (left_far_below, bend_far_above)]
    pair_sums(slot, blocks, rows_scratch, sums)
    owners, entries, _ = message.shape
    message[:, :, 0:256] = near_sums[...].reshape(owners, entries, 256)
    message[:, :, 256:384] = sums[:, 0:128].reshape(owners, entries, 128)
    message[:, :, 384:512] = jnp.concatenate([sums[:, 128:192], own_sums[...]], axis=1).reshape(
        owners, entries, 128
    )
    lane = lax.broadcasted_iota(jnp.int32, total.shape, 1)
    panels = [total, total_above, total_far_above, total_far_below, total_below]
    places = jnp.zeros(total.shape, f32)
    for place, panel in enumerate(panels):
        places = jnp.where(lane == place, panel[...], places)
    message[:, :, 512:640] = jnp.broadcast_to(places[None], (owners, entries, 128))


def three_parts(x):
    a = x.astype(bf16)
    rest = x - a.astype(f32)
    b = rest.astype(bf16)
    return a, b, (rest - b.astype(f32)).astype(bf16)


def exact_dot(x, y, parts_of_y):
    if parts_of_y:
        return sum(jnp.dot(x, part, preferred_element_type=f32) for part in three_parts(y))
    return sum(jnp.dot(part, y, preferred_element_type=f32) for part in three_parts(x))


def gather_zones(received, lists, zoned):
    places, width = received.shape
    zones = zoned.shape[0] - 8
    body = width - 128
    chosen = jnp.broadcast_to(lists[...], (zones, places)) == lax.broadcasted_iota(
        jnp.int32, (zones, places), 0
    )
    chosen = jnp.where(chosen, 1.0, 0.0).astype(bf16)
    zoned[0:zones, :] = exact_dot(chosen, received[:, 0:body], True)
    totals = jnp.sum(received[:, body:].reshape(places // 8, 8, 128), axis=0)
    zoned[zones:, :] = jnp.concatenate([totals, jnp.zeros((8, body - 128), f32)], axis=1)


def normalise(place, mine, from_above, from_below, from_far, energy):
    zones = energy.shape[0]
    z = slice(0, zones)
    t = slice(zones, zones + 8)
    sums = jnp.concatenate(
        [
            mine[z, 448:512], mine[z, 128:192], from_above[z, 0:64], from_above[z, 256:320],
            from_far[z, 384:448], from_below[z, 320:384], from_below[z, 64:128], mine[z, 192:256],
        ],
        axis=1,
    )
    own = mine[t, 0:128]
    columns = [
        own[:, 0:1], own[:, 1:2], own[:, 2:3], from_above[t, 2:3],
        from_far[t, 2:3], from_below[t, 3:4], own[:, 3:4], own[:, 4:5],
    ]
    spread = jnp.concatenate([jnp.broadcast_to(c, (8, 64)) for c in columns], axis=1)
    sub = lax.broadcasted_iota(jnp.int32, (8, 512), 0)
    lane = lax.broadcasted_iota(jnp.int32, (8, 512), 1)
    total_j = jnp.sum(jnp.where(lane % 8 == sub, spread, 0.0), axis=0, keepdims=True)
    total_i = jnp.sum(
        jnp.where((lane // 8) % 8 == sub, jnp.broadcast_to(own[:, 0:1], (8, 512)), 0.0), axis=0, keepdims=True
    )
    scaled = ZONES * (0.5 * sums) / jnp.sqrt((0.5 * total_i) * (0.5 * total_j))
    r = lax.broadcasted_iota(jnp.int32, (512, 512), 0)
    c = lax.broadcasted_iota(jnp.int32, (512, 512), 1)
    panel = (r // 64 + place[0]) % 8
    target = ((r // 8) % 8) * 64 + panel * 8 + r % 8
    order = jnp.where(c == target, 1.0, 0.0).astype(bf16)
    ordered = exact_dot(scaled, order, False)
    for i in range(8):
        energy[:, i, :] = ordered[:, i * 64 : (i + 1) * 64]


def vmem(shape, dtype=f32):
    return pltpu.VMEM(shape, dtype)


def call(body, outs, scratch, *args, scalars=0):
    specs = [pl.BlockSpec(memory_space=pltpu.SMEM)] * scalars + [
        pl.BlockSpec(memory_space=pltpu.VMEM)
    ] * (len(args) - scalars)
    return pl.pallas_call(
        body,
        out_shape=[jax.ShapeDtypeStruct(s, d) for s, d in outs],
        in_specs=specs,
        out_specs=[pl.BlockSpec(memory_space=pltpu.VMEM)] * len(outs),
        scratch_shapes=scratch,
        name=body.__name__,
    )(*args)


def per_device(mode_shapes, stiffness, node_slot, slot_zone):
    modes, rows, cells = mode_shapes.shape
    tiles = lax.axis_size("tile")
    panels = lax.axis_size("mode")
    entries = slot_zone.shape[2]
    slots = tiles * entries
    owned = ZONES // tiles
    up = [(i, i + 1) for i in range(tiles - 1)]
    down = [(i + 1, i) for i in range(tiles - 1)]

    def turn(x, by):
        return lax.ppermute(x, "mode", [(i, (i + by) % panels) for i in range(panels)])

    head = lax.ppermute(mode_shapes[:, rows - 1], "tile", up)
    tail = lax.ppermute(mode_shapes[:, 0], "tile", down)
    framed = jnp.concatenate([head[None], jnp.transpose(mode_shapes, (1, 0, 2)), tail[None]], axis=0)
    below = turn(framed, 1)
    above = turn(framed, -1)
    far_below = turn(below, 1)
    far_above = turn(above, -1)

    factor = ((3, rows, modes, cells), bf16)
    total = ((modes, 128), f32)
    lines = [vmem((rows + 2, modes, cells)), vmem((rows + 2, modes, cells))]
    pairs = modes * modes
    bend0, left0, total0, own_sums = call(
        stage_own, [factor, factor, total, ((slots, pairs), f32)],
        lines + [vmem((1, 3, modes, CHUNK))],
        framed, stiffness, node_slot,
    )
    _, left_below, total_below, _, left_above, total_above, near_sums = call(
        stage_near, [factor, factor, total, factor, factor, total, ((slots, 4 * pairs), f32)],
        lines + [vmem((4, 3, modes, CHUNK))],
        below, above, stiffness, node_slot, bend0, left0,
    )
    (message,) = call(
        stage_far, [((tiles, entries, 8 * pairs + 128), f32)],
        [vmem(*factor), vmem(*factor), vmem(*factor), vmem(*total), vmem(*total)]
        + lines + [vmem((3, 3, modes, CHUNK)), vmem((slots, 3 * pairs))],
        far_below, far_above, stiffness, node_slot, left_below, left_above,
        total0, total_below, total_above, own_sums, near_sums,
    )
    received = lax.all_to_all(message, "tile", 0, 0, tiled=True)
    lists = lax.dynamic_index_in_dim(slot_zone, lax.axis_index("tile"), 1, keepdims=False)
    (zoned,) = call(
        gather_zones, [((owned + 8, 8 * pairs), f32)], [],
        received.reshape(slots, 8 * pairs + 128), lists.reshape(1, slots),
    )
    from_above = turn(zoned, -1)
    from_below = turn(zoned, 1)
    from_far = turn(zoned, -2)
    place = lax.axis_index("mode").astype(jnp.int32).reshape(1)
    (energy,) = call(
        normalise, [((owned, modes, panels * modes), f32)], [],
        place, zoned, from_above, from_below, from_far, scalars=1,
    )
    return energy


def solution(mesh):
    placed = (P("mode", "tile", None), P("tile", None), P("tile", None), P())
    return jax.shard_map(
        per_device, mesh=mesh, in_specs=placed, out_specs=P("tile", "mode", None), check_vma=False
    )
```

time: 283 us -> 110 us (0.39)
  blocking collectives: 74.7 us -> 0 us
  waiting for transfers between devices: 82.2 us -> 23.2 us
  Pallas kernels: 0 us -> 53.4 us
  other arithmetic: 42.3 us -> 0.04 us
  matrix products: 39.4 us -> 0 us
  starting transfers between devices: 7.72 us -> 26.7 us
  local copies, waits for them, and re-layouts: 21.7 us -> 4.8 us
  between operations: 13.5 us -> 0.12 us
    psum x1 -> x0, blocking collectives: 74.7 us -> none  [per_device(): totals = 0.5 * lax.psum(placed_sums, ('tile', 'mode'))]
    all_gather x1 -> x0, waiting for transfers between devices: 71.7 us -> none  [per_device(): gathered_bend = lax.all_gather(own_bending, 'mode', axis=1, tiled=True)]
    pallas_call x0 -> x5, Pallas kernels: none -> 53.4 us  [call(): pl.pallas_call(body, out_shape=[jax.ShapeDtypeStruct(s, d) for s, d in ou...]
    dot_general x9 -> x0, matrix products: 39.4 us -> none  [the longest x8 37.5 us: one_block(): jnp.dot(products, member_block, precision=lax.Precision.HIGHEST)]
    reduce_sum x9 -> x0, other arithmetic: 24.8 us -> none  [the longest x8 24.5 us: one_block(): jnp.sum(left_block[:, :, None, :] * right_block[:, None, :, :], axis=0)]
    ppermute x2 -> x9, starting transfers between devices: 7.67 us -> 20.4 us  [the longest x7 12.7 us: turn(): lax.ppermute(x, 'mode', [(i, (i + by) % panels) for i in range(panels)])]
    convert_element_type x17 -> x0, other arithmetic: 11.8 us -> none  [the longest x8 10.4 us: one_block(): lax.dynamic_slice_in_dim(right_flat, first_node, block_nodes, 2)]
    ppermute x2 -> x9, waiting for transfers between devices: 1.88 us -> 13.6 us  [the longest x7 12.1 us: turn(): lax.ppermute(x, 'mode', [(i, (i + by) % panels) for i in range(panels)])]
  transfers between devices with their start and end apart: 4 -> 10, of which waited for: 3 -> 6; matrix products, arithmetic and copies ran while one was open for 2% -> 1% of each run, Pallas kernels for 0% -> 30%
where the time goes in v1:
time: 110 us; the launch traced here: 108 us
  Pallas kernels  53.4 us (49%)
  starting transfers between devices  26.7 us (24%)
  waiting for transfers between devices  23.2 us (21%)
  local copies, waits for them, and re-layouts  4.8 us (4%)
    pallas_call x5, Pallas kernels, call(): pl.pallas_call(body, out_shape=[jax.ShapeDtypeStruct(s, d) for s, d in ou...  53.4 us
    ppermute x7, starting transfers between devices, turn(): lax.ppermute(x, 'mode', [(i, (i + by) % panels) for i in range(panels)])  12.7 us
    ppermute x7, waiting for transfers between devices, turn(): lax.ppermute(x, 'mode', [(i, (i + by) % panels) for i in range(panels)])  12.1 us
    all_to_all x1, waiting for transfers between devices, per_device(): received = lax.all_to_all(message, 'tile', 0, 0, tiled=True)  9.58 us
    all_to_all x1, starting transfers between devices, per_device(): received = lax.all_to_all(message, 'tile', 0, 0, tiled=True)  6.25 us
    ppermute x1, starting transfers between devices, per_device(): tail = lax.ppermute(mode_shapes[:, 0], 'tile', down)  5.75 us
    unnamed x21, local copies, waits for them, and re-layouts  3.45 us
  transfers between devices with their start and end apart: 10, of which 6 were waited for; matrix products, arithmetic and copies ran while one was open for 1% of the time, Pallas kernels for 30%

profile of v1, /device:TPU:4, one launch (start us, length us, event | category | flops | bytes accessed | tf_op | source)
XLA Modules:
  0.0 108.2 jit_solution(875367674309270196)
XLA Ops:
  0.0 1.1 %copy.13 = bf16[8,8,2048]{2,0,1:T(8,128)(2,1)S(1)} copy(bf16[8,8,2048]{2,1,0:T(8,128)(2,1)} %param.4) | data formatting | bytes 524288 | tf_op args[0]
  1.2 1.9 %collective-permute-start = (bf16[8,2048]{1,0:T(8,128)(2,1)S(1)}, bf16[8,2048]{1,0:T(8,128)(2,1)S(1)}, u32[]{:S(2)}, u32[]{:S(2)}) collective-permute-start(bf16[8,2048]{1,0:T(8,128)(2,1)S(1)} %get-tuple-element.23), channel_id=1, source_target_pairs={{0,8},{8,16},{16,24},{24,32},{32,40},{40,48},{48,56},{56,64},{64,7... | collective-permute-start | bytes 98312 | tf_op jit(solution)/shard_map/ppermute | solution.py:234
  3.1 5.8 %collective-permute-start.1 = (bf16[8,2048]{1,0:T(8,128)(2,1)S(1)}, bf16[8,2048]{1,0:T(8,128)(2,1)S(1)}, u32[]{:S(2)}, u32[]{:S(2)}) collective-permute-start(bf16[8,2048]{1,0:T(8,128)(2,1)S(1)} %get-tuple-element.24), channel_id=1, source_target_pairs={{8,0},{16,8},{24,16},{32,24},{40,32},{48,40},{56,48},{64,56},{72,6... | collective-permute-start | bytes 98312 | tf_op jit(solution)/shard_map/ppermute | solution.py:235
  8.8 0.0 collective-permute-done
  8.9 1.6 %collective-permute-done.1 = bf16[8,2048]{1,0:T(8,128)(2,1)S(1)} collective-permute-done((bf16[8,2048]{1,0:T(8,128)(2,1)S(1)}, bf16[8,2048]{1,0:T(8,128)(2,1)S(1)}, u32[]{:S(2)}, u32[]{:S(2)}) %collective-permute-start.1) | collective-permute-done | bytes 32800 | tf_op jit(solution)/shard_map/ppermute | solution.py:235
  10.5 2.0 %collective-permute-start.2 = (bf16[10,8,2048]{2,1,0:T(8,128)(2,1)S(1)}, bf16[10,8,2048]{2,1,0:T(8,128)(2,1)S(1)}, u32[]{:S(2)}, u32[]{:S(2)}) collective-permute-start(bf16[10,8,2048]{2,1,0:T(8,128)(2,1)S(1)} %pad_maximum_fusion.shapes), channel_id=1, source_target_pairs={{0,1},{1,2},{2,3},{3,4},{4,5},{5,6},{6,7},{7,0},{8,9},{9,10},{10,1... | collective-permute-start | bytes 983048 | tf_op jit(solution)/shard_map/ppermute | solution.py:232
  12.5 4.0 %collective-permute-start.4 = (bf16[10,8,2048]{2,1,0:T(8,128)(2,1)S(1)}, bf16[10,8,2048]{2,1,0:T(8,128)(2,1)S(1)}, u32[]{:S(2)}, u32[]{:S(2)}) collective-permute-start(bf16[10,8,2048]{2,1,0:T(8,128)(2,1)S(1)} %pad_maximum_fusion.shapes), channel_id=1, source_target_pairs={{0,7},{1,0},{2,1},{3,2},{4,3},{5,4},{6,5},{7,6},{8,15},{9,8},{10,9... | collective-permute-start | bytes 983048 | tf_op jit(solution)/shard_map/ppermute | solution.py:232
  16.5 7.4 %collective-permute-done.2.below = bf16[10,8,2048]{2,1,0:T(8,128)(2,1)S(1)} collective-permute-done((bf16[10,8,2048]{2,1,0:T(8,128)(2,1)S(1)}, bf16[10,8,2048]{2,1,0:T(8,128)(2,1)S(1)}, u32[]{:S(2)}, u32[]{:S(2)}) %collective-permute-start.2) | collective-permute-done | bytes 327712 | tf_op jit(solution)/shard_map/ppermute | solution.py:232
  23.9 0.0 collective-permute-start.3
  23.9 0.0 collective-permute-done.4.above
  23.9 3.2 %collective-permute-start.5 = (bf16[10,8,2048]{2,1,0:T(8,128)(2,1)S(1)}, bf16[10,8,2048]{2,1,0:T(8,128)(2,1)S(1)}, u32[]{:S(2)}, u32[]{:S(2)}) collective-permute-start(bf16[10,8,2048]{2,1,0:T(8,128)(2,1)S(1)} %collective-permute-done.4.above), channel_id=1, source_target_pairs={{0,7},{1,0},{2,1},{3,2},{4,3},{5,4},{6,5},{7,6},{8,15},{9,8},{10,9... | collective-permute-start | bytes 983048 | tf_op jit(solution)/shard_map/ppermute | solution.py:232
  27.1 13.8 %stage_own.1 = (bf16[3,8,8,2048]{3,2,1,0:T(8,128)(2,1)}, bf16[3,8,8,2048]{3,2,1,0:T(8,128)(2,1)}, f32[8,128]{1,0:T(8,128)}, f32[256,64]{1,0:T(8,128)}) custom-call(bf16[10,8,2048]{2,1,0:T(8,128)(2,1)} %copy-done.2, f32[8,2048]{1,0:T(8,128)} %stiff.5, s32[8,2048]{1,0:T(8,128)} %slot.5), custom_call_target="tpu_custom_call" | custom-call | tf_op jit(solution)/shard_map/stage_own/pallas_call | solution.py:211
  40.9 18.4 %stage_near.1 = (bf16[3,8,8,2048]{3,2,1,0:T(8,128)(2,1)}, bf16[3,8,8,2048]{3,2,1,0:T(8,128)(2,1)}, f32[8,128]{1,0:T(8,128)}, bf16[3,8,8,2048]{3,2,1,0:T(8,128)(2...) custom-call(bf16[10,8,2048]{2,1,0:T(8,128)(2,1)} %copy-done.3, ...), custom_call_target="tpu_custom_call" | custom-call | tf_op jit(solution)/shard_map/stage_near/pallas_call | solution.py:211
  59.3 0.0 collective-permute-done.3.below
  59.3 0.0 collective-permute-done.5.above
  59.3 0.7 copy-done.5
  60.0 0.1 copy-done.6
  60.1 17.1 %stage_far.1 = f32[32,8,640]{2,1,0:T(8,128)} custom-call(bf16[10,8,2048]{2,1,0:T(8,128)(2,1)} %copy-done.5, bf16[10,8,2048]{2,1,0:T(8,128)(2,1)} %copy-done.6, f32[8,2048]{1,0:T(8,128)} %stiff.5, s32[8,2048]{1,0:T(8,128)} %slot.5, bf16[3,8,8,2048]{3,2,1,0:T(8,128)(2,1)} %get-tuple-element.16.left_below, ...), custom_call_target="tpu_custom_call" | custom-call | tf_op jit(solution)/shard_map/stage_far/pallas_call | solution.py:211
  77.2 6.3 %all-to-all-start = ((f32[32,8,640]{2,1,0:T(8,128)}), f32[32,8,640]{2,1,0:T(8,128)S(1)}, u32[]{:S(2)}, u32[]{:S(2)}) async-start(f32[32,8,640]{2,1,0:T(8,128)} %stage_far.1), calls=%async_computation | async-start | bytes 1310720 | tf_op jit(solution)/shard_map/all_to_all | solution.py:263
  83.5 0.7 dynamic-slice_reduce_fusion
  84.2 0.7 reshape.12.lists
  84.8 9.6 %all-to-all-done = f32[32,8,640]{2,1,0:T(8,128)S(1)} async-done(((f32[32,8,640]{2,1,0:T(8,128)}), f32[32,8,640]{2,1,0:T(8,128)S(1)}, u32[]{:S(2)}, u32[]{:S(2)}) %all-to-all-start) | async-done | bytes 655392 | tf_op jit(solution)/shard_map/all_to_all | solution.py:263
  94.4 0.9 copy-done.1
  95.3 2.0 %gather_zones.1.mine = f32[24,512]{1,0:T(8,128)} custom-call(f32[256,640]{1,0:T(8,128)} %bitcast.11, s32[1,256]{1,0:T(1,128)} %reshape.12.lists), custom_call_target="tpu_custom_call" | custom-call | tf_op jit(solution)/shard_map/gather_zones/pallas_call | solution.py:211
  97.2 1.0 collective-permute-start.6
  98.2 1.0 collective-permute-start.7
  99.3 1.5 %collective-permute-start.8 = (f32[24,512]{1,0:T(8,128)}, f32[24,512]{1,0:T(8,128)S(1)}, u32[]{:S(2)}, u32[]{:S(2)}) collective-permute-start(f32[24,512]{1,0:T(8,128)} %gather_zones.1.mine), channel_id=1, source_target_pairs={{0,6},{1,7},{2,0},{3,1},{4,2},{5,3},{6,4},{7,5},{8,14},{9,15},{10,... | collective-permute-start | bytes 147464 | tf_op jit(solution)/shard_map/ppermute | solution.py:232
  100.7 0.8 collective-permute-done.6.from_above
  101.5 2.2 %collective-permute-done.7.from_below = f32[24,512]{1,0:T(8,128)S(1)} collective-permute-done((f32[24,512]{1,0:T(8,128)}, f32[24,512]{1,0:T(8,128)S(1)}, u32[]{:S(2)}, u32[]{:S(2)}) %collective-permute-start.7) | collective-permute-done | bytes 49184 | tf_op jit(solution)/shard_map/ppermute | solution.py:232
  103.8 1.6 %collective-permute-done.8.from_far = f32[24,512]{1,0:T(8,128)S(1)} collective-permute-done((f32[24,512]{1,0:T(8,128)}, f32[24,512]{1,0:T(8,128)S(1)}, u32[]{:S(2)}, u32[]{:S(2)}) %collective-permute-start.8) | collective-permute-done | bytes 49184 | tf_op jit(solution)/shard_map/ppermute | solution.py:232
  105.4 0.6 copy-done.9
  106.0 2.2 %normalise.1 = f32[16,8,64]{2,1,0:T(8,128)} custom-call(s32[1]{0:T(128)} %bitcast.place, f32[24,512]{1,0:T(8,128)} %gather_zones.1.mine, f32[24,512]{1,0:T(8,128)} %copy-done.7, f32[24,512]{1,0:T(8,128)} %copy-done.8, f32[24,512]{1,0:T(8,128)} %copy-done.9), custom_call_target="tpu_custom_call" | custom-call | tf_op jit(solution)/shard_map/normalise/pallas_call | solution.py:211
  (18 shorter events, 0.1 us)
Async XLA Ops:
  0.0 83.5 %copy-start = (s32[32,32,8]{1,2,0:T(8,128)S(1)}, s32[32,32,8]{1,2,0:T(8,128)}, u32[]{:S(2)}) copy-start(s32[32,32,8]{1,2,0:T(8,128)} %param.7) | copy-start | bytes 98308
  1.2 7.7 %collective-permute-start = (bf16[8,2048]{1,0:T(8,128)(2,1)S(1)}, bf16[8,2048]{1,0:T(8,128)(2,1)S(1)}, u32[]{:S(2)}, u32[]{:S(2)}) collective-permute-start(bf16[8,2048]{1,0:T(8,128)(2,1)S(1)} %get-tuple-element.23), channel_id=1, source_target_pairs={{0,8},{8,16},{16,24},{24,32},{32,40},{40,48},{48,56},{56,64},{64,7... | collective-permute-start | bytes 98312 | tf_op jit(solution)/shard_map/ppermute | solution.py:234
  3.1 7.3 %collective-permute-start.1 = (bf16[8,2048]{1,0:T(8,128)(2,1)S(1)}, bf16[8,2048]{1,0:T(8,128)(2,1)S(1)}, u32[]{:S(2)}, u32[]{:S(2)}) collective-permute-start(bf16[8,2048]{1,0:T(8,128)(2,1)S(1)} %get-tuple-element.24), channel_id=1, source_target_pairs={{8,0},{16,8},{24,16},{32,24},{40,32},{48,40},{56,48},{64,56},{72,6... | collective-permute-start | bytes 98312 | tf_op jit(solution)/shard_map/ppermute | solution.py:235
  10.5 16.6 %copy-start.2 = (bf16[10,8,2048]{2,1,0:T(8,128)(2,1)}, bf16[10,8,2048]{2,1,0:T(8,128)(2,1)S(1)}, u32[]{:S(2)}) copy-start(bf16[10,8,2048]{2,1,0:T(8,128)(2,1)S(1)} %pad_maximum_fusion.shapes) | copy-start | bytes 983044
  10.5 13.4 %collective-permute-start.2 = (bf16[10,8,2048]{2,1,0:T(8,128)(2,1)S(1)}, bf16[10,8,2048]{2,1,0:T(8,128)(2,1)S(1)}, u32[]{:S(2)}, u32[]{:S(2)}) collective-permute-start(bf16[10,8,2048]{2,1,0:T(8,128)(2,1)S(1)} %pad_maximum_fusion.shapes), channel_id=1, source_target_pairs={{0,1},{1,2},{2,3},{3,4},{4,5},{5,6},{6,7},{7,0},{8,9},{9,10},{10,1... | collective-permute-start | bytes 983048 | tf_op jit(solution)/shard_map/ppermute | solution.py:232
  12.5 11.4 %collective-permute-start.4 = (bf16[10,8,2048]{2,1,0:T(8,128)(2,1)S(1)}, bf16[10,8,2048]{2,1,0:T(8,128)(2,1)S(1)}, u32[]{:S(2)}, u32[]{:S(2)}) collective-permute-start(bf16[10,8,2048]{2,1,0:T(8,128)(2,1)S(1)} %pad_maximum_fusion.shapes), channel_id=1, source_target_pairs={{0,7},{1,0},{2,1},{3,2},{4,3},{5,4},{6,5},{7,6},{8,15},{9,8},{10,9... | collective-permute-start | bytes 983048 | tf_op jit(solution)/shard_map/ppermute | solution.py:232
  23.9 17.0 %copy-start.3 = (bf16[10,8,2048]{2,1,0:T(8,128)(2,1)}, bf16[10,8,2048]{2,1,0:T(8,128)(2,1)S(1)}, u32[]{:S(2)}) copy-start(bf16[10,8,2048]{2,1,0:T(8,128)(2,1)S(1)} %collective-permute-done.2.below) | copy-start | bytes 983044
  23.9 35.4 %collective-permute-start.3 = (bf16[10,8,2048]{2,1,0:T(8,128)(2,1)S(1)}, bf16[10,8,2048]{2,1,0:T(8,128)(2,1)S(1)}, u32[]{:S(2)}, u32[]{:S(2)}) collective-permute-start(bf16[10,8,2048]{2,1,0:T(8,128)(2,1)S(1)} %collective-permute-done.2.below), channel_id=1, source_target_pairs={{0,1},{1,2},{2,3},{3,4},{4,5},{5,6},{6,7},{7,0},{8,9},{9,10},{10,1... | collective-permute-start | bytes 983048 | tf_op jit(solution)/shard_map/ppermute | solution.py:232
  23.9 17.0 %copy-start.4 = (bf16[10,8,2048]{2,1,0:T(8,128)(2,1)}, bf16[10,8,2048]{2,1,0:T(8,128)(2,1)S(1)}, u32[]{:S(2)}) copy-start(bf16[10,8,2048]{2,1,0:T(8,128)(2,1)S(1)} %collective-permute-done.4.above) | copy-start | bytes 983044
  23.9 35.4 %collective-permute-start.5 = (bf16[10,8,2048]{2,1,0:T(8,128)(2,1)S(1)}, bf16[10,8,2048]{2,1,0:T(8,128)(2,1)S(1)}, u32[]{:S(2)}, u32[]{:S(2)}) collective-permute-start(bf16[10,8,2048]{2,1,0:T(8,128)(2,1)S(1)} %collective-permute-done.4.above), channel_id=1, source_target_pairs={{0,7},{1,0},{2,1},{3,2},{4,3},{5,4},{6,5},{7,6},{8,15},{9,8},{10,9... | collective-permute-start | bytes 983048 | tf_op jit(solution)/shard_map/ppermute | solution.py:232
  59.3 0.7 copy-start.5
  59.3 0.8 copy-start.6
  77.2 17.2 %all-to-all-start = ((f32[32,8,640]{2,1,0:T(8,128)}), f32[32,8,640]{2,1,0:T(8,128)S(1)}, u32[]{:S(2)}, u32[]{:S(2)}) async-start(f32[32,8,640]{2,1,0:T(8,128)} %stage_far.1), calls=%async_computation | async-start | bytes 1310720 | tf_op jit(solution)/shard_map/all_to_all | solution.py:263
  94.4 0.9 copy-start.1
  97.2 4.3 %collective-permute-start.6 = (f32[24,512]{1,0:T(8,128)}, f32[24,512]{1,0:T(8,128)S(1)}, u32[]{:S(2)}, u32[]{:S(2)}) collective-permute-start(f32[24,512]{1,0:T(8,128)} %gather_zones.1.mine), channel_id=1, source_target_pairs={{0,7},{1,0},{2,1},{3,2},{4,3},{5,4},{6,5},{7,6},{8,15},{9,8},{10,9... | collective-permute-start | bytes 147464 | tf_op jit(solution)/shard_map/ppermute | solution.py:232
  98.2 5.5 %collective-permute-start.7 = (f32[24,512]{1,0:T(8,128)}, f32[24,512]{1,0:T(8,128)S(1)}, u32[]{:S(2)}, u32[]{:S(2)}) collective-permute-start(f32[24,512]{1,0:T(8,128)} %gather_zones.1.mine), channel_id=1, source_target_pairs={{0,1},{1,2},{2,3},{3,4},{4,5},{5,6},{6,7},{7,0},{8,9},{9,10},{10,1... | collective-permute-start | bytes 147464 | tf_op jit(solution)/shard_map/ppermute | solution.py:232
  99.3 6.1 %collective-permute-start.8 = (f32[24,512]{1,0:T(8,128)}, f32[24,512]{1,0:T(8,128)S(1)}, u32[]{:S(2)}, u32[]{:S(2)}) collective-permute-start(f32[24,512]{1,0:T(8,128)} %gather_zones.1.mine), channel_id=1, source_target_pairs={{0,6},{1,7},{2,0},{3,1},{4,2},{5,3},{6,4},{7,5},{8,14},{9,15},{10,... | collective-permute-start | bytes 147464 | tf_op jit(solution)/shard_map/ppermute | solution.py:232
  101.5 3.9 %copy-start.7 = (f32[24,512]{1,0:T(8,128)}, f32[24,512]{1,0:T(8,128)S(1)}, u32[]{:S(2)}) copy-start(f32[24,512]{1,0:T(8,128)S(1)} %collective-permute-done.6.from_above) | copy-start | bytes 147460
  103.8 1.7 %copy-start.8 = (f32[24,512]{1,0:T(8,128)}, f32[24,512]{1,0:T(8,128)S(1)}, u32[]{:S(2)}) copy-start(f32[24,512]{1,0:T(8,128)S(1)} %collective-permute-done.7.from_below) | copy-start | bytes 147460
  105.4 0.6 copy-start.9

commit v2 on v1

--- a/solution.py
+++ b/solution.py
@@ -1,5 +1,3 @@
-import functools
-
 import jax
 import jax.numpy as jnp
 from jax import lax
@@ -7,32 +5,37 @@
 from jax.experimental.pallas import tpu as pltpu
 from jax.sharding import PartitionSpec as P
 
+
 ZONES = 512
 POISSON = 0.3
 SHEAR = 2.0 * (1.0 - POISSON)
 CHUNK = 512
+MERGE = 4
 
 f32 = jnp.float32
 bf16 = jnp.bfloat16
 
 
-def stencil(shapes, stiff, cross, second, bend_out, left_out, total_out):
+def stencil(shapes, stiff, plain, cross, second, bend_out, left_out, total_out):
     framed_rows, modes, cells = shapes.shape
     lane = lax.broadcasted_iota(jnp.int32, (modes, cells), 1)
-
-    def across(r, carry):
-        w = shapes[r].astype(f32)
-        right = jnp.where(lane == cells - 1, 0.0, pltpu.roll(w, cells - 1, 1))
-        left = jnp.where(lane == 0, 0.0, pltpu.roll(w, 1, 1))
-        cross[r] = right - left
-        second[r] = (right - 2.0 * w) + left
+    group = 5
+
+    def across(n, carry):
+        for k in range(group):
+            r = n * group + k
+            w = shapes[r].astype(f32)
+            right = jnp.where(lane == cells - 1, 0.0, pltpu.roll(w, cells - 1, 1))
+            left = jnp.where(lane == 0, 0.0, pltpu.roll(w, 1, 1))
+            plain[r] = w
+            cross[r] = right - left
+            second[r] = (right - 2.0 * w) + left
         return carry
 
-    lax.fori_loop(0, framed_rows, across, 0)
+    lax.fori_loop(0, framed_rows // group, across, 0)
 
     def along(r, total):
-        w = shapes[r + 1].astype(f32)
-        along_x = (shapes[r + 2].astype(f32) - 2.0 * w) + shapes[r].astype(f32)
+        along_x = (plain[r + 2] - 2.0 * plain[r + 1]) + plain[r]
         bent = [along_x, second[r + 1], 0.25 * (cross[r + 2] - cross[r])]
         rounded = [b.astype(bf16) for b in bent]
         bx, by, bt = [b.astype(f32) for b in rounded]
@@ -42,77 +45,95 @@
             bend_out[c, r] = rounded[c]
             if left_out is not None:
                 left_out[c, r] = weighted[c].astype(bf16)
-        if total_out is None:
-            return total
         energy = weighted[0] * bx + weighted[1] * by + weighted[2] * bt
         for k in range(cells // 128):
             total = total + energy[:, k * 128 : (k + 1) * 128]
         return total
 
     total = lax.fori_loop(0, framed_rows - 2, along, jnp.zeros((modes, 128), f32))
-    if total_out is not None:
-        total_out[...] = jnp.broadcast_to(jnp.sum(total, axis=1, keepdims=True), (modes, 128))
-
-
-def pair_sums(slot, blocks, rows_scratch, acc):
+    total_out[...] = jnp.broadcast_to(jnp.sum(total, axis=1, keepdims=True), (modes, 128))
+
+
+def pair_sums(slot, lefts, bends, blocks, wide, acc):
     rows, cells = slot.shape
-    slots = acc.shape[0]
-    per_row = cells // CHUNK
+    slots, width = acc.shape
+    pairs = bends[0].shape[2] ** 2
+    narrow = width == 2 * len(blocks) * pairs
     acc[...] = jnp.zeros_like(acc)
     slot_id = lax.broadcasted_iota(jnp.int32, (slots, CHUNK), 0).astype(f32).astype(bf16)
 
-    def step(n, carry):
-        r = n // per_row
-        first = pl.multiple_of((n % per_row) * CHUNK, CHUNK)
-        here = slot[pl.ds(r, 1), pl.ds(first, CHUNK)].astype(f32).astype(bf16)
-        member = jnp.where(
-            jnp.broadcast_to(here, (slots, CHUNK)) == slot_id,
-            jnp.ones((slots, CHUNK), bf16),
-            jnp.zeros((slots, CHUNK), bf16),
-        )
-        high, low = [], []
-        for index, (left, bend) in enumerate(blocks):
-            modes = left.shape[2]
+    def widen(r, carry):
+        for index, left in enumerate(lefts):
             for c in range(3):
-                rows_scratch[index, c] = left[c, r, :, pl.ds(first, CHUNK)].astype(f32)
-            right = [bend[c, r, :, pl.ds(first, CHUNK)].astype(f32) for c in range(3)]
-            for i in range(0, modes, 2):
-                pair = []
-                for k in (i, i + 1):
-                    spread = [
-                        jnp.broadcast_to(rows_scratch[index, c, pl.ds(k, 1), :], (modes, CHUNK))
-                        for c in range(3)
-                    ]
-                    pair.append(spread[0] * right[0] + spread[1] * right[1] + spread[2] * right[2])
-                product = jnp.concatenate(pair, axis=0)
-                top = product.astype(bf16)
-                high.append(top)
-                low.append((product - top.astype(f32)).astype(bf16))
-        contract = (((1,), (1,)), ((), ()))
-        acc[...] += lax.dot_general(
-            member, jnp.concatenate(high, axis=0), contract, preferred_element_type=f32
-        ) + lax.dot_general(
-            member, jnp.concatenate(low, axis=0), contract, preferred_element_type=f32
-        )
+                wide[index, c, r] = left[c, r].astype(f32)
         return carry
 
-    lax.fori_loop(0, rows * per_row, step, 0)
-
-
-def stage_own(shapes, stiff, slot, bend, left, total, sums, cross, second, rows_scratch):
-    stencil(shapes, stiff, cross, second, bend, left, total)
-    pair_sums(slot, [(left, bend)], rows_scratch, sums)
+    lax.fori_loop(0, rows, widen, 0)
+
+    def one_row(r, carry):
+        for base in range(0, cells, CHUNK * MERGE):
+            members, high, low = [], [], []
+            for first in range(base, base + CHUNK * MERGE, CHUNK):
+                cut = slice(first, first + CHUNK)
+                here = slot[pl.ds(r, 1), cut].astype(f32).astype(bf16)
+                members.append(
+                    jnp.where(
+                        jnp.broadcast_to(here, (slots, CHUNK)) == slot_id,
+                        jnp.ones((slots, CHUNK), bf16),
+                        jnp.zeros((slots, CHUNK), bf16),
+                    )
+                )
+                top, rest = [], []
+                for left, bend in blocks:
+                    right = [bends[bend][c, r, :, cut].astype(f32) for c in range(3)]
+                    modes = right[0].shape[0]
+                    for i in range(0, modes, 2):
+                        pair = []
+                        for k in (i, i + 1):
+                            spread = [
+                                jnp.broadcast_to(wide[left, c, r, pl.ds(k, 1), cut], (modes, CHUNK))
+                                for c in range(3)
+                            ]
+                            pair.append(
+                                spread[0] * right[0] + spread[1] * right[1] + spread[2] * right[2]
+                            )
+                        product = jnp.concatenate(pair, axis=0)
+                        top.append(product.astype(bf16))
+                        rest.append((product - top[-1].astype(f32)).astype(bf16))
+                high.append(jnp.concatenate(top, axis=0))
+                low.append(jnp.concatenate(rest, axis=0))
+            if narrow:
+                member = jnp.concatenate(members, axis=1)
+                product = jnp.concatenate(
+                    [jnp.concatenate(high, axis=1), jnp.concatenate(low, axis=1)], axis=0
+                )
+            else:
+                member = jnp.concatenate(members + members, axis=1)
+                product = jnp.concatenate(high + low, axis=1)
+            acc[...] += lax.dot_general(
+                member, product, (((1,), (1,)), ((), ())), preferred_element_type=f32
+            )
+        return carry
+
+    lax.fori_loop(0, rows, one_row, 0)
+
+
+def stage_own(shapes, stiff, slot, bend, left, total, sums, plain, cross, second, wide, acc):
+    stencil(shapes, stiff, plain, cross, second, bend, left, total)
+    pair_sums(slot, [left], [bend], [(0, 0)], wide, acc)
+    pairs = sums.shape[1]
+    sums[...] = acc[:, 0:pairs] + acc[:, pairs : 2 * pairs]
 
 
 def stage_near(
     below, above, stiff, slot, bend, left,
     bend_below, left_below, total_below, bend_above, left_above, total_above, sums,
-    cross, second, rows_scratch,
+    plain, cross, second, wide,
 ):
-    stencil(below, stiff, cross, second, bend_below, left_below, total_below)
-    stencil(above, stiff, cross, second, bend_above, left_above, total_above)
-    blocks = [(left_below, bend_above), (left_above, bend_below), (left, bend_above), (left, bend_below)]
-    pair_sums(slot, blocks, rows_scratch, sums)
+    stencil(below, stiff, plain, cross, second, bend_below, left_below, total_below)
+    stencil(above, stiff, plain, cross, second, bend_above, left_above, total_above)
+    blocks = [(0, 1), (1, 0), (2, 1), (2, 0)]
+    pair_sums(slot, [left_below, left_above, left], [bend_below, bend_above], blocks, wide, sums)
 
 
 def stage_far(
@@ -120,12 +141,12 @@
     total, total_below, total_above, own_sums, near_sums,
     message,
     bend_far_below, left_far_below, bend_far_above, total_far_below, total_far_above,
-    cross, second, rows_scratch, sums,
+    plain, cross, second, sums, wide,
 ):
-    stencil(below, stiff, cross, second, bend_far_below, left_far_below, total_far_below)
-    stencil(above, stiff, cross, second, bend_far_above, None, total_far_above)
-    blocks = [(left_below, bend_far_above), (left_above, bend_far_below), (left_far_below, bend_far_above)]
-    pair_sums(slot, blocks, rows_scratch, sums)
+    stencil(below, stiff, plain, cross, second, bend_far_below, left_far_below, total_far_below)
+    stencil(above, stiff, plain, cross, second, bend_far_above, None, total_far_above)
+    lefts = [left_below, left_above, left_far_below]
+    pair_sums(slot, lefts, [bend_far_below, bend_far_above], [(0, 1), (1, 0), (2, 1)], wide, sums)
     owners, entries, _ = message.shape
     message[:, :, 0:256] = near_sums[...].reshape(owners, entries, 256)
     message[:, :, 256:384] = sums[:, 0:128].reshape(owners, entries, 128)
@@ -214,7 +235,6 @@
         in_specs=specs,
         out_specs=[pl.BlockSpec(memory_space=pltpu.VMEM)] * len(outs),
         scratch_shapes=scratch,
-        name=body.__name__,
     )(*args)
 
 
@@ -239,32 +259,34 @@
     far_below = turn(below, 1)
     far_above = turn(above, -1)
 
+    lists = lax.dynamic_index_in_dim(slot_zone, lax.axis_index("tile"), 1, keepdims=False)
+    lists = lists.reshape(1, slots)
     factor = ((3, rows, modes, cells), bf16)
     total = ((modes, 128), f32)
-    lines = [vmem((rows + 2, modes, cells)), vmem((rows + 2, modes, cells))]
+    lines = [vmem((rows + 2, modes, cells))] * 3
     pairs = modes * modes
     bend0, left0, total0, own_sums = call(
         stage_own, [factor, factor, total, ((slots, pairs), f32)],
-        lines + [vmem((1, 3, modes, CHUNK))],
+        lines + [vmem((1, 3, rows, modes, cells)), vmem((slots, 2 * pairs))],
         framed, stiffness, node_slot,
     )
     _, left_below, total_below, _, left_above, total_above, near_sums = call(
         stage_near, [factor, factor, total, factor, factor, total, ((slots, 4 * pairs), f32)],
-        lines + [vmem((4, 3, modes, CHUNK))],
+        lines + [vmem((3, 3, rows, modes, cells))],
         below, above, stiffness, node_slot, bend0, left0,
     )
     (message,) = call(
         stage_far, [((tiles, entries, 8 * pairs + 128), f32)],
         [vmem(*factor), vmem(*factor), vmem(*factor), vmem(*total), vmem(*total)]
-        + lines + [vmem((3, 3, modes, CHUNK)), vmem((slots, 3 * pairs))],
+        + lines + [vmem((slots, 3 * pairs)), vmem((3, 3, rows, modes, cells))],
         far_below, far_above, stiffness, node_slot, left_below, left_above,
         total0, total_below, total_above, own_sums, near_sums,
     )
+    message, lists = lax.optimization_barrier((message, lists))
     received = lax.all_to_all(message, "tile", 0, 0, tiled=True)
-    lists = lax.dynamic_index_in_dim(slot_zone, lax.axis_index("tile"), 1, keepdims=False)
     (zoned,) = call(
         gather_zones, [((owned + 8, 8 * pairs), f32)], [],
-        received.reshape(slots, 8 * pairs + 128), lists.reshape(1, slots),
+        received.reshape(slots, 8 * pairs + 128), lists,
     )
     from_above = turn(zoned, -1)
     from_below = turn(zoned, 1)
@@ -279,6 +301,5 @@
 
 def solution(mesh):
     placed = (P("mode", "tile", None), P("tile", None), P("tile", None), P())
-    return jax.shard_map(
-        per_device, mesh=mesh, in_specs=placed, out_specs=P("tile", "mode", None), check_vma=False
-    )
+
+    return jax.shard_map(per_device, mesh=mesh, in_specs=placed, out_specs=P("tile", "mode", None), check_vma=False)

time: 110 us -> 90.2 us (0.82)
  Pallas kernels: 53.4 us -> 33.5 us
  blocking collectives: 0 us -> 17.3 us
  waiting for transfers between devices: 23.2 us -> 13.7 us
  starting transfers between devices: 26.7 us -> 20.4 us
    pallas_call x5, Pallas kernels: 53.4 us -> 33.5 us  [call(): pl.pallas_call(body, out_shape=[jax.ShapeDtypeStruct(s, d) for s, d in ou...]
    all_to_all x0 -> x1, blocking collectives: none -> 17.3 us  [per_device(): received = lax.all_to_all(message, 'tile', 0, 0, tiled=True)]
    all_to_all x1 -> x0, waiting for transfers between devices: 9.58 us -> none  [per_device(): received = lax.all_to_all(message, 'tile', 0, 0, tiled=True)]
    all_to_all x1 -> x0, starting transfers between devices: 6.25 us -> none  [per_device(): received = lax.all_to_all(message, 'tile', 0, 0, tiled=True)]
    unnamed x21 -> x19, local copies, waits for them, and re-layouts: 3.45 us -> 2.6 us
  transfers between devices with their start and end apart: 10 -> 9, of which waited for: 6 -> 5; matrix products, arithmetic and copies ran while one was open for 1% -> 1% of each run, Pallas kernels for 30% -> 21%
where the time goes in v2:
time: 90.2 us; the launch traced here: 88.9 us
  Pallas kernels  33.5 us (37%)
  starting transfers between devices  20.4 us (23%)
  blocking collectives  17.3 us (19%)
  waiting for transfers between devices  13.7 us (15%)
  local copies, waits for them, and re-layouts  3.93 us (4%)
    pallas_call x5, Pallas kernels, call(): pl.pallas_call(body, out_shape=[jax.ShapeDtypeStruct(s, d) for s, d in ou...  33.5 us
    all_to_all x1, blocking collectives, per_device(): received = lax.all_to_all(message, 'tile', 0, 0, tiled=True)  17.3 us
    ppermute x7, starting transfers between devices, turn(): lax.ppermute(x, 'mode', [(i, (i + by) % panels) for i in range(panels)])  12.7 us
    ppermute x7, waiting for transfers between devices, turn(): lax.ppermute(x, 'mode', [(i, (i + by) % panels) for i in range(panels)])  12.1 us
    ppermute x1, starting transfers between devices, per_device(): tail = lax.ppermute(mode_shapes[:, 0], 'tile', down)  5.75 us
    unnamed x19, local copies, waits for them, and re-layouts  2.6 us
    ppermute x1, starting transfers between devices, per_device(): head = lax.ppermute(mode_shapes[:, rows - 1], 'tile', up)  1.92 us
  transfers between devices with their start and end apart: 9, of which 5 were waited for; matrix products, arithmetic and copies ran while one was open for 1% of the time, Pallas kernels for 21%

profile of v2, /device:TPU:4, one launch (start us, length us, event | category | flops | bytes accessed | tf_op | source)
XLA Modules:
  0.0 88.9 jit_solution(6631876596349667484)
XLA Ops:
  0.0 0.0 copy-start
  0.0 1.1 %copy.13 = bf16[8,8,2048]{2,0,1:T(8,128)(2,1)S(1)} copy(bf16[8,8,2048]{2,1,0:T(8,128)(2,1)} %param.4) | data formatting | bytes 524288 | tf_op args[0]
  1.2 1.9 %collective-permute-start = (bf16[8,2048]{1,0:T(8,128)(2,1)S(1)}, bf16[8,2048]{1,0:T(8,128)(2,1)S(1)}, u32[]{:S(2)}, u32[]{:S(2)}) collective-permute-start(bf16[8,2048]{1,0:T(8,128)(2,1)S(1)} %get-tuple-element.27), channel_id=1, source_target_pairs={{0,8},{8,16},{16,24},{24,32},{32,40},{40,48},{48,56},{56,64},{64,7... | collective-permute-start | bytes 98312 | tf_op jit(solution)/shard_map/ppermute | solution.py:254
  3.1 5.8 %collective-permute-start.1 = (bf16[8,2048]{1,0:T(8,128)(2,1)S(1)}, bf16[8,2048]{1,0:T(8,128)(2,1)S(1)}, u32[]{:S(2)}, u32[]{:S(2)}) collective-permute-start(bf16[8,2048]{1,0:T(8,128)(2,1)S(1)} %get-tuple-element.28), channel_id=1, source_target_pairs={{8,0},{16,8},{24,16},{32,24},{40,32},{48,40},{56,48},{64,56},{72,6... | collective-permute-start | bytes 98312 | tf_op jit(solution)/shard_map/ppermute | solution.py:255
  8.8 0.0 collective-permute-done
  8.9 1.6 %collective-permute-done.1 = bf16[8,2048]{1,0:T(8,128)(2,1)S(1)} collective-permute-done((bf16[8,2048]{1,0:T(8,128)(2,1)S(1)}, bf16[8,2048]{1,0:T(8,128)(2,1)S(1)}, u32[]{:S(2)}, u32[]{:S(2)}) %collective-permute-start.1) | collective-permute-done | bytes 32800 | tf_op jit(solution)/shard_map/ppermute | solution.py:255
  10.5 0.0 copy-start.1
  10.5 2.0 %collective-permute-start.2 = (bf16[10,8,2048]{2,1,0:T(8,128)(2,1)S(1)}, bf16[10,8,2048]{2,1,0:T(8,128)(2,1)S(1)}, u32[]{:S(2)}, u32[]{:S(2)}) collective-permute-start(bf16[10,8,2048]{2,1,0:T(8,128)(2,1)S(1)} %pad_maximum_fusion.shapes), channel_id=1, source_target_pairs={{0,1},{1,2},{2,3},{3,4},{4,5},{5,6},{6,7},{7,0},{8,9},{9,10},{10,1... | collective-permute-start | bytes 983048 | tf_op jit(solution)/shard_map/ppermute | solution.py:252
  12.5 4.0 %collective-permute-start.4 = (bf16[10,8,2048]{2,1,0:T(8,128)(2,1)S(1)}, bf16[10,8,2048]{2,1,0:T(8,128)(2,1)S(1)}, u32[]{:S(2)}, u32[]{:S(2)}) collective-permute-start(bf16[10,8,2048]{2,1,0:T(8,128)(2,1)S(1)} %pad_maximum_fusion.shapes), channel_id=1, source_target_pairs={{0,7},{1,0},{2,1},{3,2},{4,3},{5,4},{6,5},{7,6},{8,15},{9,8},{10,9... | collective-permute-start | bytes 983048 | tf_op jit(solution)/shard_map/ppermute | solution.py:252
  16.5 7.4 %collective-permute-done.2.below = bf16[10,8,2048]{2,1,0:T(8,128)(2,1)S(1)} collective-permute-done((bf16[10,8,2048]{2,1,0:T(8,128)(2,1)S(1)}, bf16[10,8,2048]{2,1,0:T(8,128)(2,1)S(1)}, u32[]{:S(2)}, u32[]{:S(2)}) %collective-permute-start.2) | collective-permute-done | bytes 327712 | tf_op jit(solution)/shard_map/ppermute | solution.py:252
  23.9 0.0 collective-permute-start.3
  23.9 0.0 collective-permute-done.4.above
  23.9 3.2 %collective-permute-start.5 = (bf16[10,8,2048]{2,1,0:T(8,128)(2,1)S(1)}, bf16[10,8,2048]{2,1,0:T(8,128)(2,1)S(1)}, u32[]{:S(2)}, u32[]{:S(2)}) collective-permute-start(bf16[10,8,2048]{2,1,0:T(8,128)(2,1)S(1)} %collective-permute-done.4.above), channel_id=1, source_target_pairs={{0,7},{1,0},{2,1},{3,2},{4,3},{5,4},{6,5},{7,6},{8,15},{9,8},{10,9... | collective-permute-start | bytes 983048 | tf_op jit(solution)/shard_map/ppermute | solution.py:252
  27.1 0.7 dynamic-slice_reduce_fusion
  27.8 0.6 reshape.11.lists
  28.4 6.6 %shard_map.46 = (bf16[3,8,8,2048]{3,2,1,0:T(8,128)(2,1)}, bf16[3,8,8,2048]{3,2,1,0:T(8,128)(2,1)}, f32[8,128]{1,0:T(8,128)}, f32[256,64]{1,0:T(8,128)}) custom-call(bf16[10,8,2048]{2,1,0:T(8,128)(2,1)} %copy-done.1, f32[8,2048]{1,0:T(8,128)} %stiff.5, s32[8,2048]{1,0:T(8,128)} %slot.5), custom_call_target="tpu_custom_call" | custom-call | tf_op jit(solution)/shard_map/pallas_call | solution.py:232
  35.1 11.7 %shard_map.47 = (bf16[3,8,8,2048]{3,2,1,0:T(8,128)(2,1)}, bf16[3,8,8,2048]{3,2,1,0:T(8,128)(2,1)}, f32[8,128]{1,0:T(8,128)}, bf16[3,8,8,2048]{3,2,1,0:T(8,128)(2...) custom-call(bf16[10,8,2048]{2,1,0:T(8,128)(2,1)} %copy-done.2, ...), custom_call_target="tpu_custom_call" | custom-call | tf_op jit(solution)/shard_map/pallas_call | solution.py:232
  46.8 0.0 collective-permute-done.3.below
  46.8 0.0 collective-permute-done.5.above
  46.8 0.7 copy-done.4
  47.5 0.1 copy-done.5
  47.7 11.0 %shard_map.48 = f32[32,8,640]{2,1,0:T(8,128)} custom-call(bf16[10,8,2048]{2,1,0:T(8,128)(2,1)} %copy-done.4, bf16[10,8,2048]{2,1,0:T(8,128)(2,1)} %copy-done.5, f32[8,2048]{1,0:T(8,128)} %stiff.5, s32[8,2048]{1,0:T(8,128)} %slot.5, bf16[3,8,8,2048]{3,2,1,0:T(8,128)(2,1)} %get-tuple-element.18.left_below, ...), custom_call_target="tpu_custom_call" | custom-call | tf_op jit(solution)/shard_map/pallas_call | solution.py:232
  58.6 17.3 %all_to_all.5 = f32[32,8,640]{2,1,0:T(8,128)} all-to-all(f32[32,8,640]{2,1,0:T(8,128)} %shard_map.48), channel_id=1, replica_groups=mesh['tile'=32,'mode'=8] {'tile'}, dimensions={0} | all-to-all | bytes 1310720 | tf_op jit(solution)/shard_map/all_to_all | solution.py:286
  75.9 2.0 %shard_map.49.mine = f32[24,512]{1,0:T(8,128)} custom-call(f32[256,640]{1,0:T(8,128)} %bitcast.11, s32[1,256]{1,0:T(1,128)} %reshape.11.lists), custom_call_target="tpu_custom_call" | custom-call | tf_op jit(solution)/shard_map/pallas_call | solution.py:232
  77.9 1.0 %collective-permute-start.6 = (f32[24,512]{1,0:T(8,128)}, f32[24,512]{1,0:T(8,128)S(1)}, u32[]{:S(2)}, u32[]{:S(2)}) collective-permute-start(f32[24,512]{1,0:T(8,128)} %shard_map.49.mine), channel_id=1, source_target_pairs={{0,7},{1,0},{2,1},{3,2},{4,3},{5,4},{6,5},{7,6},{8,15},{9,8},{10,9... | collective-permute-start | bytes 147464 | tf_op jit(solution)/shard_map/ppermute | solution.py:252
  78.9 1.0 %collective-permute-start.7 = (f32[24,512]{1,0:T(8,128)}, f32[24,512]{1,0:T(8,128)S(1)}, u32[]{:S(2)}, u32[]{:S(2)}) collective-permute-start(f32[24,512]{1,0:T(8,128)} %shard_map.49.mine), channel_id=1, source_target_pairs={{0,1},{1,2},{2,3},{3,4},{4,5},{5,6},{6,7},{7,0},{8,9},{9,10},{10,1... | collective-permute-start | bytes 147464 | tf_op jit(solution)/shard_map/ppermute | solution.py:252
  79.9 1.5 %collective-permute-start.8 = (f32[24,512]{1,0:T(8,128)}, f32[24,512]{1,0:T(8,128)S(1)}, u32[]{:S(2)}, u32[]{:S(2)}) collective-permute-start(f32[24,512]{1,0:T(8,128)} %shard_map.49.mine), channel_id=1, source_target_pairs={{0,6},{1,7},{2,0},{3,1},{4,2},{5,3},{6,4},{7,5},{8,14},{9,15},{10,... | collective-permute-start | bytes 147464 | tf_op jit(solution)/shard_map/ppermute | solution.py:252
  81.4 0.8 collective-permute-done.6.from_above
  82.2 2.2 %collective-permute-done.7.from_below = f32[24,512]{1,0:T(8,128)S(1)} collective-permute-done((f32[24,512]{1,0:T(8,128)}, f32[24,512]{1,0:T(8,128)S(1)}, u32[]{:S(2)}, u32[]{:S(2)}) %collective-permute-start.7) | collective-permute-done | bytes 49184 | tf_op jit(solution)/shard_map/ppermute | solution.py:252
  84.4 1.7 %collective-permute-done.8.from_far = f32[24,512]{1,0:T(8,128)S(1)} collective-permute-done((f32[24,512]{1,0:T(8,128)}, f32[24,512]{1,0:T(8,128)S(1)}, u32[]{:S(2)}, u32[]{:S(2)}) %collective-permute-start.8) | collective-permute-done | bytes 49184 | tf_op jit(solution)/shard_map/ppermute | solution.py:252
  86.1 0.6 copy-done.8
  86.7 2.2 %shard_map.50 = f32[16,8,64]{2,1,0:T(8,128)} custom-call(s32[1]{0:T(128)} %bitcast.place, f32[24,512]{1,0:T(8,128)} %shard_map.49.mine, f32[24,512]{1,0:T(8,128)} %copy-done.6, f32[24,512]{1,0:T(8,128)} %copy-done.7, f32[24,512]{1,0:T(8,128)} %copy-done.8), custom_call_target="tpu_custom_call" | custom-call | tf_op jit(solution)/shard_map/pallas_call | solution.py:232
  (15 shorter events, 0.1 us)
Async XLA Ops:
  0.0 27.1 %copy-start = (s32[32,32,8]{1,2,0:T(8,128)S(1)}, s32[32,32,8]{1,2,0:T(8,128)}, u32[]{:S(2)}) copy-start(s32[32,32,8]{1,2,0:T(8,128)} %param.7) | copy-start | bytes 98308
  1.2 7.7 %collective-permute-start = (bf16[8,2048]{1,0:T(8,128)(2,1)S(1)}, bf16[8,2048]{1,0:T(8,128)(2,1)S(1)}, u32[]{:S(2)}, u32[]{:S(2)}) collective-permute-start(bf16[8,2048]{1,0:T(8,128)(2,1)S(1)} %get-tuple-element.27), channel_id=1, source_target_pairs={{0,8},{8,16},{16,24},{24,32},{32,40},{40,48},{48,56},{56,64},{64,7... | collective-permute-start | bytes 98312 | tf_op jit(solution)/shard_map/ppermute | solution.py:254
  3.1 7.3 %collective-permute-start.1 = (bf16[8,2048]{1,0:T(8,128)(2,1)S(1)}, bf16[8,2048]{1,0:T(8,128)(2,1)S(1)}, u32[]{:S(2)}, u32[]{:S(2)}) collective-permute-start(bf16[8,2048]{1,0:T(8,128)(2,1)S(1)} %get-tuple-element.28), channel_id=1, source_target_pairs={{8,0},{16,8},{24,16},{32,24},{40,32},{48,40},{56,48},{64,56},{72,6... | collective-permute-start | bytes 98312 | tf_op jit(solution)/shard_map/ppermute | solution.py:255
  10.5 18.0 %copy-start.1 = (bf16[10,8,2048]{2,1,0:T(8,128)(2,1)}, bf16[10,8,2048]{2,1,0:T(8,128)(2,1)S(1)}, u32[]{:S(2)}) copy-start(bf16[10,8,2048]{2,1,0:T(8,128)(2,1)S(1)} %pad_maximum_fusion.shapes) | copy-start | bytes 983044
  10.5 13.4 %collective-permute-start.2 = (bf16[10,8,2048]{2,1,0:T(8,128)(2,1)S(1)}, bf16[10,8,2048]{2,1,0:T(8,128)(2,1)S(1)}, u32[]{:S(2)}, u32[]{:S(2)}) collective-permute-start(bf16[10,8,2048]{2,1,0:T(8,128)(2,1)S(1)} %pad_maximum_fusion.shapes), channel_id=1, source_target_pairs={{0,1},{1,2},{2,3},{3,4},{4,5},{5,6},{6,7},{7,0},{8,9},{9,10},{10,1... | collective-permute-start | bytes 983048 | tf_op jit(solution)/shard_map/ppermute | solution.py:252
  12.5 11.4 %collective-permute-start.4 = (bf16[10,8,2048]{2,1,0:T(8,128)(2,1)S(1)}, bf16[10,8,2048]{2,1,0:T(8,128)(2,1)S(1)}, u32[]{:S(2)}, u32[]{:S(2)}) collective-permute-start(bf16[10,8,2048]{2,1,0:T(8,128)(2,1)S(1)} %pad_maximum_fusion.shapes), channel_id=1, source_target_pairs={{0,7},{1,0},{2,1},{3,2},{4,3},{5,4},{6,5},{7,6},{8,15},{9,8},{10,9... | collective-permute-start | bytes 983048 | tf_op jit(solution)/shard_map/ppermute | solution.py:252
  23.9 11.2 %copy-start.2 = (bf16[10,8,2048]{2,1,0:T(8,128)(2,1)}, bf16[10,8,2048]{2,1,0:T(8,128)(2,1)S(1)}, u32[]{:S(2)}) copy-start(bf16[10,8,2048]{2,1,0:T(8,128)(2,1)S(1)} %collective-permute-done.2.below) | copy-start | bytes 983044
  23.9 22.9 %collective-permute-start.3 = (bf16[10,8,2048]{2,1,0:T(8,128)(2,1)S(1)}, bf16[10,8,2048]{2,1,0:T(8,128)(2,1)S(1)}, u32[]{:S(2)}, u32[]{:S(2)}) collective-permute-start(bf16[10,8,2048]{2,1,0:T(8,128)(2,1)S(1)} %collective-permute-done.2.below), channel_id=1, source_target_pairs={{0,1},{1,2},{2,3},{3,4},{4,5},{5,6},{6,7},{7,0},{8,9},{9,10},{10,1... | collective-permute-start | bytes 983048 | tf_op jit(solution)/shard_map/ppermute | solution.py:252
  23.9 11.2 %copy-start.3 = (bf16[10,8,2048]{2,1,0:T(8,128)(2,1)}, bf16[10,8,2048]{2,1,0:T(8,128)(2,1)S(1)}, u32[]{:S(2)}) copy-start(bf16[10,8,2048]{2,1,0:T(8,128)(2,1)S(1)} %collective-permute-done.4.above) | copy-start | bytes 983044
  23.9 22.9 %collective-permute-start.5 = (bf16[10,8,2048]{2,1,0:T(8,128)(2,1)S(1)}, bf16[10,8,2048]{2,1,0:T(8,128)(2,1)S(1)}, u32[]{:S(2)}, u32[]{:S(2)}) collective-permute-start(bf16[10,8,2048]{2,1,0:T(8,128)(2,1)S(1)} %collective-permute-done.4.above), channel_id=1, source_target_pairs={{0,7},{1,0},{2,1},{3,2},{4,3},{5,4},{6,5},{7,6},{8,15},{9,8},{10,9... | collective-permute-start | bytes 983048 | tf_op jit(solution)/shard_map/ppermute | solution.py:252
  46.8 0.7 copy-start.4
  46.8 0.8 copy-start.5
  77.9 4.3 %collective-permute-start.6 = (f32[24,512]{1,0:T(8,128)}, f32[24,512]{1,0:T(8,128)S(1)}, u32[]{:S(2)}, u32[]{:S(2)}) collective-permute-start(f32[24,512]{1,0:T(8,128)} %shard_map.49.mine), channel_id=1, source_target_pairs={{0,7},{1,0},{2,1},{3,2},{4,3},{5,4},{6,5},{7,6},{8,15},{9,8},{10,9... | collective-permute-start | bytes 147464 | tf_op jit(solution)/shard_map/ppermute | solution.py:252
  78.9 5.5 %collective-permute-start.7 = (f32[24,512]{1,0:T(8,128)}, f32[24,512]{1,0:T(8,128)S(1)}, u32[]{:S(2)}, u32[]{:S(2)}) collective-permute-start(f32[24,512]{1,0:T(8,128)} %shard_map.49.mine), channel_id=1, source_target_pairs={{0,1},{1,2},{2,3},{3,4},{4,5},{5,6},{6,7},{7,0},{8,9},{9,10},{10,1... | collective-permute-start | bytes 147464 | tf_op jit(solution)/shard_map/ppermute | solution.py:252
  79.9 6.2 %collective-permute-start.8 = (f32[24,512]{1,0:T(8,128)}, f32[24,512]{1,0:T(8,128)S(1)}, u32[]{:S(2)}, u32[]{:S(2)}) collective-permute-start(f32[24,512]{1,0:T(8,128)} %shard_map.49.mine), channel_id=1, source_target_pairs={{0,6},{1,7},{2,0},{3,1},{4,2},{5,3},{6,4},{7,5},{8,14},{9,15},{10,... | collective-permute-start | bytes 147464 | tf_op jit(solution)/shard_map/ppermute | solution.py:252
  82.2 3.9 %copy-start.6 = (f32[24,512]{1,0:T(8,128)}, f32[24,512]{1,0:T(8,128)S(1)}, u32[]{:S(2)}) copy-start(f32[24,512]{1,0:T(8,128)S(1)} %collective-permute-done.6.from_above) | copy-start | bytes 147460
  84.4 1.7 %copy-start.7 = (f32[24,512]{1,0:T(8,128)}, f32[24,512]{1,0:T(8,128)S(1)}, u32[]{:S(2)}) copy-start(f32[24,512]{1,0:T(8,128)S(1)} %collective-permute-done.7.from_below) | copy-start | bytes 147460
  86.1 0.6 copy-start.8

commit v3 on v2

v3 whole, which is shorter than its diff:
```python
import jax
import jax.numpy as jnp
from jax import lax
from jax.experimental import pallas as pl
from jax.experimental.pallas import tpu as pltpu
from jax.sharding import PartitionSpec as P


ZONES = 512
POISSON = 0.3
SHEAR = 2.0 * (1.0 - POISSON)
CHUNK = 512

f32 = jnp.float32
bf16 = jnp.bfloat16


def stencil(shapes, stiff, lines, bend_out, left_out=None, total_out=None):
    framed_rows, modes, cells = shapes.shape
    plain, cross, second = lines
    lane = lax.broadcasted_iota(jnp.int32, (modes, cells), 1)
    group = 5

    def across(n, carry):
        for k in range(group):
            r = n * group + k
            w = shapes[r].astype(f32)
            right = jnp.where(lane == cells - 1, 0.0, pltpu.roll(w, cells - 1, 1))
            left = jnp.where(lane == 0, 0.0, pltpu.roll(w, 1, 1))
            plain[r] = w
            cross[r] = right - left
            second[r] = (right - 2.0 * w) + left
        return carry

    lax.fori_loop(0, framed_rows // group, across, 0)

    def along(r, total):
        along_x = (plain[r + 2] - 2.0 * plain[r + 1]) + plain[r]
        bent = [along_x, second[r + 1], 0.25 * (cross[r + 2] - cross[r])]
        bx, by, bt = [b.astype(bf16).astype(f32) for b in bent]
        for c, b in enumerate((bx, by, bt)):
            bend_out[c, r] = b
        if left_out is None and total_out is None:
            return total
        s = jnp.broadcast_to(stiff[pl.ds(r, 1), :], (modes, cells))
        weighted = [s * (bx + POISSON * by), s * (by + POISSON * bx), s * (SHEAR * bt)]
        if left_out is not None:
            for c in range(3):
                left_out[c, r] = weighted[c].astype(bf16).astype(f32)
        if total_out is None:
            return total
        energy = weighted[0] * bx + weighted[1] * by + weighted[2] * bt
        for k in range(cells // 128):
            total = total + energy[:, k * 128 : (k + 1) * 128]
        return total

    total = lax.fori_loop(0, framed_rows - 2, along, jnp.zeros((modes, 128), f32))
    if total_out is not None:
        total_out[...] = jnp.broadcast_to(jnp.sum(total, axis=1, keepdims=True), (modes, 128))


def pair_sums(slot, blocks, acc):
    rows, cells = slot.shape
    width, slots = acc.shape
    half = len(blocks) * blocks[0][0].shape[2] ** 2
    spare = [jnp.zeros((width - 2 * half, cells), bf16)] if width > 2 * half else []
    acc[...] = jnp.zeros_like(acc)
    slot_id = lax.broadcasted_iota(jnp.int32, (slots, CHUNK), 0).astype(f32).astype(bf16)

    def one_row(r, carry):
        members, high, low = [], [], []
        for first in range(0, cells, CHUNK):
            cut = slice(first, first + CHUNK)
            here = slot[pl.ds(r, 1), cut].astype(f32).astype(bf16)
            members.append(
                jnp.where(
                    jnp.broadcast_to(here, (slots, CHUNK)) == slot_id,
                    jnp.ones((slots, CHUNK), bf16),
                    jnp.zeros((slots, CHUNK), bf16),
                )
            )
            top, rest = [], []
            for left, bend in blocks:
                right = [bend[c, r, :, cut] for c in range(3)]
                modes = right[0].shape[0]
                for i in range(0, modes, 2):
                    pair = []
                    for k in (i, i + 1):
                        spread = [
                            jnp.broadcast_to(left[c, r, pl.ds(k, 1), cut], (modes, CHUNK))
                            for c in range(3)
                        ]
                        pair.append(spread[0] * right[0] + spread[1] * right[1] + spread[2] * right[2])
                    product = jnp.concatenate(pair, axis=0)
                    top.append(product.astype(bf16))
                    rest.append((product - top[-1].astype(f32)).astype(bf16))
            high.append(jnp.concatenate(top, axis=0))
            low.append(jnp.concatenate(rest, axis=0))
        products = jnp.concatenate(
            [jnp.concatenate(high, axis=1), jnp.concatenate(low, axis=1)] + spare, axis=0
        )
        acc[...] += lax.dot_general(
            products, jnp.concatenate(members, axis=1), (((1,), (1,)), ((), ())), preferred_element_type=f32
        )
        return carry

    lax.fori_loop(0, rows, one_row, 0, unroll=2)
    return jnp.transpose(acc[0:half, :] + acc[half : 2 * half, :])


def stage_own(shapes, stiff, slot, bend, left, total, sums, plain, cross, second, acc):
    stencil(shapes, stiff, (plain, cross, second), bend, left, total)
    sums[...] = pair_sums(slot, [(left, bend)], acc)


def stage_near(
    below, above, stiff, slot, bend, left,
    bend_above, left_above, total_above, sums,
    bend_below, plain, cross, second, acc,
):
    lines = (plain, cross, second)
    stencil(below, stiff, lines, bend_below)
    stencil(above, stiff, lines, bend_above, left_above, total_above)
    sums[...] = pair_sums(slot, [(left, bend_above), (left, bend_below)], acc)


def stage_far(
    below, above, stiff, slot, left, bend_above, left_above,
    total, total_above, own_sums, near_sums,
    message,
    bend_far_below, left_far_below, bend_far_above, total_far_below, total_far_above,
    plain, cross, second, acc,
):
    lines = (plain, cross, second)
    stencil(below, stiff, lines, bend_far_below, left_far_below, total_far_below)
    stencil(above, stiff, lines, bend_far_above, None, total_far_above)
    blocks = [
        (left, bend_far_above), (left, bend_far_below), (left_far_below, bend_above),
        (left_far_below, bend_far_above), (left_above, bend_far_below),
    ]
    sums = pair_sums(slot, blocks, acc)
    owners, entries, _ = message.shape
    message[:, :, 0:128] = near_sums[...].reshape(owners, entries, 128)
    message[:, :, 128:512] = jnp.concatenate([sums, own_sums[...]], axis=1).reshape(owners, entries, 384)
    lane = lax.broadcasted_iota(jnp.int32, total.shape, 1)
    places = jnp.zeros(total.shape, f32)
    for place, panel in enumerate([total, total_above, total_far_above, total_far_below]):
        places = jnp.where(lane == place, panel[...], places)
    message[:, :, 512:640] = jnp.broadcast_to(places[None], (owners, entries, 128))


def three_parts(x):
    a = x.astype(bf16)
    rest = x - a.astype(f32)
    b = rest.astype(bf16)
    return a, b, (rest - b.astype(f32)).astype(bf16)


def exact_dot(x, y, parts_of_y):
    if parts_of_y:
        return sum(jnp.dot(x, part, preferred_element_type=f32) for part in three_parts(y))
    return sum(jnp.dot(part, y, preferred_element_type=f32) for part in three_parts(x))


def gather_zones(received, lists, mine, to_far, to_next):
    places, width = received.shape
    zones = mine.shape[0]
    body = width - 128
    chosen = jnp.broadcast_to(lists[...], (zones, places)) == lax.broadcasted_iota(
        jnp.int32, (zones, places), 0
    )
    chosen = jnp.where(chosen, 1.0, 0.0).astype(bf16)
    zoned = exact_dot(chosen, received[:, 0:body], True)
    totals = jnp.sum(received[:, body:].reshape(places // 8, 8, 128), axis=0)
    mine[...] = zoned[:, 0:256]
    to_far[0:zones, :] = zoned[:, 256:384]
    to_far[zones:, :] = totals
    to_next[0:zones, :] = zoned[:, 384:512]
    to_next[zones:, :] = totals


def normalise(place, mine, kept, from_far, from_below, energy):
    zones = energy.shape[0]
    z = slice(0, zones)
    t = slice(zones, zones + 8)
    sums = jnp.concatenate(
        [
            kept[z, 64:128], mine[:, 0:64], mine[:, 128:192], from_far[z, 0:64],
            from_far[z, 64:128], from_below[z, 0:64], mine[:, 192:256], mine[:, 64:128],
        ],
        axis=1,
    )
    own, far, below = kept[t, :], from_far[t, :], from_below[t, :]
    columns = [
        own[:, 0:1], own[:, 1:2], own[:, 2:3], far[:, 1:2],
        far[:, 2:3], below[:, 3:4], own[:, 3:4], below[:, 0:1],
    ]
    spread = jnp.concatenate([jnp.broadcast_to(c, (8, 64)) for c in columns], axis=1)
    sub = lax.broadcasted_iota(jnp.int32, (8, 512), 0)
    lane = lax.broadcasted_iota(jnp.int32, (8, 512), 1)
    total_j = jnp.sum(jnp.where(lane % 8 == sub, spread, 0.0), axis=0, keepdims=True)
    total_i = jnp.sum(
        jnp.where((lane // 8) % 8 == sub, jnp.broadcast_to(own[:, 0:1], (8, 512)), 0.0), axis=0, keepdims=True
    )
    scaled = ZONES * (0.5 * sums) / jnp.sqrt((0.5 * total_i) * (0.5 * total_j))
    r = lax.broadcasted_iota(jnp.int32, (512, 512), 0)
    c = lax.broadcasted_iota(jnp.int32, (512, 512), 1)
    panel = (r // 64 + place[0]) % 8
    target = ((r // 8) % 8) * 64 + panel * 8 + r % 8
    order = jnp.where(c == target, 1.0, 0.0).astype(bf16)
    ordered = exact_dot(scaled, order, False)
    for i in range(8):
        energy[:, i, :] = ordered[:, i * 64 : (i + 1) * 64]


def vmem(shape, dtype=f32):
    return pltpu.VMEM(shape, dtype)


def call(body, outs, scratch, *args, scalars=0):
    specs = [pl.BlockSpec(memory_space=pltpu.SMEM)] * scalars + [
        pl.BlockSpec(memory_space=pltpu.VMEM)
    ] * (len(args) - scalars)
    return pl.pallas_call(
        body,
        out_shape=[jax.ShapeDtypeStruct(s, d) for s, d in outs],
        in_specs=specs,
        out_specs=[pl.BlockSpec(memory_space=pltpu.VMEM)] * len(outs),
        scratch_shapes=scratch,
        compiler_params=pltpu.CompilerParams(vmem_limit_bytes=24 << 20),
    )(*args)


def per_device(mode_shapes, stiffness, node_slot, slot_zone):
    modes, rows, cells = mode_shapes.shape
    tiles = lax.axis_size("tile")
    panels = lax.axis_size("mode")
    entries = slot_zone.shape[2]
    slots = tiles * entries
    owned = ZONES // tiles
    up = [(i, i + 1) for i in range(tiles - 1)]
    down = [(i + 1, i) for i in range(tiles - 1)]

    def turn(x, by):
        return lax.ppermute(x, "mode", [(i, (i + by) % panels) for i in range(panels)])

    lists = lax.dynamic_index_in_dim(slot_zone, lax.axis_index("tile"), 1, keepdims=False)
    lists = lists.reshape(1, slots)
    head = lax.ppermute(mode_shapes[:, rows - 1], "tile", up)
    tail = lax.ppermute(mode_shapes[:, 0], "tile", down)
    framed = jnp.concatenate([head[None], jnp.transpose(mode_shapes, (1, 0, 2)), tail[None]], axis=0)
    framed, lists = lax.optimization_barrier((framed, lists))
    below = turn(framed, 1)
    above = turn(framed, -1)
    far_below = turn(below, 1)
    far_above = turn(above, -1)

    factor = ((3, rows, modes, cells), f32)
    total = ((modes, 128), f32)
    lines = [vmem((rows + 2, modes, cells))] * 3
    pairs = modes * modes
    bend0, left0, total0, own_sums = call(
        stage_own, [factor, factor, total, ((slots, pairs), f32)],
        lines + [vmem((2 * pairs, slots))],
        framed, stiffness, node_slot,
    )
    bend_above, left_above, total_above, near_sums = call(
        stage_near, [factor, factor, total, ((slots, 2 * pairs), f32)],
        [vmem(*factor)] + lines + [vmem((4 * pairs, slots))],
        below, above, stiffness, node_slot, bend0, left0,
    )
    (message,) = call(
        stage_far, [((tiles, entries, 8 * pairs + 128), f32)],
        [vmem(*factor)] * 3 + [vmem(*total)] * 2 + lines + [vmem((10 * pairs, slots))],
        far_below, far_above, stiffness, node_slot, left0, bend_above, left_above,
        total0, total_above, own_sums, near_sums,
    )
    message, lists = lax.optimization_barrier((message, lists))
    received = lax.all_to_all(message, "tile", 0, 0, tiled=True)
    mine, to_far, to_next = call(
        gather_zones,
        [((owned, 4 * pairs), f32), ((owned + 8, 2 * pairs), f32), ((owned + 8, 2 * pairs), f32)], [],
        received.reshape(slots, 8 * pairs + 128), lists,
    )
    from_far = turn(to_far, -2)
    from_below = turn(to_next, 1)
    place = lax.axis_index("mode").astype(jnp.int32).reshape(1)
    (energy,) = call(
        normalise, [((owned, modes, panels * modes), f32)], [],
        place, mine, to_next, from_far, from_below, scalars=1,
    )
    return energy


def solution(mesh):
    placed = (P("mode", "tile", None), P("tile", None), P("tile", None), P())

    return jax.shard_map(per_device, mesh=mesh, in_specs=placed, out_specs=P("tile", "mode", None), check_vma=False)
```

time: 90.2 us -> 75.5 us (0.84)
  the two profiles are of different devices: /device:TPU:4 before, /device:TPU:1 now
where the time goes in v3:
time: 75.5 us; the launch traced here: 75.2 us
  Pallas kernels  21.5 us (28%)
  blocking collectives  21.3 us (28%)
  starting transfers between devices  17.2 us (23%)
  waiting for transfers between devices  11.5 us (15%)
  local copies, waits for them, and re-layouts  3.6 us (5%)
    pallas_call x5, Pallas kernels, call(): pl.pallas_call(body, out_shape=[jax.ShapeDtypeStruct(s, d) for s, d in ou...  21.5 us
    all_to_all x1, blocking collectives, per_device(): received = lax.all_to_all(message, 'tile', 0, 0, tiled=True)  21.3 us
    ppermute x6, starting transfers between devices, turn(): lax.ppermute(x, 'mode', [(i, (i + by) % panels) for i in range(panels)])  10.7 us
    ppermute x6, waiting for transfers between devices, turn(): lax.ppermute(x, 'mode', [(i, (i + by) % panels) for i in range(panels)])  8.97 us
    ppermute x1, starting transfers between devices, per_device(): head = lax.ppermute(mode_shapes[:, rows - 1], 'tile', up)  4.58 us
    unnamed x7, local copies, waits for them, and re-layouts  2.82 us
    ppermute x1, waiting for transfers between devices, per_device(): tail = lax.ppermute(mode_shapes[:, 0], 'tile', down)  2.5 us
    ppermute x1, starting transfers between devices, per_device(): tail = lax.ppermute(mode_shapes[:, 0], 'tile', down)  1.92 us
  transfers between devices with their start and end apart: 8, of which 4 were waited for; matrix products, arithmetic and copies ran while one was open for 1% of the time, Pallas kernels for 13%

profile of v3, /device:TPU:1, one launch (start us, length us, event | category | flops | bytes accessed | tf_op | source)
XLA Modules:
  0.0 75.2 jit_solution(8939174561277265647)
XLA Ops:
  0.0 0.0 copy-start
  0.0 1.1 %copy.13 = bf16[8,8,2048]{2,0,1:T(8,128)(2,1)S(1)} copy(bf16[8,8,2048]{2,1,0:T(8,128)(2,1)} %param.4) | data formatting | bytes 524288 | tf_op args[0]
  1.2 4.6 %collective-permute-start = (bf16[8,2048]{1,0:T(8,128)(2,1)S(1)}, bf16[8,2048]{1,0:T(8,128)(2,1)S(1)}, u32[]{:S(2)}, u32[]{:S(2)}) collective-permute-start(bf16[8,2048]{1,0:T(8,128)(2,1)S(1)} %get-tuple-element.35), channel_id=1, source_target_pairs={{0,8},{8,16},{16,24},{24,32},{32,40},{40,48},{48,56},{56,64},{64,7... | collective-permute-start | bytes 98312 | tf_op jit(solution)/shard_map/ppermute | solution.py:249
  5.7 1.9 %collective-permute-start.1 = (bf16[8,2048]{1,0:T(8,128)(2,1)S(1)}, bf16[8,2048]{1,0:T(8,128)(2,1)S(1)}, u32[]{:S(2)}, u32[]{:S(2)}) collective-permute-start(bf16[8,2048]{1,0:T(8,128)(2,1)S(1)} %get-tuple-element.36), channel_id=1, source_target_pairs={{8,0},{16,8},{24,16},{32,24},{40,32},{48,40},{56,48},{64,56},{72,6... | collective-permute-start | bytes 98312 | tf_op jit(solution)/shard_map/ppermute | solution.py:250
  7.7 0.0 copy-done
  7.7 0.7 dynamic-slice_reduce_fusion
  8.4 0.1 reshape.11.lists
  8.5 0.0 collective-permute-done
  8.5 2.5 %collective-permute-done.1 = bf16[8,2048]{1,0:T(8,128)(2,1)S(1)} collective-permute-done((bf16[8,2048]{1,0:T(8,128)(2,1)S(1)}, bf16[8,2048]{1,0:T(8,128)(2,1)S(1)}, u32[]{:S(2)}, u32[]{:S(2)}) %collective-permute-start.1) | collective-permute-done | bytes 32800 | tf_op jit(solution)/shard_map/ppermute | solution.py:250
  11.0 1.7 %collective-permute-start.2 = (bf16[10,8,2048]{2,1,0:T(8,128)(2,1)S(1)}, bf16[10,8,2048]{2,1,0:T(8,128)(2,1)S(1)}, u32[]{:S(2)}, u32[]{:S(2)}) collective-permute-start(bf16[10,8,2048]{2,1,0:T(8,128)(2,1)S(1)} %pad_maximum_fusion.shapes), channel_id=1, source_target_pairs={{0,1},{1,2},{2,3},{3,4},{4,5},{5,6},{6,7},{7,0},{8,9},{9,10},{10,1... | collective-permute-start | bytes 983048 | tf_op jit(solution)/shard_map/ppermute | solution.py:245
  12.7 4.0 %collective-permute-start.4 = (bf16[10,8,2048]{2,1,0:T(8,128)(2,1)S(1)}, bf16[10,8,2048]{2,1,0:T(8,128)(2,1)S(1)}, u32[]{:S(2)}, u32[]{:S(2)}) collective-permute-start(bf16[10,8,2048]{2,1,0:T(8,128)(2,1)S(1)} %pad_maximum_fusion.shapes), channel_id=1, source_target_pairs={{0,7},{1,0},{2,1},{3,2},{4,3},{5,4},{6,5},{7,6},{8,15},{9,8},{10,9... | collective-permute-start | bytes 983048 | tf_op jit(solution)/shard_map/ppermute | solution.py:245
  16.8 5.9 %collective-permute-done.2.below = bf16[10,8,2048]{2,1,0:T(8,128)(2,1)S(1)} collective-permute-done((bf16[10,8,2048]{2,1,0:T(8,128)(2,1)S(1)}, bf16[10,8,2048]{2,1,0:T(8,128)(2,1)S(1)}, u32[]{:S(2)}, u32[]{:S(2)}) %collective-permute-start.2) | collective-permute-done | bytes 327712 | tf_op jit(solution)/shard_map/ppermute | solution.py:245
  22.7 0.0 collective-permute-start.3
  22.7 0.0 collective-permute-done.4.above
  22.7 3.0 %collective-permute-start.5 = (bf16[10,8,2048]{2,1,0:T(8,128)(2,1)S(1)}, bf16[10,8,2048]{2,1,0:T(8,128)(2,1)S(1)}, u32[]{:S(2)}, u32[]{:S(2)}) collective-permute-start(bf16[10,8,2048]{2,1,0:T(8,128)(2,1)S(1)} %collective-permute-done.4.above), channel_id=1, source_target_pairs={{0,7},{1,0},{2,1},{3,2},{4,3},{5,4},{6,5},{7,6},{8,15},{9,8},{10,9... | collective-permute-start | bytes 983048 | tf_op jit(solution)/shard_map/ppermute | solution.py:245
  25.8 0.0 copy-start.1
  25.8 0.8 %copy-done.1 = f32[8,2048]{1,0:T(8,128)S(1)} copy-done((f32[8,2048]{1,0:T(8,128)S(1)}, f32[8,2048]{1,0:T(8,128)}, u32[]{:S(2)}) %copy-start.1) | copy-done | bytes 65560
  26.6 0.0 copy-start.2
  26.6 0.8 %copy-done.2 = s32[8,2048]{1,0:T(8,128)S(1)} copy-done((s32[8,2048]{1,0:T(8,128)S(1)}, s32[8,2048]{1,0:T(8,128)}, u32[]{:S(2)}) %copy-start.2) | copy-done | bytes 65560
  27.4 4.5 %shard_map.46 = (f32[3,8,8,2048]{3,2,1,0:T(8,128)S(1)}, f32[3,8,8,2048]{3,2,1,0:T(8,128)S(1)}, f32[8,128]{1,0:T(8,128)S(1)}, f32[256,64]{1,0:T(8,128)S(1)}) custom-call(bf16[10,8,2048]{2,1,0:T(8,128)(2,1)S(1)} %pad_maximum_fusion.shapes, f32[8,2048]{1,0:T(8,128)S(1)} %copy-done.1, s32[8,2048]{1,0:T(8,128)S(1)} %copy-done.2), custom_call_target="tpu_custom_call" | custom-call | tf_op jit(solution)/shard_map/pallas_call | solution.py:224
  31.9 5.5 %shard_map.47 = (f32[3,8,8,2048]{3,2,1,0:T(8,128)S(1)}, f32[3,8,8,2048]{3,2,1,0:T(8,128)S(1)}, f32[8,128]{1,0:T(8,128)S(1)}, f32[256,128]{1,0:T(8,128)S(1)}) custom-call(bf16[10,8,2048]{2,1,0:T(8,128)(2,1)S(1)} %collective-permute-done.2.below, bf16[10,8,2048]{2,1,0:T(8,128)(2,1)S(1)} %collective-permute-done.4.above, f32[8,2048]{1,0:T(8,128)S(1)} %copy-done.1, ...), custom_call_target="tpu_custom_call" | custom-call | tf_op jit(solution)/shard_map/pallas_call | solution.py:224
  37.4 0.0 collective-permute-done.3.below
  37.4 0.0 collective-permute-done.5.above
  37.4 10.0 %shard_map.48 = f32[32,8,640]{2,1,0:T(8,128)S(1)} custom-call(bf16[10,8,2048]{2,1,0:T(8,128)(2,1)S(1)} %collective-permute-done.3.below, bf16[10,8,2048]{2,1,0:T(8,128)(2,1)S(1)} %collective-permute-done.5.above, f32[8,2048]{1,0:T(8,128)S(1)} %copy-done.1, s32[8,2048]{1,0:T(8,128)S(1)} %copy-done.2, f32[3,8,8,2048]{3,2,1,0:T(8,128)S(1)} %get-tuple-element.21.left, ...), custom_call_target="tpu_custom_call" | custom-call | tf_op jit(solution)/shard_map/pallas_call | solution.py:224
  47.4 21.3 %all_to_all.5 = f32[32,8,640]{2,1,0:T(8,128)S(1)} all-to-all(f32[32,8,640]{2,1,0:T(8,128)S(1)} %shard_map.48), channel_id=1, replica_groups=mesh['tile'=32,'mode'=8] {'tile'}, dimensions={0} | all-to-all | bytes 1310720 | tf_op jit(solution)/shard_map/all_to_all | solution.py:279
  68.7 0.3 shard_map.49
  68.9 1.2 %collective-permute-start.6 = (f32[24,128]{1,0:T(8,128)S(1)}, f32[24,128]{1,0:T(8,128)S(1)}, u32[]{:S(2)}, u32[]{:S(2)}) collective-permute-start(f32[24,128]{1,0:T(8,128)S(1)} %get-tuple-element.34), channel_id=1, source_target_pairs={{0,6},{1,7},{2,0},{3,1},{4,2},{5,3},{6,4},{7,5},{8,14},{9,15},{10,... | collective-permute-start | bytes 36872 | tf_op jit(solution)/shard_map/ppermute | solution.py:245
  70.1 0.7 collective-permute-start.7
  70.8 1.5 %collective-permute-done.6.from_far = f32[24,128]{1,0:T(8,128)S(1)} collective-permute-done((f32[24,128]{1,0:T(8,128)S(1)}, f32[24,128]{1,0:T(8,128)S(1)}, u32[]{:S(2)}, u32[]{:S(2)}) %collective-permute-start.6) | collective-permute-done | bytes 12320 | tf_op jit(solution)/shard_map/ppermute | solution.py:245
  72.4 1.5 %collective-permute-done.7.from_below = f32[24,128]{1,0:T(8,128)S(1)} collective-permute-done((f32[24,128]{1,0:T(8,128)S(1)}, f32[24,128]{1,0:T(8,128)S(1)}, u32[]{:S(2)}, u32[]{:S(2)}) %collective-permute-start.7) | collective-permute-done | bytes 12320 | tf_op jit(solution)/shard_map/ppermute | solution.py:245
  73.9 1.3 %shard_map.50 = f32[16,8,64]{2,1,0:T(8,128)} custom-call(s32[1]{0:T(128)} %bitcast.place, f32[16,256]{1,0:T(8,128)S(1)} %get-tuple-element.32.mine, f32[24,128]{1,0:T(8,128)S(1)} %get-tuple-element.33.kept, f32[24,128]{1,0:T(8,128)S(1)} %collective-permute-done.6.from_far, f32[24,128]{1,0:T(8,128)S(1)} %collective-permute-done.7.from_below), custom_call_target="tpu_custom_call" | custom-call | tf_op jit(solution)/shard_map/pallas_call | solution.py:224
  (2 shorter events, 0.1 us)
Async XLA Ops:
  0.0 7.7 %copy-start = (s32[32,32,8]{1,2,0:T(8,128)S(1)}, s32[32,32,8]{1,2,0:T(8,128)}, u32[]{:S(2)}) copy-start(s32[32,32,8]{1,2,0:T(8,128)} %param.7) | copy-start | bytes 98308
  1.2 7.3 %collective-permute-start = (bf16[8,2048]{1,0:T(8,128)(2,1)S(1)}, bf16[8,2048]{1,0:T(8,128)(2,1)S(1)}, u32[]{:S(2)}, u32[]{:S(2)}) collective-permute-start(bf16[8,2048]{1,0:T(8,128)(2,1)S(1)} %get-tuple-element.35), channel_id=1, source_target_pairs={{0,8},{8,16},{16,24},{24,32},{32,40},{40,48},{48,56},{56,64},{64,7... | collective-permute-start | bytes 98312 | tf_op jit(solution)/shard_map/ppermute | solution.py:249
  5.7 5.2 %collective-permute-start.1 = (bf16[8,2048]{1,0:T(8,128)(2,1)S(1)}, bf16[8,2048]{1,0:T(8,128)(2,1)S(1)}, u32[]{:S(2)}, u32[]{:S(2)}) collective-permute-start(bf16[8,2048]{1,0:T(8,128)(2,1)S(1)} %get-tuple-element.36), channel_id=1, source_target_pairs={{8,0},{16,8},{24,16},{32,24},{40,32},{48,40},{56,48},{64,56},{72,6... | collective-permute-start | bytes 98312 | tf_op jit(solution)/shard_map/ppermute | solution.py:250
  11.0 11.7 %collective-permute-start.2 = (bf16[10,8,2048]{2,1,0:T(8,128)(2,1)S(1)}, bf16[10,8,2048]{2,1,0:T(8,128)(2,1)S(1)}, u32[]{:S(2)}, u32[]{:S(2)}) collective-permute-start(bf16[10,8,2048]{2,1,0:T(8,128)(2,1)S(1)} %pad_maximum_fusion.shapes), channel_id=1, source_target_pairs={{0,1},{1,2},{2,3},{3,4},{4,5},{5,6},{6,7},{7,0},{8,9},{9,10},{10,1... | collective-permute-start | bytes 983048 | tf_op jit(solution)/shard_map/ppermute | solution.py:245
  12.7 10.0 %collective-permute-start.4 = (bf16[10,8,2048]{2,1,0:T(8,128)(2,1)S(1)}, bf16[10,8,2048]{2,1,0:T(8,128)(2,1)S(1)}, u32[]{:S(2)}, u32[]{:S(2)}) collective-permute-start(bf16[10,8,2048]{2,1,0:T(8,128)(2,1)S(1)} %pad_maximum_fusion.shapes), channel_id=1, source_target_pairs={{0,7},{1,0},{2,1},{3,2},{4,3},{5,4},{6,5},{7,6},{8,15},{9,8},{10,9... | collective-permute-start | bytes 983048 | tf_op jit(solution)/shard_map/ppermute | solution.py:245
  22.7 14.7 %collective-permute-start.3 = (bf16[10,8,2048]{2,1,0:T(8,128)(2,1)S(1)}, bf16[10,8,2048]{2,1,0:T(8,128)(2,1)S(1)}, u32[]{:S(2)}, u32[]{:S(2)}) collective-permute-start(bf16[10,8,2048]{2,1,0:T(8,128)(2,1)S(1)} %collective-permute-done.2.below), channel_id=1, source_target_pairs={{0,1},{1,2},{2,3},{3,4},{4,5},{5,6},{6,7},{7,0},{8,9},{9,10},{10,1... | collective-permute-start | bytes 983048 | tf_op jit(solution)/shard_map/ppermute | solution.py:245
  22.7 14.7 %collective-permute-start.5 = (bf16[10,8,2048]{2,1,0:T(8,128)(2,1)S(1)}, bf16[10,8,2048]{2,1,0:T(8,128)(2,1)S(1)}, u32[]{:S(2)}, u32[]{:S(2)}) collective-permute-start(bf16[10,8,2048]{2,1,0:T(8,128)(2,1)S(1)} %collective-permute-done.4.above), channel_id=1, source_target_pairs={{0,7},{1,0},{2,1},{3,2},{4,3},{5,4},{6,5},{7,6},{8,15},{9,8},{10,9... | collective-permute-start | bytes 983048 | tf_op jit(solution)/shard_map/ppermute | solution.py:245
  25.8 0.8 %copy-start.1 = (f32[8,2048]{1,0:T(8,128)S(1)}, f32[8,2048]{1,0:T(8,128)}, u32[]{:S(2)}) copy-start(f32[8,2048]{1,0:T(8,128)} %stiff.5) | copy-start | bytes 196612
  26.6 0.8 %copy-start.2 = (s32[8,2048]{1,0:T(8,128)S(1)}, s32[8,2048]{1,0:T(8,128)}, u32[]{:S(2)}) copy-start(s32[8,2048]{1,0:T(8,128)} %slot.5) | copy-start | bytes 196612
  68.9 3.4 %collective-permute-start.6 = (f32[24,128]{1,0:T(8,128)S(1)}, f32[24,128]{1,0:T(8,128)S(1)}, u32[]{:S(2)}, u32[]{:S(2)}) collective-permute-start(f32[24,128]{1,0:T(8,128)S(1)} %get-tuple-element.34), channel_id=1, source_target_pairs={{0,6},{1,7},{2,0},{3,1},{4,2},{5,3},{6,4},{7,5},{8,14},{9,15},{10,... | collective-permute-start | bytes 36872 | tf_op jit(solution)/shard_map/ppermute | solution.py:245
  70.1 3.8 %collective-permute-start.7 = (f32[24,128]{1,0:T(8,128)S(1)}, f32[24,128]{1,0:T(8,128)S(1)}, u32[]{:S(2)}, u32[]{:S(2)}) collective-permute-start(f32[24,128]{1,0:T(8,128)S(1)} %get-tuple-element.33.kept), channel_id=1, source_target_pairs={{0,1},{1,2},{2,3},{3,4},{4,5},{5,6},{6,7},{7,0},{8,9},{9,10},{10,1... | collective-permute-start | bytes 36872 | tf_op jit(solution)/shard_map/ppermute | solution.py:245

commit v4 on v3

--- a/solution.py
+++ b/solution.py
@@ -15,24 +15,28 @@
 bf16 = jnp.bfloat16
 
 
-def stencil(shapes, stiff, lines, bend_out, left_out=None, total_out=None):
-    framed_rows, modes, cells = shapes.shape
+def stencil(panel, stiff, lines, bend_out, left_out=None, total_out=None):
+    body, edge = panel
+    rows, modes, cells = body.shape
     plain, cross, second = lines
     lane = lax.broadcasted_iota(jnp.int32, (modes, cells), 1)
-    group = 5
-
-    def across(n, carry):
+    group = 4
+
+    def across(r, w):
+        right = jnp.where(lane == cells - 1, 0.0, pltpu.roll(w, cells - 1, 1))
+        left = jnp.where(lane == 0, 0.0, pltpu.roll(w, 1, 1))
+        plain[r] = w
+        cross[r] = right - left
+        second[r] = (right - 2.0 * w) + left
+
+    def some_rows(n, carry):
         for k in range(group):
-            r = n * group + k
-            w = shapes[r].astype(f32)
-            right = jnp.where(lane == cells - 1, 0.0, pltpu.roll(w, cells - 1, 1))
-            left = jnp.where(lane == 0, 0.0, pltpu.roll(w, 1, 1))
-            plain[r] = w
-            cross[r] = right - left
-            second[r] = (right - 2.0 * w) + left
+            across(n * group + k + 1, body[n * group + k].astype(f32))
         return carry
 
-    lax.fori_loop(0, framed_rows // group, across, 0)
+    across(0, edge[0].astype(f32))
+    across(rows + 1, edge[1].astype(f32))
+    lax.fori_loop(0, rows // group, some_rows, 0)
 
     def along(r, total):
         along_x = (plain[r + 2] - 2.0 * plain[r + 1]) + plain[r]
@@ -54,7 +58,7 @@
             total = total + energy[:, k * 128 : (k + 1) * 128]
         return total
 
-    total = lax.fori_loop(0, framed_rows - 2, along, jnp.zeros((modes, 128), f32))
+    total = lax.fori_loop(0, rows, along, jnp.zeros((modes, 128), f32))
     if total_out is not None:
         total_out[...] = jnp.broadcast_to(jnp.sum(total, axis=1, keepdims=True), (modes, 128))
 
@@ -108,40 +112,52 @@
     return jnp.transpose(acc[0:half, :] + acc[half : 2 * half, :])
 
 
-def stage_own(shapes, stiff, slot, bend, left, total, sums, plain, cross, second, acc):
-    stencil(shapes, stiff, (plain, cross, second), bend, left, total)
+def stage_own(
+    body, edge, stiff_far_away, slot_far_away,
+    bend, left, total, sums, stiff, slot,
+    plain, cross, second, acc, arrived,
+):
+    stiff_copy = pltpu.make_async_copy(stiff_far_away, stiff, arrived.at[0])
+    slot_copy = pltpu.make_async_copy(slot_far_away, slot, arrived.at[1])
+    stiff_copy.start()
+    slot_copy.start()
+    stiff_copy.wait()
+    slot_copy.wait()
+    stencil((body, edge), stiff, (plain, cross, second), bend, left, total)
     sums[...] = pair_sums(slot, [(left, bend)], acc)
 
 
 def stage_near(
-    below, above, stiff, slot, bend, left,
+    below, below_edge, above, above_edge, stiff, slot, bend, left,
     bend_above, left_above, total_above, sums,
     bend_below, plain, cross, second, acc,
 ):
     lines = (plain, cross, second)
-    stencil(below, stiff, lines, bend_below)
-    stencil(above, stiff, lines, bend_above, left_above, total_above)
-    sums[...] = pair_sums(slot, [(left, bend_above), (left, bend_below)], acc)
+    stencil((below, below_edge), stiff, lines, bend_below)
+    stencil((above, above_edge), stiff, lines, bend_above, left_above, total_above)
+    blocks = [(left, bend_above), (left, bend_below), (left_above, bend_below)]
+    sums[...] = pair_sums(slot, blocks, acc)
 
 
 def stage_far(
-    below, above, stiff, slot, left, bend_above, left_above,
+    below, below_edge, above, above_edge, stiff, slot, left, bend_above, left_above,
     total, total_above, own_sums, near_sums,
     message,
     bend_far_below, left_far_below, bend_far_above, total_far_below, total_far_above,
     plain, cross, second, acc,
 ):
     lines = (plain, cross, second)
-    stencil(below, stiff, lines, bend_far_below, left_far_below, total_far_below)
-    stencil(above, stiff, lines, bend_far_above, None, total_far_above)
+    stencil((below, below_edge), stiff, lines, bend_far_below, left_far_below, total_far_below)
+    stencil((above, above_edge), stiff, lines, bend_far_above, None, total_far_above)
     blocks = [
-        (left, bend_far_above), (left, bend_far_below), (left_far_below, bend_above),
-        (left_far_below, bend_far_above), (left_above, bend_far_below),
+        (left_above, bend_far_below), (left, bend_far_above),
+        (left_far_below, bend_above), (left_far_below, bend_far_above),
     ]
     sums = pair_sums(slot, blocks, acc)
     owners, entries, _ = message.shape
-    message[:, :, 0:128] = near_sums[...].reshape(owners, entries, 128)
-    message[:, :, 128:512] = jnp.concatenate([sums, own_sums[...]], axis=1).reshape(owners, entries, 384)
+    early = jnp.concatenate([near_sums[...], own_sums[...]], axis=1)
+    message[:, :, 0:256] = early.reshape(owners, entries, 256)
+    message[:, :, 256:512] = sums.reshape(owners, entries, 256)
     lane = lax.broadcasted_iota(jnp.int32, total.shape, 1)
     places = jnp.zeros(total.shape, f32)
     for place, panel in enumerate([total, total_above, total_far_above, total_far_below]):
@@ -172,21 +188,23 @@
     chosen = jnp.where(chosen, 1.0, 0.0).astype(bf16)
     zoned = exact_dot(chosen, received[:, 0:body], True)
     totals = jnp.sum(received[:, body:].reshape(places // 8, 8, 128), axis=0)
-    mine[...] = zoned[:, 0:256]
-    to_far[0:zones, :] = zoned[:, 256:384]
-    to_far[zones:, :] = totals
-    to_next[0:zones, :] = zoned[:, 384:512]
-    to_next[zones:, :] = totals
+    mine[...] = zoned[:, 0:128]
+    to_far[0:8, :] = totals
+    to_far[8:, :] = zoned[:, 384:512]
+    to_next[0:8, :] = totals
+    to_next[8 : zones + 8, :] = zoned[:, 128:256]
+    to_next[zones + 8 :, :] = zoned[:, 256:384]
 
 
 def normalise(place, mine, kept, from_far, from_below, energy):
     zones = energy.shape[0]
-    z = slice(0, zones)
-    t = slice(zones, zones + 8)
+    t = slice(0, 8)
+    y = slice(8, zones + 8)
+    z = slice(zones + 8, 2 * zones + 8)
     sums = jnp.concatenate(
         [
-            kept[z, 64:128], mine[:, 0:64], mine[:, 128:192], from_far[z, 0:64],
-            from_far[z, 64:128], from_below[z, 0:64], mine[:, 192:256], mine[:, 64:128],
+            kept[y, 64:128], mine[:, 0:64], kept[z, 64:128], from_far[y, 0:64],
+            from_far[y, 64:128], from_below[z, 0:64], from_below[y, 0:64], mine[:, 64:128],
         ],
         axis=1,
     )
@@ -217,14 +235,12 @@
     return pltpu.VMEM(shape, dtype)
 
 
-def call(body, outs, scratch, *args, scalars=0):
-    specs = [pl.BlockSpec(memory_space=pltpu.SMEM)] * scalars + [
-        pl.BlockSpec(memory_space=pltpu.VMEM)
-    ] * (len(args) - scalars)
+def call(body, outs, scratch, *args, spaces=()):
+    where = list(spaces) + [pltpu.VMEM] * (len(args) - len(spaces))
     return pl.pallas_call(
         body,
         out_shape=[jax.ShapeDtypeStruct(s, d) for s, d in outs],
-        in_specs=specs,
+        in_specs=[pl.BlockSpec(memory_space=space) for space in where],
         out_specs=[pl.BlockSpec(memory_space=pltpu.VMEM)] * len(outs),
         scratch_shapes=scratch,
         compiler_params=pltpu.CompilerParams(vmem_limit_bytes=24 << 20),
@@ -248,38 +264,47 @@
     lists = lists.reshape(1, slots)
     head = lax.ppermute(mode_shapes[:, rows - 1], "tile", up)
     tail = lax.ppermute(mode_shapes[:, 0], "tile", down)
-    framed = jnp.concatenate([head[None], jnp.transpose(mode_shapes, (1, 0, 2)), tail[None]], axis=0)
-    framed, lists = lax.optimization_barrier((framed, lists))
-    below = turn(framed, 1)
-    above = turn(framed, -1)
+    inner = jnp.transpose(mode_shapes, (1, 0, 2))
+    below = turn(inner, 1)
+    above = turn(inner, -1)
+    edge, lists = lax.optimization_barrier((jnp.stack([head, tail]), lists))
+    below_edge = turn(edge, 1)
+    above_edge = turn(edge, -1)
     far_below = turn(below, 1)
     far_above = turn(above, -1)
+    far_below_edge = turn(below_edge, 1)
+    far_above_edge = turn(above_edge, -1)
 
     factor = ((3, rows, modes, cells), f32)
     total = ((modes, 128), f32)
     lines = [vmem((rows + 2, modes, cells))] * 3
     pairs = modes * modes
-    bend0, left0, total0, own_sums = call(
-        stage_own, [factor, factor, total, ((slots, pairs), f32)],
-        lines + [vmem((2 * pairs, slots))],
-        framed, stiffness, node_slot,
+    bend0, left0, total0, own_sums, stiff, slot = call(
+        stage_own,
+        [
+            factor, factor, total, ((slots, pairs), f32),
+            (stiffness.shape, stiffness.dtype), (node_slot.shape, node_slot.dtype),
+        ],
+        lines + [vmem((2 * pairs, slots)), pltpu.SemaphoreType.DMA((2,))],
+        inner, edge, stiffness, node_slot,
+        spaces=(pltpu.VMEM, pltpu.VMEM, pltpu.HBM, pltpu.HBM),
     )
     bend_above, left_above, total_above, near_sums = call(
-        stage_near, [factor, factor, total, ((slots, 2 * pairs), f32)],
-        [vmem(*factor)] + lines + [vmem((4 * pairs, slots))],
-        below, above, stiffness, node_slot, bend0, left0,
+        stage_near, [factor, factor, total, ((slots, 3 * pairs), f32)],
+        [vmem(*factor)] + lines + [vmem((6 * pairs, slots))],
+        below, below_edge, above, above_edge, stiff, slot, bend0, left0,
     )
     (message,) = call(
         stage_far, [((tiles, entries, 8 * pairs + 128), f32)],
-        [vmem(*factor)] * 3 + [vmem(*total)] * 2 + lines + [vmem((10 * pairs, slots))],
-        far_below, far_above, stiffness, node_slot, left0, bend_above, left_above,
+        [vmem(*factor)] * 3 + [vmem(*total)] * 2 + lines + [vmem((8 * pairs, slots))],
+        far_below, far_below_edge, far_above, far_above_edge, stiff, slot, left0, bend_above, left_above,
         total0, total_above, own_sums, near_sums,
     )
     message, lists = lax.optimization_barrier((message, lists))
     received = lax.all_to_all(message, "tile", 0, 0, tiled=True)
     mine, to_far, to_next = call(
         gather_zones,
-        [((owned, 4 * pairs), f32), ((owned + 8, 2 * pairs), f32), ((owned + 8, 2 * pairs), f32)], [],
+        [((owned, 128), f32), ((owned + 8, 128), f32), ((2 * owned + 8, 128), f32)], [],
         received.reshape(slots, 8 * pairs + 128), lists,
     )
     from_far = turn(to_far, -2)
@@ -287,7 +312,7 @@
     place = lax.axis_index("mode").astype(jnp.int32).reshape(1)
     (energy,) = call(
         normalise, [((owned, modes, panels * modes), f32)], [],
-        place, mine, to_next, from_far, from_below, scalars=1,
+        place, mine, to_next, from_far, from_below, spaces=(pltpu.SMEM,),
     )
     return energy
 

time: 75.5 us -> 77 us (1.020)
  the two profiles are of different devices: /device:TPU:1 before, /device:TPU:96 now
where the time goes in v4:
time: 77 us; the launch traced here: 76.8 us
  Pallas kernels  21.8 us (28%)
  starting transfers between devices  19.9 us (26%)
  blocking collectives  19.4 us (25%)
  waiting for transfers between devices  12 us (16%)
  local copies, waits for them, and re-layouts  3.6 us (5%)
    pallas_call x5, Pallas kernels, call(): pl.pallas_call(body, out_shape=[jax.ShapeDtypeStruct(s, d) for s, d in ou...  21.8 us
    all_to_all x1, blocking collectives, per_device(): received = lax.all_to_all(message, 'tile', 0, 0, tiled=True)  19.4 us
    ppermute x10, starting transfers between devices, turn(): lax.ppermute(x, 'mode', [(i, (i + by) % panels) for i in range(panels)])  17.1 us
    ppermute x10, waiting for transfers between devices, turn(): lax.ppermute(x, 'mode', [(i, (i + by) % panels) for i in range(panels)])  12 us
    unnamed x7, local copies, waits for them, and re-layouts  2.82 us
  transfers between devices with their start and end apart: 12, of which 3 were waited for; matrix products, arithmetic and copies ran while one was open for 1% of the time, Pallas kernels for 15%

profile of v4, /device:TPU:96, one launch (start us, length us, event | category | flops | bytes accessed | tf_op | source)
XLA Modules:
  0.0 76.8 jit_solution(10972471785956739909)
XLA Ops:
  0.0 1.1 %copy.13 = bf16[8,8,2048]{2,0,1:T(8,128)(2,1)S(1)} copy(bf16[8,8,2048]{2,1,0:T(8,128)(2,1)} %param.4) | data formatting | bytes 524288 | tf_op args[0]
  1.1 3.2 %collective-permute-start = (bf16[8,8,2048]{2,1,0:T(8,128)(2,1)S(1)}, bf16[8,8,2048]{2,1,0:T(8,128)(2,1)S(1)}, u32[]{:S(2)}, u32[]{:S(2)}) collective-permute-start(bf16[8,8,2048]{2,1,0:T(8,128)(2,1)S(1)} %bitcast.11), channel_id=1, source_target_pairs={{0,1},{1,2},{2,3},{3,4},{4,5},{5,6},{6,7},{7,0},{8,9},{9,10},{10,1... | collective-permute-start | bytes 786440 | tf_op jit(solution)/shard_map/ppermute | solution.py:261
  4.3 0.0 collective-permute-start.6
  4.4 1.5 %collective-permute-start.2 = (bf16[8,2048]{1,0:T(8,128)(2,1)S(1)}, bf16[8,2048]{1,0:T(8,128)(2,1)S(1)}, u32[]{:S(2)}, u32[]{:S(2)}) collective-permute-start(bf16[8,2048]{1,0:T(8,128)(2,1)S(1)} %get-tuple-element.39), channel_id=1, source_target_pairs={{0,8},{8,16},{16,24},{24,32},{32,40},{40,48},{48,56},{56,64},{64,7... | collective-permute-start | bytes 98312 | tf_op jit(solution)/shard_map/ppermute | solution.py:265
  5.8 1.3 %collective-permute-start.3 = (bf16[8,2048]{1,0:T(8,128)(2,1)S(1)}, bf16[8,2048]{1,0:T(8,128)(2,1)S(1)}, u32[]{:S(2)}, u32[]{:S(2)}) collective-permute-start(bf16[8,2048]{1,0:T(8,128)(2,1)S(1)} %get-tuple-element.40), channel_id=1, source_target_pairs={{8,0},{16,8},{24,16},{32,24},{40,32},{48,40},{56,48},{64,56},{72,6... | collective-permute-start | bytes 98312 | tf_op jit(solution)/shard_map/ppermute | solution.py:266
  7.1 0.7 dynamic-slice_reduce_fusion
  7.8 0.1 reshape.11.lists
  7.9 2.0 %collective-permute-done.below = bf16[8,8,2048]{2,1,0:T(8,128)(2,1)S(1)} collective-permute-done((bf16[8,8,2048]{2,1,0:T(8,128)(2,1)S(1)}, bf16[8,8,2048]{2,1,0:T(8,128)(2,1)S(1)}, u32[]{:S(2)}, u32[]{:S(2)}) %collective-permute-start) | collective-permute-done | bytes 262176 | tf_op jit(solution)/shard_map/ppermute | solution.py:261
  9.9 3.7 %collective-permute-start.1 = (bf16[8,8,2048]{2,1,0:T(8,128)(2,1)S(1)}, bf16[8,8,2048]{2,1,0:T(8,128)(2,1)S(1)}, u32[]{:S(2)}, u32[]{:S(2)}) collective-permute-start(bf16[8,8,2048]{2,1,0:T(8,128)(2,1)S(1)} %collective-permute-done.below), channel_id=1, source_target_pairs={{0,1},{1,2},{2,3},{3,4},{4,5},{5,6},{6,7},{7,0},{8,9},{9,10},{10,1... | collective-permute-start | bytes 786440 | tf_op jit(solution)/shard_map/ppermute | solution.py:261
  13.6 0.0 collective-permute-done.6.above
  13.6 0.0 collective-permute-start.7
  13.6 0.0 collective-permute-done.3
  13.6 3.3 %collective-permute-start.4 = (bf16[2,8,2048]{2,1,0:T(8,128)(2,1)S(1)}, bf16[2,8,2048]{2,1,0:T(8,128)(2,1)S(1)}, u32[]{:S(2)}, u32[]{:S(2)}) collective-permute-start(bf16[2,8,2048]{2,1,0:T(8,128)(2,1)S(1)} %pad_maximum_fusion.edge), channel_id=1, source_target_pairs={{0,1},{1,2},{2,3},{3,4},{4,5},{5,6},{6,7},{7,0},{8,9},{9,10},{10,1... | collective-permute-start | bytes 196616 | tf_op jit(solution)/shard_map/ppermute | solution.py:261
  16.9 0.0 collective-permute-start.8
  16.9 4.2 %collective-permute-done.4.below_edge = bf16[2,8,2048]{2,1,0:T(8,128)(2,1)S(1)} collective-permute-done((bf16[2,8,2048]{2,1,0:T(8,128)(2,1)S(1)}, bf16[2,8,2048]{2,1,0:T(8,128)(2,1)S(1)}, u32[]{:S(2)}, u32[]{:S(2)}) %collective-permute-start.4) | collective-permute-done | bytes 65568 | tf_op jit(solution)/shard_map/ppermute | solution.py:261
  21.1 3.7 %collective-permute-start.5 = (bf16[2,8,2048]{2,1,0:T(8,128)(2,1)S(1)}, bf16[2,8,2048]{2,1,0:T(8,128)(2,1)S(1)}, u32[]{:S(2)}, u32[]{:S(2)}) collective-permute-start(bf16[2,8,2048]{2,1,0:T(8,128)(2,1)S(1)} %collective-permute-done.4.below_edge), channel_id=1, source_target_pairs={{0,1},{1,2},{2,3},{3,4},{4,5},{5,6},{6,7},{7,0},{8,9},{9,10},{10,1... | collective-permute-start | bytes 196616 | tf_op jit(solution)/shard_map/ppermute | solution.py:261
  24.8 0.0 collective-permute-done.8.above_edge
  24.8 0.0 collective-permute-start.9
  24.8 0.8 %copy-done.1 = f32[8,2048]{1,0:T(8,128)S(1)} copy-done((f32[8,2048]{1,0:T(8,128)S(1)}, f32[8,2048]{1,0:T(8,128)}, u32[]{:S(2)}) %copy-start.1) | copy-done | bytes 65560
  25.7 0.8 %copy-done.2 = s32[8,2048]{1,0:T(8,128)S(1)} copy-done((s32[8,2048]{1,0:T(8,128)S(1)}, s32[8,2048]{1,0:T(8,128)}, u32[]{:S(2)}) %copy-start.2) | copy-done | bytes 65560
  26.5 4.7 %shard_map.46 = (f32[3,8,8,2048]{3,2,1,0:T(8,128)S(1)}, f32[3,8,8,2048]{3,2,1,0:T(8,128)S(1)}, f32[8,128]{1,0:T(8,128)S(1)}, f32[256,64]{1,0:T(8,128)S(1)}, f32[...) custom-call(bf16[8,8,2048]{2,1,0:T(8,128)(2,1)S(1)} %bitcast.13, bf16[2,8,2048]{2,1,0:T(8,128)(2,1)S(1)} %pad_maximum_fusion.edge, ...), custom_call_target="tpu_custom_call" | custom-call | tf_op jit(solution)/shard_map/pallas_call | solution.py:240
  31.2 7.0 %shard_map.47 = (f32[3,8,8,2048]{3,2,1,0:T(8,128)S(1)}, f32[3,8,8,2048]{3,2,1,0:T(8,128)S(1)}, f32[8,128]{1,0:T(8,128)S(1)}, f32[256,192]{1,0:T(8,128)S(1)}) custom-call(bf16[8,8,2048]{2,1,0:T(8,128)(2,1)S(1)} %collective-permute-done.below, bf16[2,8,2048]{2,1,0:T(8,128)(2,1)S(1)} %collective-permute-done.4.below_edge, ...), custom_call_target="tpu_custom_call" | custom-call | tf_op jit(solution)/shard_map/pallas_call | solution.py:240
  38.2 0.0 collective-permute-done.5.below_edge
  38.2 0.0 collective-permute-done.1.below
  38.3 0.0 collective-permute-done.7.above
  38.3 8.5 %shard_map.48 = f32[32,8,640]{2,1,0:T(8,128)S(1)} custom-call(bf16[8,8,2048]{2,1,0:T(8,128)(2,1)S(1)} %collective-permute-done.1.below, bf16[2,8,2048]{2,1,0:T(8,128)(2,1)S(1)} %collective-permute-done.5.below_edge, bf16[8,8,2048]{2,1,0:T(8,128)(2,1)S(1)} %collective-permute-done.7.above, bf16[2,8,2048]{2,1,0:T(8,128)(2,1)S(1)} %collective-permute-done.9.above_edge, ...), custom_call_target="tpu_custom_call" | custom-call | tf_op jit(solution)/shard_map/pallas_call | solution.py:240
  46.8 19.4 %all_to_all.5 = f32[32,8,640]{2,1,0:T(8,128)S(1)} all-to-all(f32[32,8,640]{2,1,0:T(8,128)S(1)} %shard_map.48), channel_id=1, replica_groups=mesh['tile'=32,'mode'=8] {'tile'}, dimensions={0} | all-to-all | bytes 1310720 | tf_op jit(solution)/shard_map/all_to_all | solution.py:304
  66.1 0.3 shard_map.49
  66.4 3.2 %collective-permute-start.11 = (f32[40,128]{1,0:T(8,128)S(1)}, f32[40,128]{1,0:T(8,128)S(1)}, u32[]{:S(2)}, u32[]{:S(2)}) collective-permute-start(f32[40,128]{1,0:T(8,128)S(1)} %get-tuple-element.37.kept), channel_id=1, source_target_pairs={{0,1},{1,2},{2,3},{3,4},{4,5},{5,6},{6,7},{7,0},{8,9},{9,10},{10,1... | collective-permute-start | bytes 61448 | tf_op jit(solution)/shard_map/ppermute | solution.py:261
  69.6 0.0 collective-permute-start.10
  69.6 5.8 %collective-permute-done.10.from_far = f32[24,128]{1,0:T(8,128)S(1)} collective-permute-done((f32[24,128]{1,0:T(8,128)S(1)}, f32[24,128]{1,0:T(8,128)S(1)}, u32[]{:S(2)}, u32[]{:S(2)}) %collective-permute-start.10) | collective-permute-done | bytes 12320 | tf_op jit(solution)/shard_map/ppermute | solution.py:261
  75.4 1.3 %shard_map.50 = f32[16,8,64]{2,1,0:T(8,128)} custom-call(s32[1]{0:T(128)} %bitcast.place, f32[16,128]{1,0:T(8,128)S(1)} %get-tuple-element.36.mine, f32[40,128]{1,0:T(8,128)S(1)} %get-tuple-element.37.kept, f32[24,128]{1,0:T(8,128)S(1)} %collective-permute-done.10.from_far, f32[40,128]{1,0:T(8,128)S(1)} %collective-permute-done.11.from_below), custom_call_target="tpu_custom_call" | custom-call | tf_op jit(solution)/shard_map/pallas_call | solution.py:240
  (9 shorter events, 0.0 us)
Async XLA Ops:
  0.0 7.1 %copy-start = (s32[32,32,8]{1,2,0:T(8,128)S(1)}, s32[32,32,8]{1,2,0:T(8,128)}, u32[]{:S(2)}) copy-start(s32[32,32,8]{1,2,0:T(8,128)} %param.7) | copy-start | bytes 98308
  1.1 8.8 %collective-permute-start = (bf16[8,8,2048]{2,1,0:T(8,128)(2,1)S(1)}, bf16[8,8,2048]{2,1,0:T(8,128)(2,1)S(1)}, u32[]{:S(2)}, u32[]{:S(2)}) collective-permute-start(bf16[8,8,2048]{2,1,0:T(8,128)(2,1)S(1)} %bitcast.11), channel_id=1, source_target_pairs={{0,1},{1,2},{2,3},{3,4},{4,5},{5,6},{6,7},{7,0},{8,9},{9,10},{10,1... | collective-permute-start | bytes 786440 | tf_op jit(solution)/shard_map/ppermute | solution.py:261
  4.3 9.3 %collective-permute-start.6 = (bf16[8,8,2048]{2,1,0:T(8,128)(2,1)S(1)}, bf16[8,8,2048]{2,1,0:T(8,128)(2,1)S(1)}, u32[]{:S(2)}, u32[]{:S(2)}) collective-permute-start(bf16[8,8,2048]{2,1,0:T(8,128)(2,1)S(1)} %bitcast.12), channel_id=1, source_target_pairs={{0,7},{1,0},{2,1},{3,2},{4,3},{5,4},{6,5},{7,6},{8,15},{9,8},{10,9... | collective-permute-start | bytes 786440 | tf_op jit(solution)/shard_map/ppermute | solution.py:261
  4.4 9.3 %collective-permute-start.2 = (bf16[8,2048]{1,0:T(8,128)(2,1)S(1)}, bf16[8,2048]{1,0:T(8,128)(2,1)S(1)}, u32[]{:S(2)}, u32[]{:S(2)}) collective-permute-start(bf16[8,2048]{1,0:T(8,128)(2,1)S(1)} %get-tuple-element.39), channel_id=1, source_target_pairs={{0,8},{8,16},{16,24},{24,32},{32,40},{40,48},{48,56},{56,64},{64,7... | collective-permute-start | bytes 98312 | tf_op jit(solution)/shard_map/ppermute | solution.py:265
  5.8 7.8 %collective-permute-start.3 = (bf16[8,2048]{1,0:T(8,128)(2,1)S(1)}, bf16[8,2048]{1,0:T(8,128)(2,1)S(1)}, u32[]{:S(2)}, u32[]{:S(2)}) collective-permute-start(bf16[8,2048]{1,0:T(8,128)(2,1)S(1)} %get-tuple-element.40), channel_id=1, source_target_pairs={{8,0},{16,8},{24,16},{32,24},{40,32},{48,40},{56,48},{64,56},{72,6... | collective-permute-start | bytes 98312 | tf_op jit(solution)/shard_map/ppermute | solution.py:266
  9.9 28.3 %collective-permute-start.1 = (bf16[8,8,2048]{2,1,0:T(8,128)(2,1)S(1)}, bf16[8,8,2048]{2,1,0:T(8,128)(2,1)S(1)}, u32[]{:S(2)}, u32[]{:S(2)}) collective-permute-start(bf16[8,8,2048]{2,1,0:T(8,128)(2,1)S(1)} %collective-permute-done.below), channel_id=1, source_target_pairs={{0,1},{1,2},{2,3},{3,4},{4,5},{5,6},{6,7},{7,0},{8,9},{9,10},{10,1... | collective-permute-start | bytes 786440 | tf_op jit(solution)/shard_map/ppermute | solution.py:261
  13.6 24.7 %collective-permute-start.7 = (bf16[8,8,2048]{2,1,0:T(8,128)(2,1)S(1)}, bf16[8,8,2048]{2,1,0:T(8,128)(2,1)S(1)}, u32[]{:S(2)}, u32[]{:S(2)}) collective-permute-start(bf16[8,8,2048]{2,1,0:T(8,128)(2,1)S(1)} %collective-permute-done.6.above), channel_id=1, source_target_pairs={{0,7},{1,0},{2,1},{3,2},{4,3},{5,4},{6,5},{7,6},{8,15},{9,8},{10,9... | collective-permute-start | bytes 786440 | tf_op jit(solution)/shard_map/ppermute | solution.py:261
  13.6 7.5 %collective-permute-start.4 = (bf16[2,8,2048]{2,1,0:T(8,128)(2,1)S(1)}, bf16[2,8,2048]{2,1,0:T(8,128)(2,1)S(1)}, u32[]{:S(2)}, u32[]{:S(2)}) collective-permute-start(bf16[2,8,2048]{2,1,0:T(8,128)(2,1)S(1)} %pad_maximum_fusion.edge), channel_id=1, source_target_pairs={{0,1},{1,2},{2,3},{3,4},{4,5},{5,6},{6,7},{7,0},{8,9},{9,10},{10,1... | collective-permute-start | bytes 196616 | tf_op jit(solution)/shard_map/ppermute | solution.py:261
  16.9 7.9 %collective-permute-start.8 = (bf16[2,8,2048]{2,1,0:T(8,128)(2,1)S(1)}, bf16[2,8,2048]{2,1,0:T(8,128)(2,1)S(1)}, u32[]{:S(2)}, u32[]{:S(2)}) collective-permute-start(bf16[2,8,2048]{2,1,0:T(8,128)(2,1)S(1)} %pad_maximum_fusion.edge), channel_id=1, source_target_pairs={{0,7},{1,0},{2,1},{3,2},{4,3},{5,4},{6,5},{7,6},{8,15},{9,8},{10,9... | collective-permute-start | bytes 196616 | tf_op jit(solution)/shard_map/ppermute | solution.py:261
  21.1 17.1 %collective-permute-start.5 = (bf16[2,8,2048]{2,1,0:T(8,128)(2,1)S(1)}, bf16[2,8,2048]{2,1,0:T(8,128)(2,1)S(1)}, u32[]{:S(2)}, u32[]{:S(2)}) collective-permute-start(bf16[2,8,2048]{2,1,0:T(8,128)(2,1)S(1)} %collective-permute-done.4.below_edge), channel_id=1, source_target_pairs={{0,1},{1,2},{2,3},{3,4},{4,5},{5,6},{6,7},{7,0},{8,9},{9,10},{10,1... | collective-permute-start | bytes 196616 | tf_op jit(solution)/shard_map/ppermute | solution.py:261
  24.8 13.4 %collective-permute-start.9 = (bf16[2,8,2048]{2,1,0:T(8,128)(2,1)S(1)}, bf16[2,8,2048]{2,1,0:T(8,128)(2,1)S(1)}, u32[]{:S(2)}, u32[]{:S(2)}) collective-permute-start(bf16[2,8,2048]{2,1,0:T(8,128)(2,1)S(1)} %collective-permute-done.8.above_edge), channel_id=1, source_target_pairs={{0,7},{1,0},{2,1},{3,2},{4,3},{5,4},{6,5},{7,6},{8,15},{9,8},{10,9... | collective-permute-start | bytes 196616 | tf_op jit(solution)/shard_map/ppermute | solution.py:261
  24.8 0.8 %copy-start.1 = (f32[8,2048]{1,0:T(8,128)S(1)}, f32[8,2048]{1,0:T(8,128)}, u32[]{:S(2)}) copy-start(f32[8,2048]{1,0:T(8,128)} %stiff_far_away.1) | copy-start | bytes 196612
  25.7 0.8 %copy-start.2 = (s32[8,2048]{1,0:T(8,128)S(1)}, s32[8,2048]{1,0:T(8,128)}, u32[]{:S(2)}) copy-start(s32[8,2048]{1,0:T(8,128)} %slot_far_away.1) | copy-start | bytes 196612
  66.4 9.0 %collective-permute-start.11 = (f32[40,128]{1,0:T(8,128)S(1)}, f32[40,128]{1,0:T(8,128)S(1)}, u32[]{:S(2)}, u32[]{:S(2)}) collective-permute-start(f32[40,128]{1,0:T(8,128)S(1)} %get-tuple-element.37.kept), channel_id=1, source_target_pairs={{0,1},{1,2},{2,3},{3,4},{4,5},{5,6},{6,7},{7,0},{8,9},{9,10},{10,1... | collective-permute-start | bytes 61448 | tf_op jit(solution)/shard_map/ppermute | solution.py:261
  69.6 5.8 %collective-permute-start.10 = (f32[24,128]{1,0:T(8,128)S(1)}, f32[24,128]{1,0:T(8,128)S(1)}, u32[]{:S(2)}, u32[]{:S(2)}) collective-permute-start(f32[24,128]{1,0:T(8,128)S(1)} %get-tuple-element.38), channel_id=1, source_target_pairs={{0,6},{1,7},{2,0},{3,1},{4,2},{5,3},{6,4},{7,5},{8,14},{9,15},{10,... | collective-permute-start | bytes 36872 | tf_op jit(solution)/shard_map/ppermute | solution.py:261

commit v5 on v3

--- a/solution.py
+++ b/solution.py
@@ -15,7 +15,7 @@
 bf16 = jnp.bfloat16
 
 
-def stencil(shapes, stiff, lines, bend_out, left_out=None, total_out=None):
+def stencil(shapes, plate, lines, bend_out, left_out=None, total_out=None):
     framed_rows, modes, cells = shapes.shape
     plain, cross, second = lines
     lane = lax.broadcasted_iota(jnp.int32, (modes, cells), 1)
@@ -42,7 +42,7 @@
             bend_out[c, r] = b
         if left_out is None and total_out is None:
             return total
-        s = jnp.broadcast_to(stiff[pl.ds(r, 1), :], (modes, cells))
+        s = jnp.broadcast_to(plate[0, pl.ds(r, 1), :], (modes, cells))
         weighted = [s * (bx + POISSON * by), s * (by + POISSON * bx), s * (SHEAR * bt)]
         if left_out is not None:
             for c in range(3):
@@ -59,8 +59,8 @@
         total_out[...] = jnp.broadcast_to(jnp.sum(total, axis=1, keepdims=True), (modes, 128))
 
 
-def pair_sums(slot, blocks, acc):
-    rows, cells = slot.shape
+def pair_sums(plate, blocks, acc):
+    _, rows, cells = plate.shape
     width, slots = acc.shape
     half = len(blocks) * blocks[0][0].shape[2] ** 2
     spare = [jnp.zeros((width - 2 * half, cells), bf16)] if width > 2 * half else []
@@ -71,7 +71,7 @@
         members, high, low = [], [], []
         for first in range(0, cells, CHUNK):
             cut = slice(first, first + CHUNK)
-            here = slot[pl.ds(r, 1), cut].astype(f32).astype(bf16)
+            here = plate[1, pl.ds(r, 1), cut].astype(bf16)
             members.append(
                 jnp.where(
                     jnp.broadcast_to(here, (slots, CHUNK)) == slot_id,
@@ -108,40 +108,42 @@
     return jnp.transpose(acc[0:half, :] + acc[half : 2 * half, :])
 
 
-def stage_own(shapes, stiff, slot, bend, left, total, sums, plain, cross, second, acc):
-    stencil(shapes, stiff, (plain, cross, second), bend, left, total)
-    sums[...] = pair_sums(slot, [(left, bend)], acc)
+def stage_own(shapes, plate, bend, left, total, sums, plain, cross, second, acc):
+    stencil(shapes, plate, (plain, cross, second), bend, left, total)
+    sums[...] = pair_sums(plate, [(left, bend)], acc)
 
 
 def stage_near(
-    below, above, stiff, slot, bend, left,
+    below, above, plate, bend, left,
     bend_above, left_above, total_above, sums,
     bend_below, plain, cross, second, acc,
 ):
     lines = (plain, cross, second)
-    stencil(below, stiff, lines, bend_below)
-    stencil(above, stiff, lines, bend_above, left_above, total_above)
-    sums[...] = pair_sums(slot, [(left, bend_above), (left, bend_below)], acc)
+    stencil(below, plate, lines, bend_below)
+    stencil(above, plate, lines, bend_above, left_above, total_above)
+    blocks = [(left, bend_above), (left, bend_below), (left_above, bend_below)]
+    sums[...] = pair_sums(plate, blocks, acc)
 
 
 def stage_far(
-    below, above, stiff, slot, left, bend_above, left_above,
+    below, above, plate, left, bend_above, left_above,
     total, total_above, own_sums, near_sums,
     message,
     bend_far_below, left_far_below, bend_far_above, total_far_below, total_far_above,
     plain, cross, second, acc,
 ):
     lines = (plain, cross, second)
-    stencil(below, stiff, lines, bend_far_below, left_far_below, total_far_below)
-    stencil(above, stiff, lines, bend_far_above, None, total_far_above)
+    stencil(below, plate, lines, bend_far_below, left_far_below, total_far_below)
+    stencil(above, plate, lines, bend_far_above, None, total_far_above)
     blocks = [
-        (left, bend_far_above), (left, bend_far_below), (left_far_below, bend_above),
-        (left_far_below, bend_far_above), (left_above, bend_far_below),
+        (left_above, bend_far_below), (left, bend_far_above),
+        (left_far_below, bend_above), (left_far_below, bend_far_above),
     ]
-    sums = pair_sums(slot, blocks, acc)
+    sums = pair_sums(plate, blocks, acc)
     owners, entries, _ = message.shape
-    message[:, :, 0:128] = near_sums[...].reshape(owners, entries, 128)
-    message[:, :, 128:512] = jnp.concatenate([sums, own_sums[...]], axis=1).reshape(owners, entries, 384)
+    early = jnp.concatenate([near_sums[...], own_sums[...]], axis=1)
+    message[:, :, 0:256] = early.reshape(owners, entries, 256)
+    message[:, :, 256:512] = sums.reshape(owners, entries, 256)
     lane = lax.broadcasted_iota(jnp.int32, total.shape, 1)
     places = jnp.zeros(total.shape, f32)
     for place, panel in enumerate([total, total_above, total_far_above, total_far_below]):
@@ -172,21 +174,23 @@
     chosen = jnp.where(chosen, 1.0, 0.0).astype(bf16)
     zoned = exact_dot(chosen, received[:, 0:body], True)
     totals = jnp.sum(received[:, body:].reshape(places // 8, 8, 128), axis=0)
-    mine[...] = zoned[:, 0:256]
-    to_far[0:zones, :] = zoned[:, 256:384]
-    to_far[zones:, :] = totals
-    to_next[0:zones, :] = zoned[:, 384:512]
-    to_next[zones:, :] = totals
+    mine[...] = zoned[:, 0:128]
+    to_far[0:8, :] = totals
+    to_far[8:, :] = zoned[:, 384:512]
+    to_next[0:8, :] = totals
+    to_next[8 : zones + 8, :] = zoned[:, 128:256]
+    to_next[zones + 8 :, :] = zoned[:, 256:384]
 
 
 def normalise(place, mine, kept, from_far, from_below, energy):
     zones = energy.shape[0]
-    z = slice(0, zones)
-    t = slice(zones, zones + 8)
+    t = slice(0, 8)
+    y = slice(8, zones + 8)
+    z = slice(zones + 8, 2 * zones + 8)
     sums = jnp.concatenate(
         [
-            kept[z, 64:128], mine[:, 0:64], mine[:, 128:192], from_far[z, 0:64],
-            from_far[z, 64:128], from_below[z, 0:64], mine[:, 192:256], mine[:, 64:128],
+            kept[y, 64:128], mine[:, 0:64], kept[z, 64:128], from_far[y, 0:64],
+            from_far[y, 64:128], from_below[z, 0:64], from_below[y, 0:64], mine[:, 64:128],
         ],
         axis=1,
     )
@@ -203,11 +207,12 @@
         jnp.where((lane // 8) % 8 == sub, jnp.broadcast_to(own[:, 0:1], (8, 512)), 0.0), axis=0, keepdims=True
     )
     scaled = ZONES * (0.5 * sums) / jnp.sqrt((0.5 * total_i) * (0.5 * total_j))
-    r = lax.broadcasted_iota(jnp.int32, (512, 512), 0)
-    c = lax.broadcasted_iota(jnp.int32, (512, 512), 1)
-    panel = (r // 64 + place[0]) % 8
-    target = ((r // 8) % 8) * 64 + panel * 8 + r % 8
-    order = jnp.where(c == target, 1.0, 0.0).astype(bf16)
+    r = lax.broadcasted_iota(jnp.int32, (512, 128), 0)
+    c = lax.broadcasted_iota(jnp.int32, (512, 128), 1)
+    target = ((r & 56) << 3) + ((((r >> 6) + place[0]) & 7) << 3) + (r & 7) - c
+    order = jnp.concatenate(
+        [jnp.where(target == first, 1.0, 0.0).astype(bf16) for first in range(0, 512, 128)], axis=1
+    )
     ordered = exact_dot(scaled, order, False)
     for i in range(8):
         energy[:, i, :] = ordered[:, i * 64 : (i + 1) * 64]
@@ -217,14 +222,12 @@
     return pltpu.VMEM(shape, dtype)
 
 
-def call(body, outs, scratch, *args, scalars=0):
-    specs = [pl.BlockSpec(memory_space=pltpu.SMEM)] * scalars + [
-        pl.BlockSpec(memory_space=pltpu.VMEM)
-    ] * (len(args) - scalars)
+def call(body, outs, scratch, *args, spaces=()):
+    where = list(spaces) + [pltpu.VMEM] * (len(args) - len(spaces))
     return pl.pallas_call(
         body,
         out_shape=[jax.ShapeDtypeStruct(s, d) for s, d in outs],
-        in_specs=specs,
+        in_specs=[pl.BlockSpec(memory_space=space) for space in where],
         out_specs=[pl.BlockSpec(memory_space=pltpu.VMEM)] * len(outs),
         scratch_shapes=scratch,
         compiler_params=pltpu.CompilerParams(vmem_limit_bytes=24 << 20),
@@ -246,10 +249,11 @@
 
     lists = lax.dynamic_index_in_dim(slot_zone, lax.axis_index("tile"), 1, keepdims=False)
     lists = lists.reshape(1, slots)
+    plate = jnp.stack([stiffness, node_slot.astype(f32)])
     head = lax.ppermute(mode_shapes[:, rows - 1], "tile", up)
     tail = lax.ppermute(mode_shapes[:, 0], "tile", down)
     framed = jnp.concatenate([head[None], jnp.transpose(mode_shapes, (1, 0, 2)), tail[None]], axis=0)
-    framed, lists = lax.optimization_barrier((framed, lists))
+    framed, lists, plate = lax.optimization_barrier((framed, lists, plate))
     below = turn(framed, 1)
     above = turn(framed, -1)
     far_below = turn(below, 1)
@@ -262,24 +266,24 @@
     bend0, left0, total0, own_sums = call(
         stage_own, [factor, factor, total, ((slots, pairs), f32)],
         lines + [vmem((2 * pairs, slots))],
-        framed, stiffness, node_slot,
+        framed, plate,
     )
     bend_above, left_above, total_above, near_sums = call(
-        stage_near, [factor, factor, total, ((slots, 2 * pairs), f32)],
-        [vmem(*factor)] + lines + [vmem((4 * pairs, slots))],
-        below, above, stiffness, node_slot, bend0, left0,
+        stage_near, [factor, factor, total, ((slots, 3 * pairs), f32)],
+        [vmem(*factor)] + lines + [vmem((6 * pairs, slots))],
+        below, above, plate, bend0, left0,
     )
     (message,) = call(
         stage_far, [((tiles, entries, 8 * pairs + 128), f32)],
-        [vmem(*factor)] * 3 + [vmem(*total)] * 2 + lines + [vmem((10 * pairs, slots))],
-        far_below, far_above, stiffness, node_slot, left0, bend_above, left_above,
+        [vmem(*factor)] * 3 + [vmem(*total)] * 2 + lines + [vmem((8 * pairs, slots))],
+        far_below, far_above, plate, left0, bend_above, left_above,
         total0, total_above, own_sums, near_sums,
     )
     message, lists = lax.optimization_barrier((message, lists))
     received = lax.all_to_all(message, "tile", 0, 0, tiled=True)
     mine, to_far, to_next = call(
         gather_zones,
-        [((owned, 4 * pairs), f32), ((owned + 8, 2 * pairs), f32), ((owned + 8, 2 * pairs), f32)], [],
+        [((owned, 128), f32), ((owned + 8, 128), f32), ((2 * owned + 8, 128), f32)], [],
         received.reshape(slots, 8 * pairs + 128), lists,
     )
     from_far = turn(to_far, -2)
@@ -287,7 +291,7 @@
     place = lax.axis_index("mode").astype(jnp.int32).reshape(1)
     (energy,) = call(
         normalise, [((owned, modes, panels * modes), f32)], [],
-        place, mine, to_next, from_far, from_below, scalars=1,
+        place, mine, to_next, from_far, from_below, spaces=(pltpu.SMEM,),
     )
     return energy
 

time: 75.5 us -> 74 us (0.980)
  the two profiles are of different devices: /device:TPU:1 before, /device:TPU:96 now
where the time goes in v5:
time: 74 us; the launch traced here: 73.8 us
  blocking collectives  22.2 us (30%)
  Pallas kernels  21.2 us (29%)
  waiting for transfers between devices  13.4 us (18%)
  starting transfers between devices  13.2 us (18%)
  local copies, waits for them, and re-layouts  1.92 us (3%)
  other arithmetic  1.75 us (2%)
    all_to_all x1, blocking collectives, per_device(): received = lax.all_to_all(message, 'tile', 0, 0, tiled=True)  22.2 us
    pallas_call x5, Pallas kernels, call(): pl.pallas_call(body, out_shape=[jax.ShapeDtypeStruct(s, d) for s, d in ou...  21.2 us
    ppermute x6, waiting for transfers between devices, turn(): lax.ppermute(x, 'mode', [(i, (i + by) % panels) for i in range(panels)])  12.7 us
    ppermute x6, starting transfers between devices, turn(): lax.ppermute(x, 'mode', [(i, (i + by) % panels) for i in range(panels)])  10.1 us
    ppermute x1, starting transfers between devices, per_device(): head = lax.ppermute(mode_shapes[:, rows - 1], 'tile', up)  1.74 us
    another operation x2, other arithmetic, per_device(): plate = jnp.stack([stiffness, node_slot.astype(f32)])  1.7 us
  transfers between devices with their start and end apart: 8, of which 5 were waited for; matrix products, arithmetic and copies ran while one was open for 3% of the time, Pallas kernels for 15%

profile of v5, /device:TPU:96, one launch (start us, length us, event | category | flops | bytes accessed | tf_op | source)
XLA Modules:
  0.0 73.8 jit_solution(5465098637204621056)
XLA Ops:
  0.0 0.0 copy-start
  0.0 1.1 %copy.13 = bf16[8,8,2048]{2,0,1:T(8,128)(2,1)S(1)} copy(bf16[8,8,2048]{2,1,0:T(8,128)(2,1)} %param.4) | data formatting | bytes 524288 | tf_op args[0]
  1.2 1.7 %collective-permute-start = (bf16[8,2048]{1,0:T(8,128)(2,1)S(1)}, bf16[8,2048]{1,0:T(8,128)(2,1)S(1)}, u32[]{:S(2)}, u32[]{:S(2)}) collective-permute-start(bf16[8,2048]{1,0:T(8,128)(2,1)S(1)} %get-tuple-element.37), channel_id=1, source_target_pairs={{0,8},{8,16},{16,24},{24,32},{32,40},{40,48},{48,56},{56,64},{64,7... | collective-permute-start | bytes 98312 | tf_op jit(solution)/shard_map/ppermute | solution.py:253
  2.9 1.3 %collective-permute-start.1 = (bf16[8,2048]{1,0:T(8,128)(2,1)S(1)}, bf16[8,2048]{1,0:T(8,128)(2,1)S(1)}, u32[]{:S(2)}, u32[]{:S(2)}) collective-permute-start(bf16[8,2048]{1,0:T(8,128)(2,1)S(1)} %get-tuple-element.38), channel_id=1, source_target_pairs={{8,0},{16,8},{24,16},{32,24},{40,32},{48,40},{56,48},{64,56},{72,6... | collective-permute-start | bytes 98312 | tf_op jit(solution)/shard_map/ppermute | solution.py:254
  4.2 0.8 %convert_bitcast_fusion = f32[1,8,2048]{2,1,0:T(8,128)S(1)} fusion(s32[8,2048]{1,0:T(8,128)} %param.6), kind=kLoop, calls=%fused_computation.3 | loop fusion | flops 16384 | bytes 131072 | tf_op jit(solution)/shard_map/stack | solution.py:252
  5.1 0.9 %pad_maximum_fusion.1.plate = f32[2,8,2048]{2,1,0:T(8,128)S(1)} fusion(f32[1,8,2048]{2,1,0:T(8,128)S(1)} %convert_bitcast_fusion, f32[1,8,2048]{2,1,0:T(8,128)} %bitcast.16), kind=kLoop, calls=%fused_computation.1 | loop fusion | flops 32768 | bytes 262144 | tf_op jit(solution)/shard_map/stack | solution.py:252
  5.9 0.0 copy-done
  5.9 0.7 dynamic-slice_reduce_fusion
  6.6 0.1 reshape.11.lists
  6.7 0.0 collective-permute-done
  6.7 0.7 collective-permute-done.1
  7.4 3.2 %collective-permute-start.2 = (bf16[10,8,2048]{2,1,0:T(8,128)(2,1)S(1)}, bf16[10,8,2048]{2,1,0:T(8,128)(2,1)S(1)}, u32[]{:S(2)}, u32[]{:S(2)}) collective-permute-start(bf16[10,8,2048]{2,1,0:T(8,128)(2,1)S(1)} %pad_maximum_fusion.shapes), channel_id=1, source_target_pairs={{0,1},{1,2},{2,3},{3,4},{4,5},{5,6},{6,7},{7,0},{8,9},{9,10},{10,1... | collective-permute-start | bytes 983048 | tf_op jit(solution)/shard_map/ppermute | solution.py:248
  10.6 0.0 collective-permute-start.4
  10.6 6.4 %collective-permute-done.2.below = bf16[10,8,2048]{2,1,0:T(8,128)(2,1)S(1)} collective-permute-done((bf16[10,8,2048]{2,1,0:T(8,128)(2,1)S(1)}, bf16[10,8,2048]{2,1,0:T(8,128)(2,1)S(1)}, u32[]{:S(2)}, u32[]{:S(2)}) %collective-permute-start.2) | collective-permute-done | bytes 327712 | tf_op jit(solution)/shard_map/ppermute | solution.py:248
  17.1 3.7 %collective-permute-start.3 = (bf16[10,8,2048]{2,1,0:T(8,128)(2,1)S(1)}, bf16[10,8,2048]{2,1,0:T(8,128)(2,1)S(1)}, u32[]{:S(2)}, u32[]{:S(2)}) collective-permute-start(bf16[10,8,2048]{2,1,0:T(8,128)(2,1)S(1)} %collective-permute-done.2.below), channel_id=1, source_target_pairs={{0,1},{1,2},{2,3},{3,4},{4,5},{5,6},{6,7},{7,0},{8,9},{9,10},{10,1... | collective-permute-start | bytes 983048 | tf_op jit(solution)/shard_map/ppermute | solution.py:248
  20.8 0.3 collective-permute-done.4.above
  21.0 0.0 collective-permute-start.5
  21.0 4.5 %shard_map.46 = (f32[3,8,8,2048]{3,2,1,0:T(8,128)S(1)}, f32[3,8,8,2048]{3,2,1,0:T(8,128)S(1)}, f32[8,128]{1,0:T(8,128)S(1)}, f32[256,64]{1,0:T(8,128)S(1)}) custom-call(bf16[10,8,2048]{2,1,0:T(8,128)(2,1)S(1)} %pad_maximum_fusion.shapes, f32[2,8,2048]{2,1,0:T(8,128)S(1)} %pad_maximum_fusion.1.plate), custom_call_target="tpu_custom_call" | custom-call | tf_op jit(solution)/shard_map/pallas_call | solution.py:227
  25.5 6.9 %shard_map.47 = (f32[3,8,8,2048]{3,2,1,0:T(8,128)S(1)}, f32[3,8,8,2048]{3,2,1,0:T(8,128)S(1)}, f32[8,128]{1,0:T(8,128)S(1)}, f32[256,192]{1,0:T(8,128)S(1)}) custom-call(bf16[10,8,2048]{2,1,0:T(8,128)(2,1)S(1)} %collective-permute-done.2.below, bf16[10,8,2048]{2,1,0:T(8,128)(2,1)S(1)} %collective-permute-done.4.above, ...), custom_call_target="tpu_custom_call" | custom-call | tf_op jit(solution)/shard_map/pallas_call | solution.py:227
  32.4 0.0 collective-permute-done.3.below
  32.4 0.2 collective-permute-done.5.above
  32.6 8.4 %shard_map.48 = f32[32,8,640]{2,1,0:T(8,128)S(1)} custom-call(bf16[10,8,2048]{2,1,0:T(8,128)(2,1)S(1)} %collective-permute-done.3.below, bf16[10,8,2048]{2,1,0:T(8,128)(2,1)S(1)} %collective-permute-done.5.above, f32[2,8,2048]{2,1,0:T(8,128)S(1)} %pad_maximum_fusion.1.plate, f32[3,8,8,2048]{3,2,1,0:T(8,128)S(1)} %get-tuple-element.23.left, ...), custom_call_target="tpu_custom_call" | custom-call | tf_op jit(solution)/shard_map/pallas_call | solution.py:227
  41.0 22.2 %all_to_all.5 = f32[32,8,640]{2,1,0:T(8,128)S(1)} all-to-all(f32[32,8,640]{2,1,0:T(8,128)S(1)} %shard_map.48), channel_id=1, replica_groups=mesh['tile'=32,'mode'=8] {'tile'}, dimensions={0} | all-to-all | bytes 1310720 | tf_op jit(solution)/shard_map/all_to_all | solution.py:283
  63.2 0.3 shard_map.49
  63.5 3.2 %collective-permute-start.7 = (f32[40,128]{1,0:T(8,128)S(1)}, f32[40,128]{1,0:T(8,128)S(1)}, u32[]{:S(2)}, u32[]{:S(2)}) collective-permute-start(f32[40,128]{1,0:T(8,128)S(1)} %get-tuple-element.35.kept), channel_id=1, source_target_pairs={{0,1},{1,2},{2,3},{3,4},{4,5},{5,6},{6,7},{7,0},{8,9},{9,10},{10,1... | collective-permute-start | bytes 61448 | tf_op jit(solution)/shard_map/ppermute | solution.py:248
  66.7 0.0 collective-permute-start.6
  66.7 5.8 %collective-permute-done.6.from_far = f32[24,128]{1,0:T(8,128)S(1)} collective-permute-done((f32[24,128]{1,0:T(8,128)S(1)}, f32[24,128]{1,0:T(8,128)S(1)}, u32[]{:S(2)}, u32[]{:S(2)}) %collective-permute-start.6) | collective-permute-done | bytes 12320 | tf_op jit(solution)/shard_map/ppermute | solution.py:248
  72.5 0.0 collective-permute-done.7.from_below
  72.5 1.2 %shard_map.50 = f32[16,8,64]{2,1,0:T(8,128)} custom-call(s32[1]{0:T(128)} %bitcast.place, f32[16,128]{1,0:T(8,128)S(1)} %get-tuple-element.34.mine, f32[40,128]{1,0:T(8,128)S(1)} %get-tuple-element.35.kept, f32[24,128]{1,0:T(8,128)S(1)} %collective-permute-done.6.from_far, f32[40,128]{1,0:T(8,128)S(1)} %collective-permute-done.7.from_below), custom_call_target="tpu_custom_call" | custom-call | tf_op jit(solution)/shard_map/pallas_call | solution.py:227
  (2 shorter events, 0.1 us)
Async XLA Ops:
  0.0 5.9 %copy-start = (s32[32,32,8]{1,2,0:T(8,128)S(1)}, s32[32,32,8]{1,2,0:T(8,128)}, u32[]{:S(2)}) copy-start(s32[32,32,8]{1,2,0:T(8,128)} %param.7) | copy-start | bytes 98308
  1.2 5.5 %collective-permute-start = (bf16[8,2048]{1,0:T(8,128)(2,1)S(1)}, bf16[8,2048]{1,0:T(8,128)(2,1)S(1)}, u32[]{:S(2)}, u32[]{:S(2)}) collective-permute-start(bf16[8,2048]{1,0:T(8,128)(2,1)S(1)} %get-tuple-element.37), channel_id=1, source_target_pairs={{0,8},{8,16},{16,24},{24,32},{32,40},{40,48},{48,56},{56,64},{64,7... | collective-permute-start | bytes 98312 | tf_op jit(solution)/shard_map/ppermute | solution.py:253
  2.9 4.5 %collective-permute-start.1 = (bf16[8,2048]{1,0:T(8,128)(2,1)S(1)}, bf16[8,2048]{1,0:T(8,128)(2,1)S(1)}, u32[]{:S(2)}, u32[]{:S(2)}) collective-permute-start(bf16[8,2048]{1,0:T(8,128)(2,1)S(1)} %get-tuple-element.38), channel_id=1, source_target_pairs={{8,0},{16,8},{24,16},{32,24},{40,32},{48,40},{56,48},{64,56},{72,6... | collective-permute-start | bytes 98312 | tf_op jit(solution)/shard_map/ppermute | solution.py:254
  7.4 9.6 %collective-permute-start.2 = (bf16[10,8,2048]{2,1,0:T(8,128)(2,1)S(1)}, bf16[10,8,2048]{2,1,0:T(8,128)(2,1)S(1)}, u32[]{:S(2)}, u32[]{:S(2)}) collective-permute-start(bf16[10,8,2048]{2,1,0:T(8,128)(2,1)S(1)} %pad_maximum_fusion.shapes), channel_id=1, source_target_pairs={{0,1},{1,2},{2,3},{3,4},{4,5},{5,6},{6,7},{7,0},{8,9},{9,10},{10,1... | collective-permute-start | bytes 983048 | tf_op jit(solution)/shard_map/ppermute | solution.py:248
  10.6 10.4 %collective-permute-start.4 = (bf16[10,8,2048]{2,1,0:T(8,128)(2,1)S(1)}, bf16[10,8,2048]{2,1,0:T(8,128)(2,1)S(1)}, u32[]{:S(2)}, u32[]{:S(2)}) collective-permute-start(bf16[10,8,2048]{2,1,0:T(8,128)(2,1)S(1)} %pad_maximum_fusion.shapes), channel_id=1, source_target_pairs={{0,7},{1,0},{2,1},{3,2},{4,3},{5,4},{6,5},{7,6},{8,15},{9,8},{10,9... | collective-permute-start | bytes 983048 | tf_op jit(solution)/shard_map/ppermute | solution.py:248
  17.1 15.3 %collective-permute-start.3 = (bf16[10,8,2048]{2,1,0:T(8,128)(2,1)S(1)}, bf16[10,8,2048]{2,1,0:T(8,128)(2,1)S(1)}, u32[]{:S(2)}, u32[]{:S(2)}) collective-permute-start(bf16[10,8,2048]{2,1,0:T(8,128)(2,1)S(1)} %collective-permute-done.2.below), channel_id=1, source_target_pairs={{0,1},{1,2},{2,3},{3,4},{4,5},{5,6},{6,7},{7,0},{8,9},{9,10},{10,1... | collective-permute-start | bytes 983048 | tf_op jit(solution)/shard_map/ppermute | solution.py:248
  21.0 11.6 %collective-permute-start.5 = (bf16[10,8,2048]{2,1,0:T(8,128)(2,1)S(1)}, bf16[10,8,2048]{2,1,0:T(8,128)(2,1)S(1)}, u32[]{:S(2)}, u32[]{:S(2)}) collective-permute-start(bf16[10,8,2048]{2,1,0:T(8,128)(2,1)S(1)} %collective-permute-done.4.above), channel_id=1, source_target_pairs={{0,7},{1,0},{2,1},{3,2},{4,3},{5,4},{6,5},{7,6},{8,15},{9,8},{10,9... | collective-permute-start | bytes 983048 | tf_op jit(solution)/shard_map/ppermute | solution.py:248
  63.5 9.0 %collective-permute-start.7 = (f32[40,128]{1,0:T(8,128)S(1)}, f32[40,128]{1,0:T(8,128)S(1)}, u32[]{:S(2)}, u32[]{:S(2)}) collective-permute-start(f32[40,128]{1,0:T(8,128)S(1)} %get-tuple-element.35.kept), channel_id=1, source_target_pairs={{0,1},{1,2},{2,3},{3,4},{4,5},{5,6},{6,7},{7,0},{8,9},{9,10},{10,1... | collective-permute-start | bytes 61448 | tf_op jit(solution)/shard_map/ppermute | solution.py:248
  66.7 5.8 %collective-permute-start.6 = (f32[24,128]{1,0:T(8,128)S(1)}, f32[24,128]{1,0:T(8,128)S(1)}, u32[]{:S(2)}, u32[]{:S(2)}) collective-permute-start(f32[24,128]{1,0:T(8,128)S(1)} %get-tuple-element.36), channel_id=1, source_target_pairs={{0,6},{1,7},{2,0},{3,1},{4,2},{5,3},{6,4},{7,5},{8,14},{9,15},{10,... | collective-permute-start | bytes 36872 | tf_op jit(solution)/shard_map/ppermute | solution.py:248

commit v6 on v5

--- a/solution.py
+++ b/solution.py
@@ -108,8 +108,14 @@
     return jnp.transpose(acc[0:half, :] + acc[half : 2 * half, :])
 
 
-def stage_own(shapes, plate, bend, left, total, sums, plain, cross, second, acc):
+def stage_own(place, shapes, plate, bend, left, total, sums, order, plain, cross, second, acc):
     stencil(shapes, plate, (plain, cross, second), bend, left, total)
+    size = order.shape[0]
+    r = lax.broadcasted_iota(jnp.int32, (size, 128), 0)
+    c = lax.broadcasted_iota(jnp.int32, (size, 128), 1)
+    target = ((r & 56) << 3) + ((((r >> 6) + place[0]) & 7) << 3) + (r & 7) - c
+    for first in range(0, size, 128):
+        order[:, first : first + 128] = jnp.where(target == first, 1.0, 0.0).astype(bf16)
     sums[...] = pair_sums(plate, [(left, bend)], acc)
 
 
@@ -158,12 +164,6 @@
     return a, b, (rest - b.astype(f32)).astype(bf16)
 
 
-def exact_dot(x, y, parts_of_y):
-    if parts_of_y:
-        return sum(jnp.dot(x, part, preferred_element_type=f32) for part in three_parts(y))
-    return sum(jnp.dot(part, y, preferred_element_type=f32) for part in three_parts(x))
-
-
 def gather_zones(received, lists, mine, to_far, to_next):
     places, width = received.shape
     zones = mine.shape[0]
@@ -172,7 +172,9 @@
         jnp.int32, (zones, places), 0
     )
     chosen = jnp.where(chosen, 1.0, 0.0).astype(bf16)
-    zoned = exact_dot(chosen, received[:, 0:body], True)
+    zoned = sum(
+        jnp.dot(chosen, part, preferred_element_type=f32) for part in three_parts(received[:, 0:body])
+    )
     totals = jnp.sum(received[:, body:].reshape(places // 8, 8, 128), axis=0)
     mine[...] = zoned[:, 0:128]
     to_far[0:8, :] = totals
@@ -182,7 +184,7 @@
     to_next[zones + 8 :, :] = zoned[:, 256:384]
 
 
-def normalise(place, mine, kept, from_far, from_below, energy):
+def normalise(order, mine, kept, from_far, from_below, energy):
     zones = energy.shape[0]
     t = slice(0, 8)
     y = slice(8, zones + 8)
@@ -202,18 +204,13 @@
     spread = jnp.concatenate([jnp.broadcast_to(c, (8, 64)) for c in columns], axis=1)
     sub = lax.broadcasted_iota(jnp.int32, (8, 512), 0)
     lane = lax.broadcasted_iota(jnp.int32, (8, 512), 1)
-    total_j = jnp.sum(jnp.where(lane % 8 == sub, spread, 0.0), axis=0, keepdims=True)
+    total_j = jnp.sum(jnp.where((lane & 7) == sub, spread, 0.0), axis=0, keepdims=True)
     total_i = jnp.sum(
-        jnp.where((lane // 8) % 8 == sub, jnp.broadcast_to(own[:, 0:1], (8, 512)), 0.0), axis=0, keepdims=True
+        jnp.where(((lane >> 3) & 7) == sub, jnp.broadcast_to(own[:, 0:1], (8, 512)), 0.0), axis=0, keepdims=True
     )
     scaled = ZONES * (0.5 * sums) / jnp.sqrt((0.5 * total_i) * (0.5 * total_j))
-    r = lax.broadcasted_iota(jnp.int32, (512, 128), 0)
-    c = lax.broadcasted_iota(jnp.int32, (512, 128), 1)
-    target = ((r & 56) << 3) + ((((r >> 6) + place[0]) & 7) << 3) + (r & 7) - c
-    order = jnp.concatenate(
-        [jnp.where(target == first, 1.0, 0.0).astype(bf16) for first in range(0, 512, 128)], axis=1
-    )
-    ordered = exact_dot(scaled, order, False)
+    parts = jnp.dot(jnp.concatenate(three_parts(scaled), axis=0), order[...], preferred_element_type=f32)
+    ordered = parts[0:zones] + parts[zones : 2 * zones] + parts[2 * zones :]
     for i in range(8):
         energy[:, i, :] = ordered[:, i * 64 : (i + 1) * 64]
 
@@ -249,11 +246,11 @@
 
     lists = lax.dynamic_index_in_dim(slot_zone, lax.axis_index("tile"), 1, keepdims=False)
     lists = lists.reshape(1, slots)
-    plate = jnp.stack([stiffness, node_slot.astype(f32)])
     head = lax.ppermute(mode_shapes[:, rows - 1], "tile", up)
     tail = lax.ppermute(mode_shapes[:, 0], "tile", down)
     framed = jnp.concatenate([head[None], jnp.transpose(mode_shapes, (1, 0, 2)), tail[None]], axis=0)
-    framed, lists, plate = lax.optimization_barrier((framed, lists, plate))
+    framed, lists, rigid, named = lax.optimization_barrier((framed, lists, stiffness, node_slot))
+    plate = jnp.stack([rigid, named.astype(f32)])
     below = turn(framed, 1)
     above = turn(framed, -1)
     far_below = turn(below, 1)
@@ -263,10 +260,11 @@
     total = ((modes, 128), f32)
     lines = [vmem((rows + 2, modes, cells))] * 3
     pairs = modes * modes
-    bend0, left0, total0, own_sums = call(
-        stage_own, [factor, factor, total, ((slots, pairs), f32)],
+    place = lax.axis_index("mode").astype(jnp.int32).reshape(1)
+    bend0, left0, total0, own_sums, order = call(
+        stage_own, [factor, factor, total, ((slots, pairs), f32), ((8 * pairs, 8 * pairs), bf16)],
         lines + [vmem((2 * pairs, slots))],
-        framed, plate,
+        place, framed, plate, spaces=(pltpu.SMEM,),
     )
     bend_above, left_above, total_above, near_sums = call(
         stage_near, [factor, factor, total, ((slots, 3 * pairs), f32)],
@@ -288,10 +286,9 @@
     )
     from_far = turn(to_far, -2)
     from_below = turn(to_next, 1)
-    place = lax.axis_index("mode").astype(jnp.int32).reshape(1)
     (energy,) = call(
         normalise, [((owned, modes, panels * modes), f32)], [],
-        place, mine, to_next, from_far, from_below, spaces=(pltpu.SMEM,),
+        order, mine, to_next, from_far, from_below,
     )
     return energy
 

time: 74 us -> 74.3 us (level)
  waiting for transfers between devices: 13.4 us -> 14.9 us
  other arithmetic: 1.75 us -> 0.9 us
    ppermute x1, waiting for transfers between devices: 0.65 us -> 2.35 us  [per_device(): tail = lax.ppermute(mode_shapes[:, 0], 'tile', down)]
    another operation x2, other arithmetic: 1.7 us -> 0.86 us  [per_device(): plate = jnp.stack([rigid, named.astype(f32)])]
  transfers between devices with their start and end apart: 8 -> 8, of which waited for: 5 -> 4; matrix products, arithmetic and copies ran while one was open for 3% -> 2% of each run, Pallas kernels for 15% -> 16%
where the time goes in v6:
time: 74.3 us; the launch traced here: 74.1 us
  blocking collectives  21.8 us (29%)
  Pallas kernels  21.3 us (29%)
  waiting for transfers between devices  14.9 us (20%)
  starting transfers between devices  13.2 us (18%)
  local copies, waits for them, and re-layouts  1.93 us (3%)
  other arithmetic  0.9 us (1%)
    all_to_all x1, blocking collectives, per_device(): received = lax.all_to_all(message, 'tile', 0, 0, tiled=True)  21.8 us
    pallas_call x5, Pallas kernels, call(): pl.pallas_call(body, out_shape=[jax.ShapeDtypeStruct(s, d) for s, d in ou...  21.3 us
    ppermute x6, waiting for transfers between devices, turn(): lax.ppermute(x, 'mode', [(i, (i + by) % panels) for i in range(panels)])  12.5 us
    ppermute x6, starting transfers between devices, turn(): lax.ppermute(x, 'mode', [(i, (i + by) % panels) for i in range(panels)])  10.1 us
    ppermute x1, waiting for transfers between devices, per_device(): tail = lax.ppermute(mode_shapes[:, 0], 'tile', down)  2.35 us
    ppermute x1, starting transfers between devices, per_device(): head = lax.ppermute(mode_shapes[:, rows - 1], 'tile', up)  1.74 us
  transfers between devices with their start and end apart: 8, of which 4 were waited for; matrix products, arithmetic and copies ran while one was open for 2% of the time, Pallas kernels for 16%

profile of v6, /device:TPU:96, one launch (start us, length us, event | category | flops | bytes accessed | tf_op | source)
XLA Modules:
  0.0 74.1 jit_solution(18251933751698622116)
XLA Ops:
  0.0 0.0 copy-start
  0.0 0.0 copy-start.1
  0.0 1.1 %copy.13 = bf16[8,8,2048]{2,0,1:T(8,128)(2,1)S(1)} copy(bf16[8,8,2048]{2,1,0:T(8,128)(2,1)} %param.4) | data formatting | bytes 524288 | tf_op args[0]
  1.2 1.7 %collective-permute-start = (bf16[8,2048]{1,0:T(8,128)(2,1)S(1)}, bf16[8,2048]{1,0:T(8,128)(2,1)S(1)}, u32[]{:S(2)}, u32[]{:S(2)}) collective-permute-start(bf16[8,2048]{1,0:T(8,128)(2,1)S(1)} %get-tuple-element.41), channel_id=1, source_target_pairs={{0,8},{8,16},{16,24},{24,32},{32,40},{40,48},{48,56},{56,64},{64,7... | collective-permute-start | bytes 98312 | tf_op jit(solution)/shard_map/ppermute | solution.py:249
  2.9 1.3 %collective-permute-start.1 = (bf16[8,2048]{1,0:T(8,128)(2,1)S(1)}, bf16[8,2048]{1,0:T(8,128)(2,1)S(1)}, u32[]{:S(2)}, u32[]{:S(2)}) collective-permute-start(bf16[8,2048]{1,0:T(8,128)(2,1)S(1)} %get-tuple-element.42), channel_id=1, source_target_pairs={{8,0},{16,8},{24,16},{32,24},{40,32},{48,40},{56,48},{64,56},{72,6... | collective-permute-start | bytes 98312 | tf_op jit(solution)/shard_map/ppermute | solution.py:250
  4.2 0.0 copy-done
  4.2 0.7 dynamic-slice_reduce_fusion
  4.9 0.1 reshape.11.lists
  5.0 0.0 collective-permute-done
  5.0 2.4 %collective-permute-done.1 = bf16[8,2048]{1,0:T(8,128)(2,1)S(1)} collective-permute-done((bf16[8,2048]{1,0:T(8,128)(2,1)S(1)}, bf16[8,2048]{1,0:T(8,128)(2,1)S(1)}, u32[]{:S(2)}, u32[]{:S(2)}) %collective-permute-start.1) | collective-permute-done | bytes 32800 | tf_op jit(solution)/shard_map/ppermute | solution.py:250
  7.4 3.2 %collective-permute-start.2 = (bf16[10,8,2048]{2,1,0:T(8,128)(2,1)S(1)}, bf16[10,8,2048]{2,1,0:T(8,128)(2,1)S(1)}, u32[]{:S(2)}, u32[]{:S(2)}) collective-permute-start(bf16[10,8,2048]{2,1,0:T(8,128)(2,1)S(1)} %pad_maximum_fusion.shapes), channel_id=1, source_target_pairs={{0,1},{1,2},{2,3},{3,4},{4,5},{5,6},{6,7},{7,0},{8,9},{9,10},{10,1... | collective-permute-start | bytes 983048 | tf_op jit(solution)/shard_map/ppermute | solution.py:245
  10.6 0.0 collective-permute-start.4
  10.6 6.4 %collective-permute-done.2.below = bf16[10,8,2048]{2,1,0:T(8,128)(2,1)S(1)} collective-permute-done((bf16[10,8,2048]{2,1,0:T(8,128)(2,1)S(1)}, bf16[10,8,2048]{2,1,0:T(8,128)(2,1)S(1)}, u32[]{:S(2)}, u32[]{:S(2)}) %collective-permute-start.2) | collective-permute-done | bytes 327712 | tf_op jit(solution)/shard_map/ppermute | solution.py:245
  17.1 3.7 %collective-permute-start.3 = (bf16[10,8,2048]{2,1,0:T(8,128)(2,1)S(1)}, bf16[10,8,2048]{2,1,0:T(8,128)(2,1)S(1)}, u32[]{:S(2)}, u32[]{:S(2)}) collective-permute-start(bf16[10,8,2048]{2,1,0:T(8,128)(2,1)S(1)} %collective-permute-done.2.below), channel_id=1, source_target_pairs={{0,1},{1,2},{2,3},{3,4},{4,5},{5,6},{6,7},{7,0},{8,9},{9,10},{10,1... | collective-permute-start | bytes 983048 | tf_op jit(solution)/shard_map/ppermute | solution.py:245
  20.8 0.3 collective-permute-done.4.above
  21.0 0.0 collective-permute-start.5
  21.0 0.8 %convert_bitcast_fusion = f32[1,8,2048]{2,1,0:T(8,128)S(1)} fusion(s32[8,2048]{1,0:T(8,128)} %param.6), kind=kLoop, calls=%fused_computation.3 | loop fusion | flops 16384 | bytes 131072 | tf_op jit(solution)/shard_map/stack | solution.py:253
  21.9 0.0 copy-done.1
  21.9 4.7 %shard_map.46 = (f32[3,8,8,2048]{3,2,1,0:T(8,128)S(1)}, f32[3,8,8,2048]{3,2,1,0:T(8,128)S(1)}, f32[8,128]{1,0:T(8,128)S(1)}, f32[256,64]{1,0:T(8,128)S(1)}, bf16[512,512]{1,0:T(8,128)(2,1)S(1)}) custom-call(s32[1]{0:T(128)} %bitcast.place, bf16[10,8,2048]{2,1,0:T(8,128)(2,1)S(1)} %pad_maximum_fusion.shapes, f32[2,8,2048]{2,1,0:T(8,128)S(1)} %pad_maximum_fusion.1.plate), custom_call_target="tpu_custom_call" | custom-call | tf_op jit(solution)/shard_map/pallas_call | solution.py:224
  26.6 6.9 %shard_map.47 = (f32[3,8,8,2048]{3,2,1,0:T(8,128)S(1)}, f32[3,8,8,2048]{3,2,1,0:T(8,128)S(1)}, f32[8,128]{1,0:T(8,128)S(1)}, f32[256,192]{1,0:T(8,128)S(1)}) custom-call(bf16[10,8,2048]{2,1,0:T(8,128)(2,1)S(1)} %collective-permute-done.2.below, bf16[10,8,2048]{2,1,0:T(8,128)(2,1)S(1)} %collective-permute-done.4.above, ...), custom_call_target="tpu_custom_call" | custom-call | tf_op jit(solution)/shard_map/pallas_call | solution.py:224
  33.5 0.0 collective-permute-done.3.below
  33.5 0.0 collective-permute-done.5.above
  33.5 8.4 %shard_map.48 = f32[32,8,640]{2,1,0:T(8,128)S(1)} custom-call(bf16[10,8,2048]{2,1,0:T(8,128)(2,1)S(1)} %collective-permute-done.3.below, bf16[10,8,2048]{2,1,0:T(8,128)(2,1)S(1)} %collective-permute-done.5.above, f32[2,8,2048]{2,1,0:T(8,128)S(1)} %pad_maximum_fusion.1.plate, f32[3,8,8,2048]{3,2,1,0:T(8,128)S(1)} %get-tuple-element.27.left, ...), custom_call_target="tpu_custom_call" | custom-call | tf_op jit(solution)/shard_map/pallas_call | solution.py:224
  42.0 21.8 %all_to_all.5 = f32[32,8,640]{2,1,0:T(8,128)S(1)} all-to-all(f32[32,8,640]{2,1,0:T(8,128)S(1)} %shard_map.48), channel_id=1, replica_groups=mesh['tile'=32,'mode'=8] {'tile'}, dimensions={0} | all-to-all | bytes 1310720 | tf_op jit(solution)/shard_map/all_to_all | solution.py:281
  63.8 0.3 shard_map.49
  64.0 3.2 %collective-permute-start.7 = (f32[40,128]{1,0:T(8,128)S(1)}, f32[40,128]{1,0:T(8,128)S(1)}, u32[]{:S(2)}, u32[]{:S(2)}) collective-permute-start(f32[40,128]{1,0:T(8,128)S(1)} %get-tuple-element.39.kept), channel_id=1, source_target_pairs={{0,1},{1,2},{2,3},{3,4},{4,5},{5,6},{6,7},{7,0},{8,9},{9,10},{10,1... | collective-permute-start | bytes 61448 | tf_op jit(solution)/shard_map/ppermute | solution.py:245
  67.3 0.0 collective-permute-start.6
  67.3 5.8 %collective-permute-done.6.from_far = f32[24,128]{1,0:T(8,128)S(1)} collective-permute-done((f32[24,128]{1,0:T(8,128)S(1)}, f32[24,128]{1,0:T(8,128)S(1)}, u32[]{:S(2)}, u32[]{:S(2)}) %collective-permute-start.6) | collective-permute-done | bytes 12320 | tf_op jit(solution)/shard_map/ppermute | solution.py:245
  73.1 0.0 collective-permute-done.7.from_below
  73.1 1.0 %shard_map.50 = f32[16,8,64]{2,1,0:T(8,128)} custom-call(bf16[512,512]{1,0:T(8,128)(2,1)S(1)} %get-tuple-element.26.order, f32[16,128]{1,0:T(8,128)S(1)} %get-tuple-element.38.mine, f32[40,128]{1,0:T(8,128)S(1)} %get-tuple-element.39.kept, f32[24,128]{1,0:T(8,128)S(1)} %collective-permute-done.6.from_far, f32[40,128]{1,0:T(8,128)S(1)} %collective-permute-done.7.from_below), custom_call_target="tpu_custom_call" | custom-call | tf_op jit(solution)/shard_map/pallas_call | solution.py:224
  (3 shorter events, 0.1 us)
Async XLA Ops:
  0.0 4.2 %copy-start = (s32[32,32,8]{1,2,0:T(8,128)S(1)}, s32[32,32,8]{1,2,0:T(8,128)}, u32[]{:S(2)}) copy-start(s32[32,32,8]{1,2,0:T(8,128)} %param.7) | copy-start | bytes 98308
  0.0 21.9 %copy-start.1 = (f32[8,2048]{1,0:T(8,128)S(1)}, f32[8,2048]{1,0:T(8,128)}, u32[]{:S(2)}) copy-start(f32[8,2048]{1,0:T(8,128)} %param.5) | copy-start | bytes 196612
  1.2 3.8 %collective-permute-start = (bf16[8,2048]{1,0:T(8,128)(2,1)S(1)}, bf16[8,2048]{1,0:T(8,128)(2,1)S(1)}, u32[]{:S(2)}, u32[]{:S(2)}) collective-permute-start(bf16[8,2048]{1,0:T(8,128)(2,1)S(1)} %get-tuple-element.41), channel_id=1, source_target_pairs={{0,8},{8,16},{16,24},{24,32},{32,40},{40,48},{48,56},{56,64},{64,7... | collective-permute-start | bytes 98312 | tf_op jit(solution)/shard_map/ppermute | solution.py:249
  2.9 4.5 %collective-permute-start.1 = (bf16[8,2048]{1,0:T(8,128)(2,1)S(1)}, bf16[8,2048]{1,0:T(8,128)(2,1)S(1)}, u32[]{:S(2)}, u32[]{:S(2)}) collective-permute-start(bf16[8,2048]{1,0:T(8,128)(2,1)S(1)} %get-tuple-element.42), channel_id=1, source_target_pairs={{8,0},{16,8},{24,16},{32,24},{40,32},{48,40},{56,48},{64,56},{72,6... | collective-permute-start | bytes 98312 | tf_op jit(solution)/shard_map/ppermute | solution.py:250
  7.4 9.6 %collective-permute-start.2 = (bf16[10,8,2048]{2,1,0:T(8,128)(2,1)S(1)}, bf16[10,8,2048]{2,1,0:T(8,128)(2,1)S(1)}, u32[]{:S(2)}, u32[]{:S(2)}) collective-permute-start(bf16[10,8,2048]{2,1,0:T(8,128)(2,1)S(1)} %pad_maximum_fusion.shapes), channel_id=1, source_target_pairs={{0,1},{1,2},{2,3},{3,4},{4,5},{5,6},{6,7},{7,0},{8,9},{9,10},{10,1... | collective-permute-start | bytes 983048 | tf_op jit(solution)/shard_map/ppermute | solution.py:245
  10.6 10.4 %collective-permute-start.4 = (bf16[10,8,2048]{2,1,0:T(8,128)(2,1)S(1)}, bf16[10,8,2048]{2,1,0:T(8,128)(2,1)S(1)}, u32[]{:S(2)}, u32[]{:S(2)}) collective-permute-start(bf16[10,8,2048]{2,1,0:T(8,128)(2,1)S(1)} %pad_maximum_fusion.shapes), channel_id=1, source_target_pairs={{0,7},{1,0},{2,1},{3,2},{4,3},{5,4},{6,5},{7,6},{8,15},{9,8},{10,9... | collective-permute-start | bytes 983048 | tf_op jit(solution)/shard_map/ppermute | solution.py:245
  17.1 16.5 %collective-permute-start.3 = (bf16[10,8,2048]{2,1,0:T(8,128)(2,1)S(1)}, bf16[10,8,2048]{2,1,0:T(8,128)(2,1)S(1)}, u32[]{:S(2)}, u32[]{:S(2)}) collective-permute-start(bf16[10,8,2048]{2,1,0:T(8,128)(2,1)S(1)} %collective-permute-done.2.below), channel_id=1, source_target_pairs={{0,1},{1,2},{2,3},{3,4},{4,5},{5,6},{6,7},{7,0},{8,9},{9,10},{10,1... | collective-permute-start | bytes 983048 | tf_op jit(solution)/shard_map/ppermute | solution.py:245
  21.0 12.5 %collective-permute-start.5 = (bf16[10,8,2048]{2,1,0:T(8,128)(2,1)S(1)}, bf16[10,8,2048]{2,1,0:T(8,128)(2,1)S(1)}, u32[]{:S(2)}, u32[]{:S(2)}) collective-permute-start(bf16[10,8,2048]{2,1,0:T(8,128)(2,1)S(1)} %collective-permute-done.4.above), channel_id=1, source_target_pairs={{0,7},{1,0},{2,1},{3,2},{4,3},{5,4},{6,5},{7,6},{8,15},{9,8},{10,9... | collective-permute-start | bytes 983048 | tf_op jit(solution)/shard_map/ppermute | solution.py:245
  64.0 9.0 %collective-permute-start.7 = (f32[40,128]{1,0:T(8,128)S(1)}, f32[40,128]{1,0:T(8,128)S(1)}, u32[]{:S(2)}, u32[]{:S(2)}) collective-permute-start(f32[40,128]{1,0:T(8,128)S(1)} %get-tuple-element.39.kept), channel_id=1, source_target_pairs={{0,1},{1,2},{2,3},{3,4},{4,5},{5,6},{6,7},{7,0},{8,9},{9,10},{10,1... | collective-permute-start | bytes 61448 | tf_op jit(solution)/shard_map/ppermute | solution.py:245
  67.3 5.8 %collective-permute-start.6 = (f32[24,128]{1,0:T(8,128)S(1)}, f32[24,128]{1,0:T(8,128)S(1)}, u32[]{:S(2)}, u32[]{:S(2)}) collective-permute-start(f32[24,128]{1,0:T(8,128)S(1)} %get-tuple-element.40), channel_id=1, source_target_pairs={{0,6},{1,7},{2,0},{3,1},{4,2},{5,3},{6,4},{7,5},{8,14},{9,15},{10,... | collective-permute-start | bytes 36872 | tf_op jit(solution)/shard_map/ppermute | solution.py:245

commit v7 on v6

--- a/solution.py
+++ b/solution.py
@@ -104,7 +104,7 @@
         )
         return carry
 
-    lax.fori_loop(0, rows, one_row, 0, unroll=2)
+    lax.fori_loop(0, rows, one_row, 0, unroll=4)
     return jnp.transpose(acc[0:half, :] + acc[half : 2 * half, :])
 
 
@@ -244,13 +244,16 @@
     def turn(x, by):
         return lax.ppermute(x, "mode", [(i, (i + by) % panels) for i in range(panels)])
 
-    lists = lax.dynamic_index_in_dim(slot_zone, lax.axis_index("tile"), 1, keepdims=False)
-    lists = lists.reshape(1, slots)
-    head = lax.ppermute(mode_shapes[:, rows - 1], "tile", up)
-    tail = lax.ppermute(mode_shapes[:, 0], "tile", down)
+    row = lax.broadcasted_iota(jnp.int32, mode_shapes.shape, 1)
+    last = jnp.sum(jnp.where(row == rows - 1, mode_shapes, 0), axis=1)
+    first = jnp.sum(jnp.where(row == 0, mode_shapes, 0), axis=1)
+    head = lax.ppermute(last, "tile", up)
+    tail = lax.ppermute(first, "tile", down)
     framed = jnp.concatenate([head[None], jnp.transpose(mode_shapes, (1, 0, 2)), tail[None]], axis=0)
-    framed, lists, rigid, named = lax.optimization_barrier((framed, lists, stiffness, node_slot))
+    framed, rigid, named, places = lax.optimization_barrier((framed, stiffness, node_slot, slot_zone))
     plate = jnp.stack([rigid, named.astype(f32)])
+    lists = lax.dynamic_index_in_dim(places, lax.axis_index("tile"), 1, keepdims=False).reshape(1, slots)
+    plate, lists = lax.optimization_barrier((plate, lists))
     below = turn(framed, 1)
     above = turn(framed, -1)
     far_below = turn(below, 1)

time: 74.3 us -> 73.4 us (0.988)
  Pallas kernels: 21.3 us -> 20.3 us
    reduce_sum x0 -> x1, other arithmetic: none -> 1.31 us  [per_device(): last = jnp.sum(jnp.where(row == rows - 1, mode_shapes, 0), axis=1)]
    pallas_call x5, Pallas kernels: 21.3 us -> 20.3 us  [call(): pl.pallas_call(body, out_shape=[jax.ShapeDtypeStruct(s, d) for s, d in ou...]
    another operation x2, other arithmetic: 0.86 us -> 0.02 us  [per_device(): plate = jnp.stack([rigid, named.astype(f32)])]
  transfers between devices with their start and end apart: 8 -> 8, of which waited for: 4 -> 4; matrix products, arithmetic and copies ran while one was open for 2% -> 3% of each run, Pallas kernels for 16% -> 15%
where the time goes in v7:
time: 73.4 us; the launch traced here: 73.2 us
  blocking collectives  21.8 us (30%)
  Pallas kernels  20.3 us (28%)
  waiting for transfers between devices  14.6 us (20%)
  starting transfers between devices  13.2 us (18%)
  local copies, waits for them, and re-layouts  1.89 us (3%)
  other arithmetic  1.37 us (2%)
    all_to_all x1, blocking collectives, per_device(): received = lax.all_to_all(message, 'tile', 0, 0, tiled=True)  21.8 us
    pallas_call x5, Pallas kernels, call(): pl.pallas_call(body, out_shape=[jax.ShapeDtypeStruct(s, d) for s, d in ou...  20.3 us
    ppermute x6, waiting for transfers between devices, turn(): lax.ppermute(x, 'mode', [(i, (i + by) % panels) for i in range(panels)])  12.5 us
    ppermute x6, starting transfers between devices, turn(): lax.ppermute(x, 'mode', [(i, (i + by) % panels) for i in range(panels)])  10.1 us
    ppermute x1, waiting for transfers between devices, per_device(): tail = lax.ppermute(first, 'tile', down)  2.05 us
    ppermute x1, starting transfers between devices, per_device(): head = lax.ppermute(last, 'tile', up)  1.74 us
  transfers between devices with their start and end apart: 8, of which 4 were waited for; matrix products, arithmetic and copies ran while one was open for 3% of the time, Pallas kernels for 15%

profile of v7, /device:TPU:96, one launch (start us, length us, event | category | flops | bytes accessed | tf_op | source)
XLA Modules:
  0.0 73.2 jit_solution(8574559294427415088)
XLA Ops:
  0.0 0.0 copy-start
  0.0 0.0 copy-start.2
  0.0 0.0 copy-start.1
  0.0 1.3 %select_reduce_fusion.1 = (bf16[8,2048]{1,0:T(8,128)(2,1)S(1)}, bf16[8,2048]{1,0:T(8,128)(2,1)S(1)}) fusion(bf16[8,8,2048]{2,1,0:T(8,128)(2,1)} %param.4, pred[8]{0:T(512)(128)(4,1)S(1)} %get-tuple-element.48, pred[8]{0:T(512)(128)(4,1)S(1)} %get-tuple-element.47), kind=kLoop, calls=%fused_computation.3 | loop fusion | flops 491520 | bytes 327696 | tf_op jit(solution)/shard_map/reduce_sum | solution.py:248
  1.3 1.7 %collective-permute-start = (bf16[8,2048]{1,0:T(8,128)(2,1)S(1)}, bf16[8,2048]{1,0:T(8,128)(2,1)S(1)}, u32[]{:S(2)}, u32[]{:S(2)}) collective-permute-start(bf16[8,2048]{1,0:T(8,128)(2,1)S(1)} %get-tuple-element.45), channel_id=1, source_target_pairs={{0,8},{8,16},{16,24},{24,32},{32,40},{40,48},{48,56},{56,64},{64,7... | collective-permute-start | bytes 98312 | tf_op jit(solution)/shard_map/ppermute | solution.py:250
  3.1 1.3 %collective-permute-start.1 = (bf16[8,2048]{1,0:T(8,128)(2,1)S(1)}, bf16[8,2048]{1,0:T(8,128)(2,1)S(1)}, u32[]{:S(2)}, u32[]{:S(2)}) collective-permute-start(bf16[8,2048]{1,0:T(8,128)(2,1)S(1)} %get-tuple-element.46), channel_id=1, source_target_pairs={{8,0},{16,8},{24,16},{32,24},{40,32},{48,40},{56,48},{64,56},{72,6... | collective-permute-start | bytes 98312 | tf_op jit(solution)/shard_map/ppermute | solution.py:251
  4.4 1.1 %copy.8 = bf16[8,8,2048]{2,0,1:T(8,128)(2,1)S(1)} copy(bf16[8,8,2048]{2,1,0:T(8,128)(2,1)} %param.4) | data formatting | bytes 524288 | tf_op args[0]
  5.5 0.0 collective-permute-done
  5.5 2.0 %collective-permute-done.1 = bf16[8,2048]{1,0:T(8,128)(2,1)S(1)} collective-permute-done((bf16[8,2048]{1,0:T(8,128)(2,1)S(1)}, bf16[8,2048]{1,0:T(8,128)(2,1)S(1)}, u32[]{:S(2)}, u32[]{:S(2)}) %collective-permute-start.1) | collective-permute-done | bytes 32800 | tf_op jit(solution)/shard_map/ppermute | solution.py:251
  7.6 3.2 %collective-permute-start.2 = (bf16[10,8,2048]{2,1,0:T(8,128)(2,1)S(1)}, bf16[10,8,2048]{2,1,0:T(8,128)(2,1)S(1)}, u32[]{:S(2)}, u32[]{:S(2)}) collective-permute-start(bf16[10,8,2048]{2,1,0:T(8,128)(2,1)S(1)} %pad_maximum_fusion.shapes), channel_id=1, source_target_pairs={{0,1},{1,2},{2,3},{3,4},{4,5},{5,6},{6,7},{7,0},{8,9},{9,10},{10,1... | collective-permute-start | bytes 983048 | tf_op jit(solution)/shard_map/ppermute | solution.py:245
  10.8 0.0 collective-permute-start.4
  10.8 6.4 %collective-permute-done.2.below = bf16[10,8,2048]{2,1,0:T(8,128)(2,1)S(1)} collective-permute-done((bf16[10,8,2048]{2,1,0:T(8,128)(2,1)S(1)}, bf16[10,8,2048]{2,1,0:T(8,128)(2,1)S(1)}, u32[]{:S(2)}, u32[]{:S(2)}) %collective-permute-start.2) | collective-permute-done | bytes 327712 | tf_op jit(solution)/shard_map/ppermute | solution.py:245
  17.2 3.7 %collective-permute-start.3 = (bf16[10,8,2048]{2,1,0:T(8,128)(2,1)S(1)}, bf16[10,8,2048]{2,1,0:T(8,128)(2,1)S(1)}, u32[]{:S(2)}, u32[]{:S(2)}) collective-permute-start(bf16[10,8,2048]{2,1,0:T(8,128)(2,1)S(1)} %collective-permute-done.2.below), channel_id=1, source_target_pairs={{0,1},{1,2},{2,3},{3,4},{4,5},{5,6},{6,7},{7,0},{8,9},{9,10},{10,1... | collective-permute-start | bytes 983048 | tf_op jit(solution)/shard_map/ppermute | solution.py:245
  20.9 0.3 collective-permute-done.4.above
  21.2 0.0 collective-permute-start.5
  21.2 0.0 copy-done.1
  21.2 0.0 copy-done
  21.2 0.7 dynamic-slice_reduce_fusion
  21.9 0.1 reshape.11.lists
  22.0 0.0 copy-done.2
  22.1 4.4 %shard_map.46 = (f32[3,8,8,2048]{3,2,1,0:T(8,128)S(1)}, f32[3,8,8,2048]{3,2,1,0:T(8,128)S(1)}, f32[8,128]{1,0:T(8,128)S(1)}, f32[256,64]{1,0:T(8,128)S(1)}, bf16[512,512]{1,0:T(8,128)(2,1)S(1)}) custom-call(s32[1]{0:T(128)} %bitcast.place, bf16[10,8,2048]{2,1,0:T(8,128)(2,1)S(1)} %pad_maximum_fusion.shapes, f32[2,8,2048]{2,1,0:T(8,128)S(1)} %pad_maximum_fusion.1.plate), custom_call_target="tpu_custom_call" | custom-call | tf_op jit(solution)/shard_map/pallas_call | solution.py:224
  26.5 6.5 %shard_map.47 = (f32[3,8,8,2048]{3,2,1,0:T(8,128)S(1)}, f32[3,8,8,2048]{3,2,1,0:T(8,128)S(1)}, f32[8,128]{1,0:T(8,128)S(1)}, f32[256,192]{1,0:T(8,128)S(1)}) custom-call(bf16[10,8,2048]{2,1,0:T(8,128)(2,1)S(1)} %collective-permute-done.2.below, bf16[10,8,2048]{2,1,0:T(8,128)(2,1)S(1)} %collective-permute-done.4.above, ...), custom_call_target="tpu_custom_call" | custom-call | tf_op jit(solution)/shard_map/pallas_call | solution.py:224
  33.0 0.0 collective-permute-done.3.below
  33.0 0.0 collective-permute-done.5.above
  33.0 8.0 %shard_map.48 = f32[32,8,640]{2,1,0:T(8,128)S(1)} custom-call(bf16[10,8,2048]{2,1,0:T(8,128)(2,1)S(1)} %collective-permute-done.3.below, bf16[10,8,2048]{2,1,0:T(8,128)(2,1)S(1)} %collective-permute-done.5.above, f32[2,8,2048]{2,1,0:T(8,128)S(1)} %pad_maximum_fusion.1.plate, f32[3,8,8,2048]{3,2,1,0:T(8,128)S(1)} %get-tuple-element.31.left, ...), custom_call_target="tpu_custom_call" | custom-call | tf_op jit(solution)/shard_map/pallas_call | solution.py:224
  41.1 21.8 %all_to_all.5 = f32[32,8,640]{2,1,0:T(8,128)S(1)} all-to-all(f32[32,8,640]{2,1,0:T(8,128)S(1)} %shard_map.48), channel_id=1, replica_groups=mesh['tile'=32,'mode'=8] {'tile'}, dimensions={0} | all-to-all | bytes 1310720 | tf_op jit(solution)/shard_map/all_to_all | solution.py:284
  62.9 0.3 shard_map.49
  63.2 3.2 %collective-permute-start.7 = (f32[40,128]{1,0:T(8,128)S(1)}, f32[40,128]{1,0:T(8,128)S(1)}, u32[]{:S(2)}, u32[]{:S(2)}) collective-permute-start(f32[40,128]{1,0:T(8,128)S(1)} %get-tuple-element.43.kept), channel_id=1, source_target_pairs={{0,1},{1,2},{2,3},{3,4},{4,5},{5,6},{6,7},{7,0},{8,9},{9,10},{10,1... | collective-permute-start | bytes 61448 | tf_op jit(solution)/shard_map/ppermute | solution.py:245
  66.4 0.0 collective-permute-start.6
  66.4 5.8 %collective-permute-done.6.from_far = f32[24,128]{1,0:T(8,128)S(1)} collective-permute-done((f32[24,128]{1,0:T(8,128)S(1)}, f32[24,128]{1,0:T(8,128)S(1)}, u32[]{:S(2)}, u32[]{:S(2)}) %collective-permute-start.6) | collective-permute-done | bytes 12320 | tf_op jit(solution)/shard_map/ppermute | solution.py:245
  72.2 0.0 collective-permute-done.7.from_below
  72.2 1.0 %shard_map.50 = f32[16,8,64]{2,1,0:T(8,128)} custom-call(bf16[512,512]{1,0:T(8,128)(2,1)S(1)} %get-tuple-element.30.order, f32[16,128]{1,0:T(8,128)S(1)} %get-tuple-element.42.mine, f32[40,128]{1,0:T(8,128)S(1)} %get-tuple-element.43.kept, f32[24,128]{1,0:T(8,128)S(1)} %collective-permute-done.6.from_far, f32[40,128]{1,0:T(8,128)S(1)} %collective-permute-done.7.from_below), custom_call_target="tpu_custom_call" | custom-call | tf_op jit(solution)/shard_map/pallas_call | solution.py:224
  (4 shorter events, 0.1 us)
Async XLA Ops:
  0.0 21.2 %copy-start = (s32[32,32,8]{1,2,0:T(8,128)S(1)}, s32[32,32,8]{1,2,0:T(8,128)}, u32[]{:S(2)}) copy-start(s32[32,32,8]{1,2,0:T(8,128)} %param.7) | copy-start | bytes 98308
  0.0 22.0 %copy-start.2 = (f32[8,2048]{1,0:T(8,128)S(1)}, f32[8,2048]{1,0:T(8,128)}, u32[]{:S(2)}) copy-start(f32[8,2048]{1,0:T(8,128)} %param.5) | copy-start | bytes 196612
  0.0 21.2 %copy-start.1 = (s32[8,2048]{1,0:T(8,128)S(1)}, s32[8,2048]{1,0:T(8,128)}, u32[]{:S(2)}) copy-start(s32[8,2048]{1,0:T(8,128)} %param.6) | copy-start | bytes 196612
  1.3 4.2 %collective-permute-start = (bf16[8,2048]{1,0:T(8,128)(2,1)S(1)}, bf16[8,2048]{1,0:T(8,128)(2,1)S(1)}, u32[]{:S(2)}, u32[]{:S(2)}) collective-permute-start(bf16[8,2048]{1,0:T(8,128)(2,1)S(1)} %get-tuple-element.45), channel_id=1, source_target_pairs={{0,8},{8,16},{16,24},{24,32},{32,40},{40,48},{48,56},{56,64},{64,7... | collective-permute-start | bytes 98312 | tf_op jit(solution)/shard_map/ppermute | solution.py:250
  3.1 4.5 %collective-permute-start.1 = (bf16[8,2048]{1,0:T(8,128)(2,1)S(1)}, bf16[8,2048]{1,0:T(8,128)(2,1)S(1)}, u32[]{:S(2)}, u32[]{:S(2)}) collective-permute-start(bf16[8,2048]{1,0:T(8,128)(2,1)S(1)} %get-tuple-element.46), channel_id=1, source_target_pairs={{8,0},{16,8},{24,16},{32,24},{40,32},{48,40},{56,48},{64,56},{72,6... | collective-permute-start | bytes 98312 | tf_op jit(solution)/shard_map/ppermute | solution.py:251
  7.6 9.6 %collective-permute-start.2 = (bf16[10,8,2048]{2,1,0:T(8,128)(2,1)S(1)}, bf16[10,8,2048]{2,1,0:T(8,128)(2,1)S(1)}, u32[]{:S(2)}, u32[]{:S(2)}) collective-permute-start(bf16[10,8,2048]{2,1,0:T(8,128)(2,1)S(1)} %pad_maximum_fusion.shapes), channel_id=1, source_target_pairs={{0,1},{1,2},{2,3},{3,4},{4,5},{5,6},{6,7},{7,0},{8,9},{9,10},{10,1... | collective-permute-start | bytes 983048 | tf_op jit(solution)/shard_map/ppermute | solution.py:245
  10.8 10.4 %collective-permute-start.4 = (bf16[10,8,2048]{2,1,0:T(8,128)(2,1)S(1)}, bf16[10,8,2048]{2,1,0:T(8,128)(2,1)S(1)}, u32[]{:S(2)}, u32[]{:S(2)}) collective-permute-start(bf16[10,8,2048]{2,1,0:T(8,128)(2,1)S(1)} %pad_maximum_fusion.shapes), channel_id=1, source_target_pairs={{0,7},{1,0},{2,1},{3,2},{4,3},{5,4},{6,5},{7,6},{8,15},{9,8},{10,9... | collective-permute-start | bytes 983048 | tf_op jit(solution)/shard_map/ppermute | solution.py:245
  17.2 15.8 %collective-permute-start.3 = (bf16[10,8,2048]{2,1,0:T(8,128)(2,1)S(1)}, bf16[10,8,2048]{2,1,0:T(8,128)(2,1)S(1)}, u32[]{:S(2)}, u32[]{:S(2)}) collective-permute-start(bf16[10,8,2048]{2,1,0:T(8,128)(2,1)S(1)} %collective-permute-done.2.below), channel_id=1, source_target_pairs={{0,1},{1,2},{2,3},{3,4},{4,5},{5,6},{6,7},{7,0},{8,9},{9,10},{10,1... | collective-permute-start | bytes 983048 | tf_op jit(solution)/shard_map/ppermute | solution.py:245
  21.2 11.8 %collective-permute-start.5 = (bf16[10,8,2048]{2,1,0:T(8,128)(2,1)S(1)}, bf16[10,8,2048]{2,1,0:T(8,128)(2,1)S(1)}, u32[]{:S(2)}, u32[]{:S(2)}) collective-permute-start(bf16[10,8,2048]{2,1,0:T(8,128)(2,1)S(1)} %collective-permute-done.4.above), channel_id=1, source_target_pairs={{0,7},{1,0},{2,1},{3,2},{4,3},{5,4},{6,5},{7,6},{8,15},{9,8},{10,9... | collective-permute-start | bytes 983048 | tf_op jit(solution)/shard_map/ppermute | solution.py:245
  63.2 9.0 %collective-permute-start.7 = (f32[40,128]{1,0:T(8,128)S(1)}, f32[40,128]{1,0:T(8,128)S(1)}, u32[]{:S(2)}, u32[]{:S(2)}) collective-permute-start(f32[40,128]{1,0:T(8,128)S(1)} %get-tuple-element.43.kept), channel_id=1, source_target_pairs={{0,1},{1,2},{2,3},{3,4},{4,5},{5,6},{6,7},{7,0},{8,9},{9,10},{10,1... | collective-permute-start | bytes 61448 | tf_op jit(solution)/shard_map/ppermute | solution.py:245
  66.4 5.8 %collective-permute-start.6 = (f32[24,128]{1,0:T(8,128)S(1)}, f32[24,128]{1,0:T(8,128)S(1)}, u32[]{:S(2)}, u32[]{:S(2)}) collective-permute-start(f32[24,128]{1,0:T(8,128)S(1)} %get-tuple-element.44), channel_id=1, source_target_pairs={{0,6},{1,7},{2,0},{3,1},{4,2},{5,3},{6,4},{7,5},{8,14},{9,15},{10,... | collective-permute-start | bytes 36872 | tf_op jit(solution)/shard_map/ppermute | solution.py:245

commit v8 on v7

--- a/solution.py
+++ b/solution.py
@@ -244,11 +244,8 @@
     def turn(x, by):
         return lax.ppermute(x, "mode", [(i, (i + by) % panels) for i in range(panels)])
 
-    row = lax.broadcasted_iota(jnp.int32, mode_shapes.shape, 1)
-    last = jnp.sum(jnp.where(row == rows - 1, mode_shapes, 0), axis=1)
-    first = jnp.sum(jnp.where(row == 0, mode_shapes, 0), axis=1)
-    head = lax.ppermute(last, "tile", up)
-    tail = lax.ppermute(first, "tile", down)
+    head = lax.ppermute(mode_shapes[:, rows - 1], "tile", up)
+    tail = lax.ppermute(mode_shapes[:, 0], "tile", down)
     framed = jnp.concatenate([head[None], jnp.transpose(mode_shapes, (1, 0, 2)), tail[None]], axis=0)
     framed, rigid, named, places = lax.optimization_barrier((framed, stiffness, node_slot, slot_zone))
     plate = jnp.stack([rigid, named.astype(f32)])

time: 73.4 us -> 74.1 us (level)
  waiting for transfers between devices: 14.6 us -> 15.7 us
    reduce_sum x1 -> x0, other arithmetic: 1.31 us -> none  [per_device(): last = jnp.sum(jnp.where(row == rows - 1, mode_shapes, 0), axis=1)]
    ppermute x2, waiting for transfers between devices: 2.05 us -> 3.16 us  [the longest x1 3.15 us: per_device(): tail = lax.ppermute(mode_shapes[:, 0], 'tile', down)]
    another operation x2, other arithmetic: 0.02 us -> 0.86 us  [per_device(): plate = jnp.stack([rigid, named.astype(f32)])]
  transfers between devices with their start and end apart: 8 -> 8, of which waited for: 4 -> 4; matrix products, arithmetic and copies ran while one was open for 3% -> 2% of each run, Pallas kernels for 15% -> 15%
where the time goes in v8:
time: 74.1 us; the launch traced here: 73.9 us
  blocking collectives  21.8 us (29%)
  Pallas kernels  20.3 us (27%)
  waiting for transfers between devices  15.7 us (21%)
  starting transfers between devices  13.2 us (18%)
  local copies, waits for them, and re-layouts  1.93 us (3%)
  other arithmetic  0.9 us (1%)
    all_to_all x1, blocking collectives, per_device(): received = lax.all_to_all(message, 'tile', 0, 0, tiled=True)  21.8 us
    pallas_call x5, Pallas kernels, call(): pl.pallas_call(body, out_shape=[jax.ShapeDtypeStruct(s, d) for s, d in ou...  20.3 us
    ppermute x6, waiting for transfers between devices, turn(): lax.ppermute(x, 'mode', [(i, (i + by) % panels) for i in range(panels)])  12.5 us
    ppermute x6, starting transfers between devices, turn(): lax.ppermute(x, 'mode', [(i, (i + by) % panels) for i in range(panels)])  10.1 us
    ppermute x1, waiting for transfers between devices, per_device(): tail = lax.ppermute(mode_shapes[:, 0], 'tile', down)  3.15 us
    ppermute x1, starting transfers between devices, per_device(): head = lax.ppermute(mode_shapes[:, rows - 1], 'tile', up)  1.74 us
  transfers between devices with their start and end apart: 8, of which 4 were waited for; matrix products, arithmetic and copies ran while one was open for 2% of the time, Pallas kernels for 15%

profile of v8, /device:TPU:96, one launch (start us, length us, event | category | flops | bytes accessed | tf_op | source)
XLA Modules:
  0.0 73.9 jit_solution(611586147163213772)
XLA Ops:
  0.0 0.0 copy-start
  0.0 0.0 copy-start.1
  0.0 1.1 %copy.13 = bf16[8,8,2048]{2,0,1:T(8,128)(2,1)S(1)} copy(bf16[8,8,2048]{2,1,0:T(8,128)(2,1)} %param.4) | data formatting | bytes 524288 | tf_op args[0]
  1.2 1.7 %collective-permute-start = (bf16[8,2048]{1,0:T(8,128)(2,1)S(1)}, bf16[8,2048]{1,0:T(8,128)(2,1)S(1)}, u32[]{:S(2)}, u32[]{:S(2)}) collective-permute-start(bf16[8,2048]{1,0:T(8,128)(2,1)S(1)} %get-tuple-element.45), channel_id=1, source_target_pairs={{0,8},{8,16},{16,24},{24,32},{32,40},{40,48},{48,56},{56,64},{64,7... | collective-permute-start | bytes 98312 | tf_op jit(solution)/shard_map/ppermute | solution.py:247
  2.9 1.3 %collective-permute-start.1 = (bf16[8,2048]{1,0:T(8,128)(2,1)S(1)}, bf16[8,2048]{1,0:T(8,128)(2,1)S(1)}, u32[]{:S(2)}, u32[]{:S(2)}) collective-permute-start(bf16[8,2048]{1,0:T(8,128)(2,1)S(1)} %get-tuple-element.46), channel_id=1, source_target_pairs={{8,0},{16,8},{24,16},{32,24},{40,32},{48,40},{56,48},{64,56},{72,6... | collective-permute-start | bytes 98312 | tf_op jit(solution)/shard_map/ppermute | solution.py:248
  4.2 0.0 collective-permute-done
  4.2 3.2 %collective-permute-done.1 = bf16[8,2048]{1,0:T(8,128)(2,1)S(1)} collective-permute-done((bf16[8,2048]{1,0:T(8,128)(2,1)S(1)}, bf16[8,2048]{1,0:T(8,128)(2,1)S(1)}, u32[]{:S(2)}, u32[]{:S(2)}) %collective-permute-start.1) | collective-permute-done | bytes 32800 | tf_op jit(solution)/shard_map/ppermute | solution.py:248
  7.4 3.2 %collective-permute-start.2 = (bf16[10,8,2048]{2,1,0:T(8,128)(2,1)S(1)}, bf16[10,8,2048]{2,1,0:T(8,128)(2,1)S(1)}, u32[]{:S(2)}, u32[]{:S(2)}) collective-permute-start(bf16[10,8,2048]{2,1,0:T(8,128)(2,1)S(1)} %pad_maximum_fusion.shapes), channel_id=1, source_target_pairs={{0,1},{1,2},{2,3},{3,4},{4,5},{5,6},{6,7},{7,0},{8,9},{9,10},{10,1... | collective-permute-start | bytes 983048 | tf_op jit(solution)/shard_map/ppermute | solution.py:245
  10.6 0.0 collective-permute-start.4
  10.6 6.4 %collective-permute-done.2.below = bf16[10,8,2048]{2,1,0:T(8,128)(2,1)S(1)} collective-permute-done((bf16[10,8,2048]{2,1,0:T(8,128)(2,1)S(1)}, bf16[10,8,2048]{2,1,0:T(8,128)(2,1)S(1)}, u32[]{:S(2)}, u32[]{:S(2)}) %collective-permute-start.2) | collective-permute-done | bytes 327712 | tf_op jit(solution)/shard_map/ppermute | solution.py:245
  17.1 3.7 %collective-permute-start.3 = (bf16[10,8,2048]{2,1,0:T(8,128)(2,1)S(1)}, bf16[10,8,2048]{2,1,0:T(8,128)(2,1)S(1)}, u32[]{:S(2)}, u32[]{:S(2)}) collective-permute-start(bf16[10,8,2048]{2,1,0:T(8,128)(2,1)S(1)} %collective-permute-done.2.below), channel_id=1, source_target_pairs={{0,1},{1,2},{2,3},{3,4},{4,5},{5,6},{6,7},{7,0},{8,9},{9,10},{10,1... | collective-permute-start | bytes 983048 | tf_op jit(solution)/shard_map/ppermute | solution.py:245
  20.8 0.3 collective-permute-done.4.above
  21.0 0.0 collective-permute-start.5
  21.0 0.8 %convert_bitcast_fusion = f32[1,8,2048]{2,1,0:T(8,128)S(1)} fusion(s32[8,2048]{1,0:T(8,128)} %param.6), kind=kLoop, calls=%fused_computation.3 | loop fusion | flops 16384 | bytes 131072 | tf_op jit(solution)/shard_map/stack | solution.py:251
  21.9 0.0 copy-done
  21.9 0.7 dynamic-slice_reduce_fusion
  22.6 0.1 reshape.11.lists
  22.7 0.0 copy-done.1
  22.7 4.4 %shard_map.46 = (f32[3,8,8,2048]{3,2,1,0:T(8,128)S(1)}, f32[3,8,8,2048]{3,2,1,0:T(8,128)S(1)}, f32[8,128]{1,0:T(8,128)S(1)}, f32[256,64]{1,0:T(8,128)S(1)}, bf16[512,512]{1,0:T(8,128)(2,1)S(1)}) custom-call(s32[1]{0:T(128)} %bitcast.place, bf16[10,8,2048]{2,1,0:T(8,128)(2,1)S(1)} %pad_maximum_fusion.shapes, f32[2,8,2048]{2,1,0:T(8,128)S(1)} %pad_maximum_fusion.1.plate), custom_call_target="tpu_custom_call" | custom-call | tf_op jit(solution)/shard_map/pallas_call | solution.py:224
  27.1 6.5 %shard_map.47 = (f32[3,8,8,2048]{3,2,1,0:T(8,128)S(1)}, f32[3,8,8,2048]{3,2,1,0:T(8,128)S(1)}, f32[8,128]{1,0:T(8,128)S(1)}, f32[256,192]{1,0:T(8,128)S(1)}) custom-call(bf16[10,8,2048]{2,1,0:T(8,128)(2,1)S(1)} %collective-permute-done.2.below, bf16[10,8,2048]{2,1,0:T(8,128)(2,1)S(1)} %collective-permute-done.4.above, ...), custom_call_target="tpu_custom_call" | custom-call | tf_op jit(solution)/shard_map/pallas_call | solution.py:224
  33.7 0.0 collective-permute-done.3.below
  33.7 0.0 collective-permute-done.5.above
  33.7 8.0 %shard_map.48 = f32[32,8,640]{2,1,0:T(8,128)S(1)} custom-call(bf16[10,8,2048]{2,1,0:T(8,128)(2,1)S(1)} %collective-permute-done.3.below, bf16[10,8,2048]{2,1,0:T(8,128)(2,1)S(1)} %collective-permute-done.5.above, f32[2,8,2048]{2,1,0:T(8,128)S(1)} %pad_maximum_fusion.1.plate, f32[3,8,8,2048]{3,2,1,0:T(8,128)S(1)} %get-tuple-element.31.left, ...), custom_call_target="tpu_custom_call" | custom-call | tf_op jit(solution)/shard_map/pallas_call | solution.py:224
  41.7 21.8 %all_to_all.5 = f32[32,8,640]{2,1,0:T(8,128)S(1)} all-to-all(f32[32,8,640]{2,1,0:T(8,128)S(1)} %shard_map.48), channel_id=1, replica_groups=mesh['tile'=32,'mode'=8] {'tile'}, dimensions={0} | all-to-all | bytes 1310720 | tf_op jit(solution)/shard_map/all_to_all | solution.py:281
  63.6 0.3 shard_map.49
  63.8 3.2 %collective-permute-start.7 = (f32[40,128]{1,0:T(8,128)S(1)}, f32[40,128]{1,0:T(8,128)S(1)}, u32[]{:S(2)}, u32[]{:S(2)}) collective-permute-start(f32[40,128]{1,0:T(8,128)S(1)} %get-tuple-element.43.kept), channel_id=1, source_target_pairs={{0,1},{1,2},{2,3},{3,4},{4,5},{5,6},{6,7},{7,0},{8,9},{9,10},{10,1... | collective-permute-start | bytes 61448 | tf_op jit(solution)/shard_map/ppermute | solution.py:245
  67.1 0.0 collective-permute-start.6
  67.1 5.8 %collective-permute-done.6.from_far = f32[24,128]{1,0:T(8,128)S(1)} collective-permute-done((f32[24,128]{1,0:T(8,128)S(1)}, f32[24,128]{1,0:T(8,128)S(1)}, u32[]{:S(2)}, u32[]{:S(2)}) %collective-permute-start.6) | collective-permute-done | bytes 12320 | tf_op jit(solution)/shard_map/ppermute | solution.py:245
  72.9 0.0 collective-permute-done.7.from_below
  72.9 1.0 %shard_map.50 = f32[16,8,64]{2,1,0:T(8,128)} custom-call(bf16[512,512]{1,0:T(8,128)(2,1)S(1)} %get-tuple-element.30.order, f32[16,128]{1,0:T(8,128)S(1)} %get-tuple-element.42.mine, f32[40,128]{1,0:T(8,128)S(1)} %get-tuple-element.43.kept, f32[24,128]{1,0:T(8,128)S(1)} %collective-permute-done.6.from_far, f32[40,128]{1,0:T(8,128)S(1)} %collective-permute-done.7.from_below), custom_call_target="tpu_custom_call" | custom-call | tf_op jit(solution)/shard_map/pallas_call | solution.py:224
  (3 shorter events, 0.1 us)
Async XLA Ops:
  0.0 21.9 %copy-start = (s32[32,32,8]{1,2,0:T(8,128)S(1)}, s32[32,32,8]{1,2,0:T(8,128)}, u32[]{:S(2)}) copy-start(s32[32,32,8]{1,2,0:T(8,128)} %param.7) | copy-start | bytes 98308
  0.0 22.7 %copy-start.1 = (f32[8,2048]{1,0:T(8,128)S(1)}, f32[8,2048]{1,0:T(8,128)}, u32[]{:S(2)}) copy-start(f32[8,2048]{1,0:T(8,128)} %param.5) | copy-start | bytes 196612
  1.2 3.1 %collective-permute-start = (bf16[8,2048]{1,0:T(8,128)(2,1)S(1)}, bf16[8,2048]{1,0:T(8,128)(2,1)S(1)}, u32[]{:S(2)}, u32[]{:S(2)}) collective-permute-start(bf16[8,2048]{1,0:T(8,128)(2,1)S(1)} %get-tuple-element.45), channel_id=1, source_target_pairs={{0,8},{8,16},{16,24},{24,32},{32,40},{40,48},{48,56},{56,64},{64,7... | collective-permute-start | bytes 98312 | tf_op jit(solution)/shard_map/ppermute | solution.py:247
  2.9 4.5 %collective-permute-start.1 = (bf16[8,2048]{1,0:T(8,128)(2,1)S(1)}, bf16[8,2048]{1,0:T(8,128)(2,1)S(1)}, u32[]{:S(2)}, u32[]{:S(2)}) collective-permute-start(bf16[8,2048]{1,0:T(8,128)(2,1)S(1)} %get-tuple-element.46), channel_id=1, source_target_pairs={{8,0},{16,8},{24,16},{32,24},{40,32},{48,40},{56,48},{64,56},{72,6... | collective-permute-start | bytes 98312 | tf_op jit(solution)/shard_map/ppermute | solution.py:248
  7.4 9.6 %collective-permute-start.2 = (bf16[10,8,2048]{2,1,0:T(8,128)(2,1)S(1)}, bf16[10,8,2048]{2,1,0:T(8,128)(2,1)S(1)}, u32[]{:S(2)}, u32[]{:S(2)}) collective-permute-start(bf16[10,8,2048]{2,1,0:T(8,128)(2,1)S(1)} %pad_maximum_fusion.shapes), channel_id=1, source_target_pairs={{0,1},{1,2},{2,3},{3,4},{4,5},{5,6},{6,7},{7,0},{8,9},{9,10},{10,1... | collective-permute-start | bytes 983048 | tf_op jit(solution)/shard_map/ppermute | solution.py:245
  10.6 10.4 %collective-permute-start.4 = (bf16[10,8,2048]{2,1,0:T(8,128)(2,1)S(1)}, bf16[10,8,2048]{2,1,0:T(8,128)(2,1)S(1)}, u32[]{:S(2)}, u32[]{:S(2)}) collective-permute-start(bf16[10,8,2048]{2,1,0:T(8,128)(2,1)S(1)} %pad_maximum_fusion.shapes), channel_id=1, source_target_pairs={{0,7},{1,0},{2,1},{3,2},{4,3},{5,4},{6,5},{7,6},{8,15},{9,8},{10,9... | collective-permute-start | bytes 983048 | tf_op jit(solution)/shard_map/ppermute | solution.py:245
  17.1 16.6 %collective-permute-start.3 = (bf16[10,8,2048]{2,1,0:T(8,128)(2,1)S(1)}, bf16[10,8,2048]{2,1,0:T(8,128)(2,1)S(1)}, u32[]{:S(2)}, u32[]{:S(2)}) collective-permute-start(bf16[10,8,2048]{2,1,0:T(8,128)(2,1)S(1)} %collective-permute-done.2.below), channel_id=1, source_target_pairs={{0,1},{1,2},{2,3},{3,4},{4,5},{5,6},{6,7},{7,0},{8,9},{9,10},{10,1... | collective-permute-start | bytes 983048 | tf_op jit(solution)/shard_map/ppermute | solution.py:245
  21.0 12.6 %collective-permute-start.5 = (bf16[10,8,2048]{2,1,0:T(8,128)(2,1)S(1)}, bf16[10,8,2048]{2,1,0:T(8,128)(2,1)S(1)}, u32[]{:S(2)}, u32[]{:S(2)}) collective-permute-start(bf16[10,8,2048]{2,1,0:T(8,128)(2,1)S(1)} %collective-permute-done.4.above), channel_id=1, source_target_pairs={{0,7},{1,0},{2,1},{3,2},{4,3},{5,4},{6,5},{7,6},{8,15},{9,8},{10,9... | collective-permute-start | bytes 983048 | tf_op jit(solution)/shard_map/ppermute | solution.py:245
  63.8 9.0 %collective-permute-start.7 = (f32[40,128]{1,0:T(8,128)S(1)}, f32[40,128]{1,0:T(8,128)S(1)}, u32[]{:S(2)}, u32[]{:S(2)}) collective-permute-start(f32[40,128]{1,0:T(8,128)S(1)} %get-tuple-element.43.kept), channel_id=1, source_target_pairs={{0,1},{1,2},{2,3},{3,4},{4,5},{5,6},{6,7},{7,0},{8,9},{9,10},{10,1... | collective-permute-start | bytes 61448 | tf_op jit(solution)/shard_map/ppermute | solution.py:245
  67.1 5.8 %collective-permute-start.6 = (f32[24,128]{1,0:T(8,128)S(1)}, f32[24,128]{1,0:T(8,128)S(1)}, u32[]{:S(2)}, u32[]{:S(2)}) collective-permute-start(f32[24,128]{1,0:T(8,128)S(1)} %get-tuple-element.44), channel_id=1, source_target_pairs={{0,6},{1,7},{2,0},{3,1},{4,2},{5,3},{6,4},{7,5},{8,14},{9,15},{10,... | collective-permute-start | bytes 36872 | tf_op jit(solution)/shard_map/ppermute | solution.py:245
